TPU v7x, 32 devices: a whole 2x2x4 slice. The times are simulated.
32 devices in a mesh: ctx: 8 (over z, y), wsh: 4 (over x, core).
Axes of the slice: x: 2, y: 2, z: 4, core: 2. Of those that a mesh axis runs over, the one named last changes fastest.
Arguments:
- tokens: bfloat16 [4, 1024, 2048], P('wsh', 'ctx'), may hold values from -6 to 6
- out_grad: bfloat16 [4, 1024, 2048], P('wsh', 'ctx'), may hold values from -6 to 6
- attn_weight: bfloat16 [4, 2048, 2048], P(None, None, 'wsh'), may hold values from -0.125 to 0.125
- mlp_weight: bfloat16 [3, 2048, 8192], P(None, None, 'wsh'), may hold values from -0.125 to 0.125
- norm_gains: bfloat16 [4, 2048], P(None, 'wsh'), may hold values from 0.25 to 1.75
- adapt_model: bfloat16 [11, 64, 2048], P(None, None, 'wsh'), may hold values from -0.125 to 0.125
- adapt_hidden: bfloat16 [3, 64, 8192], P(None, None, 'wsh'), may hold values from -0.0625 to 0.0625
- lengths: int32 [4], replicated, may hold values from 512 to 1024, as said below
- adapter_pick: int32 [4], replicated, may hold values from 0 to 3
- block_order: int32 [4, 16], P('wsh'), may hold values from 0 to 15, as said below
Outputs:
- layer_out: bfloat16 [4, 1024, 2048], P('wsh', 'ctx')
- input_grad: float32 [4, 1024, 2048], P('wsh', 'ctx')
- adapt_model_grad: float32 [11, 64, 2048], P(None, None, 'wsh')
- adapt_hidden_grad: float32 [3, 64, 8192], P(None, None, 'wsh')
Inputs may be any that keep to these rules, and one draw needn't show every extreme that they name: `lengths`: some sequence has exactly 1024 valid tokens. Each row of block_order is a permutation of the 16 blocks; the two blocks stored on one index of ctx are p and 15 - p for some p, in either order.
All inputs are finite; a program needn't handle non-finite values.
Results may differ from a plain program's by a relative error of at most 0.017.
Values may be sent and summed in bfloat16 or wider, within the bound.
No kernel may reach another device: no remote copies, remote signals or barrier semaphores. Data moves between devices by JAX's collectives and lax.ppermute only.
A program may use at most 512 MiB of HBM per device.

v0:
```python
import jax
import jax.numpy as jnp
from jax import lax
from jax.sharding import PartitionSpec as P

HEADS = 16
HEAD_DIM = 128
FF = 8192
RANK = 16
ADAPTERS = 4


NORM_EPS = 1e-06
ADAPTER_SCALE = 4.0
ROPE_BASE = 500000.0


def rms_scale(values):
    return lax.rsqrt(jnp.mean(values * values, axis=-1, keepdims=True) + NORM_EPS)


def norm_back(values, scale_rows, upstream):
    return scale_rows * upstream - values * scale_rows**3 * jnp.mean(
        upstream * values, axis=-1, keepdims=True
    )


def rotary_tables(positions, head_dim):
    half_dim = head_dim // 2
    frequency = ROPE_BASE ** (-(jnp.arange(half_dim, dtype=jnp.float32) * 2.0) / head_dim)
    angles = positions.astype(jnp.float32)[:, None] * frequency[None, :]
    return (jnp.cos(angles)[:, None, :], jnp.sin(angles)[:, None, :])


def rotate(values, tables, heads_total):
    cosine, sine_part = tables
    row_count = values.shape[0]
    shaped = values.reshape(row_count, heads_total, -1)
    half_dim = shaped.shape[-1] // 2
    first_half = shaped[..., :half_dim]
    second_half = shaped[..., half_dim:]
    turned = jnp.concatenate(
        [
            first_half * cosine - second_half * sine_part,
            second_half * cosine + first_half * sine_part,
        ],
        axis=-1,
    )
    return turned.reshape(row_count, -1)


def rotate_back(gradient, tables, heads_total):
    cosine, sine_part = tables
    row_count = gradient.shape[0]
    shaped = gradient.reshape(row_count, heads_total, -1)
    half_dim = shaped.shape[-1] // 2
    first_half = shaped[..., :half_dim]
    second_half = shaped[..., half_dim:]
    turned = jnp.concatenate(
        [
            first_half * cosine + second_half * sine_part,
            second_half * cosine - first_half * sine_part,
        ],
        axis=-1,
    )
    return turned.reshape(row_count, -1)


def pick_rows(stacked, onehot, adapters):
    part_count, col_count = (stacked.shape[0], stacked.shape[2])
    split_view = stacked.reshape(part_count, adapters, -1, col_count)
    return jnp.einsum(
        "kard,a->krd", split_view, onehot.astype(stacked.dtype), preferred_element_type=jnp.float32
    ).astype(stacked.dtype)


def per_device(
    tokens,
    out_grad,
    attn_weight,
    mlp_weight,
    norm_gains,
    adapt_model,
    adapt_hidden,
    lengths,
    adapter_pick,
    block_order,
):
    input_rows = tokens[0]
    row_count, model_dim = input_rows.shape
    block_rows = row_count // 2
    ctx_size = lax.axis_size("ctx")
    slot_rows = row_count * ctx_size
    heads_all = HEADS
    head_dim = HEAD_DIM
    adapters = ADAPTERS
    score_scale = head_dim ** (-0.5)
    seq_index = lax.axis_index("wsh")
    ctx_index = lax.axis_index("ctx")
    seq_length = lax.dynamic_index_in_dim(lengths, seq_index, keepdims=False)
    chosen = lax.dynamic_index_in_dim(adapter_pick, seq_index, keepdims=False)
    onehot = (jnp.arange(adapters) == chosen).astype(jnp.float32)
    all_positions = (
        block_order[0][:, None] * block_rows + jnp.arange(block_rows)[None, :]
    ).reshape(-1)
    own_positions = lax.dynamic_slice_in_dim(all_positions, ctx_index * row_count, row_count)
    valid_rows = (own_positions < seq_length).astype(jnp.float32)[:, None]
    tables = rotary_tables(own_positions, head_dim)
    key_allowed = (all_positions[None, :] <= own_positions[:, None]) & (
        all_positions[None, :] < seq_length
    )

    def heads_view(matrix):
        return matrix.reshape(matrix.shape[0], heads_all, head_dim)

    attn_full, gains_full, adapt_full = (
        lax.all_gather(attn_weight, "wsh", axis=2, tiled=True),
        lax.all_gather(norm_gains, "wsh", axis=1, tiled=True),
        lax.all_gather(adapt_model, "wsh", axis=2, tiled=True),
    )
    gain_rows = gains_full.astype(jnp.float32)
    model_reduced = pick_rows(adapt_full, onehot, adapters)
    projected_rows = jnp.einsum(
        "td,kde->kte", input_rows, attn_full[:3], preferred_element_type=jnp.float32
    )
    low_in = jnp.einsum(
        "td,krd->ktr", input_rows, model_reduced[:3], preferred_element_type=jnp.float32
    ).astype(jnp.bfloat16)
    projected_rows = projected_rows + ADAPTER_SCALE * jnp.einsum(
        "ktr,krd->ktd", low_in, model_reduced[6:9], preferred_element_type=jnp.float32
    )
    query_scale = rms_scale(projected_rows[0])
    key_scale = rms_scale(projected_rows[1])
    queries = rotate(projected_rows[0] * query_scale * gain_rows[0], tables, heads_all).astype(
        jnp.bfloat16
    )
    own_keys = rotate(projected_rows[1] * key_scale * gain_rows[1], tables, heads_all).astype(
        jnp.bfloat16
    )
    own_values = projected_rows[2].astype(jnp.bfloat16)
    all_keys, all_values = (
        lax.all_gather(own_keys, "ctx", axis=0, tiled=True),
        lax.all_gather(own_values, "ctx", axis=0, tiled=True),
    )
    query_heads = heads_view(queries)
    key_heads = heads_view(all_keys)
    value_heads = heads_view(all_values)
    scores = (
        jnp.einsum("thd,shd->hts", query_heads, key_heads, preferred_element_type=jnp.float32)
        * score_scale
    )
    scores = jnp.where(key_allowed[None], scores, -jnp.inf)
    row_max = jnp.max(scores, axis=-1, keepdims=True)
    log_full = row_max + jnp.log(jnp.sum(jnp.exp(scores - row_max), axis=-1, keepdims=True))
    weights = jnp.exp(scores - log_full).astype(jnp.bfloat16)
    attended = (
        jnp.einsum("hts,shd->thd", weights, value_heads, preferred_element_type=jnp.float32)
        .reshape(row_count, model_dim)
        .astype(jnp.bfloat16)
    )
    log_totals = log_full[..., 0]
    reduced_output = jnp.einsum(
        "td,rd->tr", attended, model_reduced[3], preferred_element_type=jnp.float32
    ).astype(jnp.bfloat16)
    branch = jnp.dot(
        attended, attn_full[3], preferred_element_type=jnp.float32
    ) + ADAPTER_SCALE * jnp.dot(
        reduced_output, model_reduced[9], preferred_element_type=jnp.float32
    )
    branch_scale = rms_scale(branch)
    hidden_in = input_rows.astype(jnp.float32) + branch * branch_scale * gain_rows[2]
    hidden_low = hidden_in.astype(jnp.bfloat16)
    reduced_gate_up = jnp.einsum(
        "td,krd->ktr", hidden_low, model_reduced[4:6], preferred_element_type=jnp.float32
    ).astype(jnp.bfloat16)

    def gate_up_parts(weight_piece, gathered_rows):
        gate_part = jnp.dot(
            hidden_low, weight_piece[0], preferred_element_type=jnp.float32
        ) + ADAPTER_SCALE * jnp.dot(
            reduced_gate_up[0], gathered_rows[0], preferred_element_type=jnp.float32
        )
        up_part = jnp.dot(
            hidden_low, weight_piece[1], preferred_element_type=jnp.float32
        ) + ADAPTER_SCALE * jnp.dot(
            reduced_gate_up[1], gathered_rows[1], preferred_element_type=jnp.float32
        )
        return (gate_part, up_part)

    weight_piece = lax.all_gather(mlp_weight, "wsh", axis=2, tiled=True)
    adapt_piece = lax.all_gather(adapt_hidden, "wsh", axis=2, tiled=True)
    gathered_rows = pick_rows(adapt_piece, onehot, adapters)
    gate_part, up_part = gate_up_parts(weight_piece, gathered_rows)
    product = (jax.nn.silu(gate_part) * up_part).astype(jnp.bfloat16)
    down_total_sum = jnp.einsum(
        "tn,dn->td", product, weight_piece[2], preferred_element_type=jnp.float32
    )
    low_down_sum = jnp.einsum(
        "tn,rn->tr", product, gathered_rows[2], preferred_element_type=jnp.float32
    )
    down_total_sum, low_down_sum = (down_total_sum, low_down_sum)
    low_down = low_down_sum.astype(jnp.bfloat16)
    feedforward_output = down_total_sum + ADAPTER_SCALE * jnp.dot(
        low_down, model_reduced[10], preferred_element_type=jnp.float32
    )
    mlp_scale = rms_scale(feedforward_output)
    result = hidden_in + feedforward_output * mlp_scale * gain_rows[3]
    upstream = out_grad[0].astype(jnp.float32) * valid_rows
    grad_mlp_out = norm_back(feedforward_output, mlp_scale, upstream * gain_rows[3]).astype(
        jnp.bfloat16
    )
    grad_low_down = (
        ADAPTER_SCALE
        * jnp.einsum(
            "td,rd->tr", grad_mlp_out, model_reduced[10], preferred_element_type=jnp.float32
        )
    ).astype(jnp.bfloat16)
    gradient_down_factor = ADAPTER_SCALE * jnp.einsum(
        "tr,td->rd", low_down, grad_mlp_out, preferred_element_type=jnp.float32
    )
    weight_piece = lax.all_gather(mlp_weight, "wsh", axis=2, tiled=True)
    adapt_piece = lax.all_gather(adapt_hidden, "wsh", axis=2, tiled=True)
    gathered_rows = pick_rows(adapt_piece, onehot, adapters)
    gate_part, up_part = gate_up_parts(weight_piece, gathered_rows)
    sigmoid_gate = jax.nn.sigmoid(gate_part)
    silu_gate = gate_part * sigmoid_gate
    product = (silu_gate * up_part).astype(jnp.bfloat16)
    grad_product = jnp.dot(
        grad_mlp_out, weight_piece[2], preferred_element_type=jnp.float32
    ) + jnp.dot(grad_low_down, gathered_rows[2], preferred_element_type=jnp.float32)
    grad_gate = (
        grad_product * up_part * sigmoid_gate * (1.0 + gate_part * (1.0 - sigmoid_gate))
    ).astype(jnp.bfloat16)
    grad_up = (grad_product * silu_gate).astype(jnp.bfloat16)
    input_sum = jnp.einsum(
        "tn,dn->td", grad_gate, weight_piece[0], preferred_element_type=jnp.float32
    ) + jnp.einsum("tn,dn->td", grad_up, weight_piece[1], preferred_element_type=jnp.float32)
    reduced_sum = ADAPTER_SCALE * jnp.stack(
        [
            jnp.einsum(
                "tn,rn->tr", grad_gate, gathered_rows[0], preferred_element_type=jnp.float32
            ),
            jnp.einsum("tn,rn->tr", grad_up, gathered_rows[1], preferred_element_type=jnp.float32),
        ]
    )
    piece_grads = jnp.stack(
        [
            ADAPTER_SCALE
            * jnp.einsum(
                "tr,tn->rn", reduced_gate_up[0], grad_gate, preferred_element_type=jnp.float32
            ),
            ADAPTER_SCALE
            * jnp.einsum(
                "tr,tn->rn", reduced_gate_up[1], grad_up, preferred_element_type=jnp.float32
            ),
            jnp.einsum("tr,tn->rn", grad_low_down, product, preferred_element_type=jnp.float32),
        ]
    )
    input_sum, reduced_sum, picked_hidden = (input_sum, reduced_sum, piece_grads)
    low_grads = reduced_sum.astype(jnp.bfloat16)
    grad_hidden = (
        upstream
        + input_sum
        + jnp.einsum(
            "ktr,krd->td", low_grads, model_reduced[4:6], preferred_element_type=jnp.float32
        )
    )
    grad_a_gate_up = jnp.einsum(
        "ktr,td->krd", low_grads, hidden_low, preferred_element_type=jnp.float32
    )
    grad_branch = norm_back(branch, branch_scale, grad_hidden * gain_rows[2]).astype(jnp.bfloat16)
    grad_low_out = (
        ADAPTER_SCALE
        * jnp.einsum("td,rd->tr", grad_branch, model_reduced[9], preferred_element_type=jnp.float32)
    ).astype(jnp.bfloat16)
    gradient_output_factor = ADAPTER_SCALE * jnp.einsum(
        "tr,td->rd", reduced_output, grad_branch, preferred_element_type=jnp.float32
    )
    grad_a_out = jnp.einsum("tr,td->rd", grad_low_out, attended, preferred_element_type=jnp.float32)
    grad_attended = (
        jnp.einsum("te,de->td", grad_branch, attn_full[3], preferred_element_type=jnp.float32)
        + jnp.einsum(
            "tr,rd->td", grad_low_out, model_reduced[3], preferred_element_type=jnp.float32
        )
    ).astype(jnp.bfloat16)
    grad_heads = heads_view(grad_attended)
    scores = (
        jnp.einsum("thd,shd->hts", query_heads, key_heads, preferred_element_type=jnp.float32)
        * score_scale
    )
    scores = jnp.where(key_allowed[None], scores, -jnp.inf)
    weights_full = jnp.exp(scores - log_totals[..., None])
    grad_probs = jnp.einsum(
        "thd,shd->hts", grad_heads, value_heads, preferred_element_type=jnp.float32
    )
    row_delta = jnp.sum(weights_full * grad_probs, axis=-1, keepdims=True)
    grad_scores = (weights_full * (grad_probs - row_delta)).astype(jnp.bfloat16)
    grad_queries = (
        jnp.einsum("hts,shd->thd", grad_scores, key_heads, preferred_element_type=jnp.float32)
        * score_scale
    ).reshape(row_count, model_dim)
    key_full = (
        jnp.einsum("hts,thd->shd", grad_scores, query_heads, preferred_element_type=jnp.float32)
        * score_scale
    ).reshape(slot_rows, model_dim)
    value_full = jnp.einsum(
        "hts,thd->shd",
        weights_full.astype(jnp.bfloat16),
        grad_heads,
        preferred_element_type=jnp.float32,
    ).reshape(slot_rows, model_dim)
    grad_keys, grad_values = (
        lax.psum_scatter(key_full, "ctx", scatter_dimension=0, tiled=True),
        lax.psum_scatter(value_full, "ctx", scatter_dimension=0, tiled=True),
    )
    grad_proj_query = norm_back(
        projected_rows[0], query_scale, rotate_back(grad_queries, tables, heads_all) * gain_rows[0]
    ).astype(jnp.bfloat16)
    grad_proj_key = norm_back(
        projected_rows[1], key_scale, rotate_back(grad_keys, tables, heads_all) * gain_rows[1]
    ).astype(jnp.bfloat16)
    grad_proj = jnp.stack([grad_proj_query, grad_proj_key, grad_values.astype(jnp.bfloat16)])
    grad_low_qkv = (
        ADAPTER_SCALE
        * jnp.einsum(
            "ktd,krd->ktr", grad_proj, model_reduced[6:9], preferred_element_type=jnp.float32
        )
    ).astype(jnp.bfloat16)
    gradient_projection_factor = ADAPTER_SCALE * jnp.einsum(
        "ktr,ktd->krd", low_in, grad_proj, preferred_element_type=jnp.float32
    )
    grad_a_qkv = jnp.einsum(
        "ktr,td->krd", grad_low_qkv, input_rows, preferred_element_type=jnp.float32
    )
    grad_inputs = (
        grad_hidden
        + jnp.einsum("kte,kde->td", grad_proj, attn_full[:3], preferred_element_type=jnp.float32)
        + jnp.einsum(
            "ktr,krd->td", grad_low_qkv, model_reduced[:3], preferred_element_type=jnp.float32
        )
    )
    picked_model = jnp.concatenate(
        [
            grad_a_qkv,
            grad_a_out[None],
            grad_a_gate_up,
            gradient_projection_factor,
            gradient_output_factor[None],
            gradient_down_factor[None],
        ],
        axis=0,
    )
    spread_model = (onehot[None, :, None, None] * picked_model[:, None]).reshape(
        picked_model.shape[0], adapters * RANK, model_dim
    )
    spread_hidden = (onehot[None, :, None, None] * picked_hidden[:, None]).reshape(
        picked_hidden.shape[0], adapters * RANK, FF
    )
    shard_model, shard_hidden = (
        lax.psum_scatter(spread_model, "wsh", scatter_dimension=2, tiled=True),
        lax.psum_scatter(spread_hidden, "wsh", scatter_dimension=2, tiled=True),
    )
    model_grads, hidden_grads_out = lax.psum((shard_model, shard_hidden), "ctx")
    return (result.astype(jnp.bfloat16)[None], grad_inputs[None], model_grads, hidden_grads_out)


def solution(mesh):
    in_specs = (
        P("wsh", "ctx", None),
        P("wsh", "ctx", None),
        P(None, None, "wsh"),
        P(None, None, "wsh"),
        P(None, "wsh"),
        P(None, None, "wsh"),
        P(None, None, "wsh"),
        P(),
        P(),
        P("wsh", None),
    )
    out_specs = (
        P("wsh", "ctx", None),
        P("wsh", "ctx", None),
        P(None, None, "wsh"),
        P(None, None, "wsh"),
    )
    return jax.shard_map(
        per_device, mesh=mesh, in_specs=in_specs, out_specs=out_specs, check_vma=False
    )
```

profile of v0, /device:TPU:0, one launch (start us, length us, event | category | flops | bytes accessed | tf_op | source)
XLA Modules:
  0.0 1708.9 jit_solution(13489928325962978200)
XLA Ops:
  7.9 11.5 copy.32
  20.4 6.4 all_gather.26
  29.2 10.2 all-gather.10.cloned.1.call-done
  39.4 4.8 fusion.19
  45.8 196.8 %all-gather.8.cloned.1.call-done = bf16[4,2048,2048]{1,2,0:T(8,128)(2,1)} async-done(((bf16[4,2048,512]{1,2,0:T(8,128)(2,1)}), bf16[4,2048,2048]{1,2,0:T(8,128)(2,1)}) %all-gather.8.cloned.1.call-update) | async-done | bytes 33554448 | tf_op jit(solution)/shard_map/all_gather | solution.py:117
  242.6 11.9 fusion.74
  272.9 6.7 fusion.17
  281.4 67.9 %all-gather.12.cloned.1.call-done = bf16[1024,2048]{0,1:T(8,128)(2,1)} async-done(((bf16[128,2048]{0,1:T(8,128)(2,1)}), bf16[1024,2048]{0,1:T(8,128)(2,1)}) %all-gather.12.cloned.1.call-update) | async-done | bytes 4194320 | tf_op jit(solution)/shard_map/all_gather | solution.py:142
  356.9 67.7 %all-gather.18.cloned.1.call-done = bf16[1,1024,2048]{1,2,0:T(8,128)(2,1)} async-done(((bf16[1,128,2048]{1,2,0:T(8,128)(2,1)}), bf16[1,1024,2048]{1,2,0:T(8,128)(2,1)}) %all-gather.18.cloned.1.call-update) | async-done | bytes 4194320 | tf_op jit(solution)/shard_map/all_gather | solution.py:143
  424.6 7.2 convolution_convert_fusion
  432.0 9.3 fusion.13
  442.3 565.8 %all-gather.14.cloned.1.call-done = bf16[3,2048,8192]{2,1,0:T(8,128)(2,1)} async-done(((bf16[3,2048,2048]{2,1,0:T(8,128)(2,1)}), bf16[3,2048,8192]{2,1,0:T(8,128)(2,1)}) %all-gather.14.cloned.1.call-update) | async-done | bytes 100663312 | tf_op jit(solution)/shard_map/all_gather | solution.py:190
  1008.1 15.0 fusion.1
  1023.1 5.0 fusion.8
  1028.1 15.2 fusion.3
  1043.3 7.1 multiply_convert_fusion.3
  1052.2 15.8 fusion.5
  1070.0 15.2 fusion.4
  1085.2 7.1 multiply_convert_fusion.1
  1093.6 16.7 fusion
  1110.4 17.0 fusion.37
  1130.7 4.6 fusion.12
  1136.0 8.2 multiply_reduce_fusion
  1146.8 4.7 broadcast_multiply_fusion
  1151.6 9.4 fusion.81
  1169.1 4.8 fusion.45
  1173.9 125.7 %reduce-scatter.5.cloned.1.call-done = f32[128,2048]{0,1:T(8,128)} async-done(((f32[1024,2048]{0,1:T(8,128)}), f32[128,2048]{0,1:T(8,128)}) %reduce-scatter.5.cloned.1.call-update) | async-done | bytes 1048592 | tf_op jit(solution)/shard_map/reduce_scatter | solution.py:313
  1316.9 133.3 %reduce-scatter.7.cloned.1.call-done = f32[128,2048]{0,1:T(8,128)} async-done(((f32[1024,2048]{0,1:T(8,128)}), f32[128,2048]{0,1:T(8,128)}) %reduce-scatter.7.cloned.1.call-update) | async-done | bytes 1048592 | tf_op jit(solution)/shard_map/reduce_scatter | solution.py:314
  1460.4 49.5 %reduce-scatter.11.cloned.1.call-done = f32[3,64,2048]{2,1,0:T(8,128)} async-done(((f32[3,64,8192]{2,1,0:T(8,128)}), f32[3,64,2048]{2,1,0:T(8,128)}) %reduce-scatter.11.cloned.1.call-update) | async-done | bytes 1572880 | tf_op jit(solution)/shard_map/reduce_scatter | solution.py:361
  1509.8 57.0 %reduce-scatter.9.cloned.1.call-done = f32[11,64,512]{2,1,0:T(8,128)} async-done(((f32[11,64,2048]{2,1,0:T(8,128)}), f32[11,64,512]{2,1,0:T(8,128)}) %reduce-scatter.9.cloned.1.call-update) | async-done | bytes 1441808 | tf_op jit(solution)/shard_map/reduce_scatter | solution.py:360
  1568.1 11.3 fusion.32
  1579.4 117.3 %all-reduce.3.cloned.1.call-done = (f32[11,64,512]{2,1,0:T(8,128)}, f32[3,64,2048]{2,1,0:T(8,128)}) async-done(((f32[11,64,512]{2,1,0:T(8,128)}, f32[3,64,2048]{2,1,0:T(8,128)}), (f32[11,64,512]{2,1,0:T(8,128)}, f32[3,64,2048]{2,1,0:T(8,128)})) %all-reduce.3.cloned.1.call-update) | async-done | bytes 3014672 | tf_op jit(solution)/shard_map/psum | solution.py:363
  (230 shorter events, 87.6 us)
Async XLA Ops:
  7.2 32.2 %all-gather.10.cloned.1.call-start = ((), (), s32[]{:S(2)}) async-start(), calls=%async_computation.5 | async-start | bytes 3604480 | tf_op jit(solution)/shard_map/all_gather | solution.py:119
  7.9 234.7 %all-gather.8.cloned.1.call-start = ((), (), s32[]{:S(2)}) async-start(), calls=%async_computation.4 | async-start | bytes 41943040 | tf_op jit(solution)/shard_map/all_gather | solution.py:117
  19.5 253.4 %all-gather.16.cloned.1.call-start = ((), (), s32[]{:S(2)}) async-start(), calls=%async_computation.8 | async-start | bytes 3932160 | tf_op jit(solution)/shard_map/all_gather | solution.py:191
  20.2 329.1 %all-gather.12.cloned.1.call-start = ((), (), s32[]{:S(2)}) async-start(), calls=%async_computation.6 | async-start | bytes 4718592 | tf_op jit(solution)/shard_map/all_gather | solution.py:142
  26.9 236.9 %copy-start.42 = (f32[1,2048]{1,0:T(1,128)}, f32[1,2048]{1,0:T(1,128)S(1)}, u32[]{:S(2)}) copy-start(f32[1,2048]{1,0:T(1,128)S(1)} %get-tuple-element.38) | copy-start | bytes 24580
  26.9 238.3 %copy-start.44 = (f32[1,2048]{1,0:T(1,128)}, f32[1,2048]{1,0:T(1,128)S(1)}, u32[]{:S(2)}) copy-start(f32[1,2048]{1,0:T(1,128)S(1)} %get-tuple-element.39) | copy-start | bytes 24580
  29.1 236.3 %copy-start.32 = (f32[128,64]{1,0:T(8,128)}, f32[128,64]{1,0:T(8,128)S(1)}, u32[]{:S(2)}) copy-start(f32[128,64]{1,0:T(8,128)S(1)} %get-tuple-element.40) | copy-start | bytes 98308
  29.1 236.3 %copy-start.34 = (f32[128,64]{1,0:T(8,128)}, f32[128,64]{1,0:T(8,128)S(1)}, u32[]{:S(2)}) copy-start(f32[128,64]{1,0:T(8,128)S(1)} %get-tuple-element.41) | copy-start | bytes 98308
  45.8 208.7 %copy-start.46 = (bf16[3,16,128]{2,1,0:T(8,128)(2,1)}, bf16[3,16,128]{2,1,0:T(8,128)(2,1)S(1)}, u32[]{:S(2)}) copy-start(bf16[3,16,128]{2,1,0:T(8,128)(2,1)S(1)} %convolution_convert_fusion.1) | copy-start | bytes 36868
  270.3 154.3 %all-gather.18.cloned.1.call-start = ((), (), s32[]{:S(2)}) async-start(), calls=%async_computation.13 | async-start | bytes 4718592 | tf_op jit(solution)/shard_map/all_gather | solution.py:143
  271.3 736.9 %all-gather.14.cloned.1.call-start = ((), (), s32[]{:S(2)}) async-start(), calls=%async_computation.7 | async-start | bytes 125829120 | tf_op jit(solution)/shard_map/all_gather | solution.py:190
  271.8 1027.7 %reduce-scatter.5.cloned.1.call-start = ((), (), s32[]{:S(2)}) async-start(), calls=%async_computation.9 | async-start | bytes 9437184 | tf_op jit(solution)/shard_map/reduce_scatter | solution.py:313
  272.9 76.4 %copy-start.20 = (bf16[128,16,64]{2,0,1:T(8,128)(2,1)S(1)}, bf16[128,16,64]{2,0,1:T(8,128)(2,1)}, u32[]{:S(2)}) copy-start(bf16[128,16,64]{2,0,1:T(8,128)(2,1)} %get-tuple-element.24) | copy-start | bytes 786436
  272.9 76.4 %copy-start.22 = (bf16[128,16,64]{2,0,1:T(8,128)(2,1)S(1)}, bf16[128,16,64]{2,0,1:T(8,128)(2,1)}, u32[]{:S(2)}) copy-start(bf16[128,16,64]{2,0,1:T(8,128)(2,1)} %get-tuple-element.25) | copy-start | bytes 786436
  442.1 586.1 %copy-start.14 = (bf16[128,2048]{1,0:T(8,128)(2,1)}, bf16[128,2048]{1,0:T(8,128)(2,1)S(1)}, u32[]{:S(2)}) copy-start(bf16[128,2048]{1,0:T(8,128)(2,1)S(1)} %fusion.68) | copy-start | bytes 1572868
  1050.5 17.5 %copy-start.7 = (bf16[128,8192]{1,0:T(8,128)(2,1)}, bf16[128,8192]{1,0:T(8,128)(2,1)S(1)}, u32[]{:S(2)}) copy-start(bf16[128,8192]{1,0:T(8,128)(2,1)S(1)} %get-tuple-element.54) | copy-start | bytes 6291460
  1092.3 18.1 %copy-start.11 = (bf16[128,8192]{1,0:T(8,128)(2,1)}, bf16[128,8192]{1,0:T(8,128)(2,1)S(1)}, u32[]{:S(2)}) copy-start(bf16[128,8192]{1,0:T(8,128)(2,1)S(1)} %get-tuple-element.14) | copy-start | bytes 6291460
  1093.6 16.8 copy-start.31
  1151.6 298.6 %reduce-scatter.7.cloned.1.call-start = ((), (), s32[]{:S(2)}) async-start(), calls=%async_computation.10 | async-start | bytes 9437184 | tf_op jit(solution)/shard_map/reduce_scatter | solution.py:314
  1161.0 348.8 %reduce-scatter.11.cloned.1.call-start = ((), (), s32[]{:S(2)}) async-start(), calls=%async_computation.12 | async-start | bytes 7864320 | tf_op jit(solution)/shard_map/reduce_scatter | solution.py:361
  1169.1 397.7 %reduce-scatter.9.cloned.1.call-start = ((), (), s32[]{:S(2)}) async-start(), calls=%async_computation.11 | async-start | bytes 7208960 | tf_op jit(solution)/shard_map/reduce_scatter | solution.py:360
  1173.9 129.5 %copy-start.33 = (f32[128,64]{1,0:T(8,128)S(1)}, f32[128,64]{1,0:T(8,128)}, u32[]{:S(2)}) copy-start(f32[128,64]{1,0:T(8,128)} %copy-done.32) | copy-start | bytes 98308
  1173.9 129.5 %copy-start.35 = (f32[128,64]{1,0:T(8,128)S(1)}, f32[128,64]{1,0:T(8,128)}, u32[]{:S(2)}) copy-start(f32[128,64]{1,0:T(8,128)} %copy-done.34) | copy-start | bytes 98308
  1312.4 139.1 %copy-start.51 = (f32[128]{0:T(128)S(1)}, f32[128]{0:T(128)}, u32[]{:S(2)}) copy-start(f32[128]{0:T(128)} %copy-done.50) | copy-start | bytes 1540
  1312.4 139.1 %copy-start.53 = (f32[128]{0:T(128)S(1)}, f32[128]{0:T(128)}, u32[]{:S(2)}) copy-start(f32[128]{0:T(128)} %copy-done.52) | copy-start | bytes 1540
  1312.4 139.1 %copy-start.55 = (f32[128]{0:T(128)S(1)}, f32[128]{0:T(128)}, u32[]{:S(2)}) copy-start(f32[128]{0:T(128)} %get-tuple-element.44) | copy-start | bytes 1540
  1312.4 139.1 %copy-start.56 = (f32[128]{0:T(128)S(1)}, f32[128]{0:T(128)}, u32[]{:S(2)}) copy-start(f32[128]{0:T(128)} %get-tuple-element.62) | copy-start | bytes 1540
  1460.3 107.8 %copy-start.27 = (f32[128,2048]{1,0:T(8,128)S(1)}, f32[128,2048]{1,0:T(8,128)}, u32[]{:S(2)}) copy-start(f32[128,2048]{1,0:T(8,128)} %copy-done.26) | copy-start | bytes 3145732
  1460.3 107.8 %copy-start.37 = (bf16[1,128,2048]{1,2,0:T(8,128)(2,1)S(1)}, bf16[1,128,2048]{1,2,0:T(8,128)(2,1)}, u32[]{:S(2)}) copy-start(bf16[1,128,2048]{1,2,0:T(8,128)(2,1)} %copy-done.36) | copy-start | bytes 1572868
  1460.3 107.8 %copy-start.39 = (bf16[1,128,2048]{1,2,0:T(8,128)(2,1)S(1)}, bf16[1,128,2048]{1,2,0:T(8,128)(2,1)}, u32[]{:S(2)}) copy-start(bf16[1,128,2048]{1,2,0:T(8,128)(2,1)} %copy-done.38) | copy-start | bytes 1572868
  1460.3 107.8 %copy-start.41 = (bf16[1,128,2048]{1,2,0:T(8,128)(2,1)S(1)}, bf16[1,128,2048]{1,2,0:T(8,128)(2,1)}, u32[]{:S(2)}) copy-start(bf16[1,128,2048]{1,2,0:T(8,128)(2,1)} %copy-done.40) | copy-start | bytes 1572868
  1460.3 236.4 %all-reduce.3.cloned.1.call-start = ((), (), s32[]{:S(2)}) async-start(), calls=%async_computation.14 | async-start | bytes 6029312 | tf_op jit(solution)/shard_map/psum | solution.py:363
  (41 other events, 206.4 us)
Sparse Core Ops, SparseCore 0:
  9.5 29.8 all-gather.9
  41.0 201.5 all-gather.7
  244.1 28.4 all-gather.15
  274.6 74.6 all-gather.11
  351.8 72.8 all-gather.17
  426.0 582.0 all-gather.13
  1151.7 147.8 reduce-scatter.4
  1303.2 146.9 reduce-scatter.6
  1452.7 57.0 reduce-scatter.10
  1512.2 54.5 reduce-scatter.8
  1570.6 126.0 all-reduce.2
where the time goes:
time: 1720 us; the launch traced here: 1710 us
  waiting for transfers between devices  1390 us (81%)
  matrix products  217 us (13%)
  local copies, waits for them, and re-layouts  42.7 us (2%)
  other arithmetic  33.2 us (2%)
    all_gather x1, waiting for transfers between devices, per_device(): weight_piece = lax.all_gather(mlp_weight, 'wsh', axis=2, tiled=True)  566 us
    all_gather x1, waiting for transfers between devices, per_device(): lax.all_gather(attn_weight, 'wsh', axis=2, tiled=True)  197 us
    reduce_scatter x1, waiting for transfers between devices, per_device(): lax.psum_scatter(value_full, 'ctx', scatter_dimension=0, tiled=True)  133 us
    reduce_scatter x1, waiting for transfers between devices, per_device(): lax.psum_scatter(key_full, 'ctx', scatter_dimension=0, tiled=True)  126 us
    psum x1, waiting for transfers between devices, per_device(): model_grads, hidden_grads_out = lax.psum((shard_model, shard_hidden), 'ctx')  117 us
    all_gather x1, waiting for transfers between devices, per_device(): lax.all_gather(own_keys, 'ctx', axis=0, tiled=True)  67.9 us
    all_gather x1, waiting for transfers between devices, per_device(): lax.all_gather(own_values, 'ctx', axis=0, tiled=True)  67.7 us
    reduce_scatter x1, waiting for transfers between devices, per_device(): lax.psum_scatter(spread_model, 'wsh', scatter_dimension=2, tiled=True)  57 us
  transfers between devices with their start and end apart: 11, of which 10 were waited for; matrix products, arithmetic and copies ran while one was open for 8% of the time, Pallas kernels for 0%

commit v1 on v0

v1 whole, which is shorter than its diff:
```python
import math

import jax
import jax.numpy as jnp
from jax import lax
from jax.sharding import PartitionSpec as P

HEADS = 16
HEAD_DIM = 128
RANK = 16
ADAPTERS = 4
NORM_EPS = 1e-06
ADAPTER_SCALE = 4.0
ROPE_BASE = 500000.0
F32 = jnp.float32
BF16 = jnp.bfloat16
CORE_SWAP = ((0, 1), (1, 0), (2, 3), (3, 2))
CHIP_SWAP = ((0, 2), (2, 0), (1, 3), (3, 1))


def dot(left, right, dims):
    return lax.dot_general(left, right, (dims, ((), ())), preferred_element_type=F32)


def mm(left, right):
    return dot(left, right, ((1,), (0,)))


def mm_t(left, right):
    return dot(left, right, ((1,), (1,)))


def tmm(left, right):
    return dot(left, right, ((0,), (0,)))


def swap_core(values):
    return lax.ppermute(values, "wsh", CORE_SWAP)


def swap_chip(values):
    return lax.ppermute(values, "wsh", CHIP_SWAP)


def sum_wsh(values):
    values = values + swap_core(values)
    return values + swap_chip(values)


def gather_wsh(block, axis, me):
    far = swap_chip(block)
    near = swap_core(block)
    far_near = swap_core(far)
    extent = block.shape[axis]
    shape = list(block.shape)
    shape[axis] = 4 * extent
    whole = jnp.zeros(shape, block.dtype)
    for flip, piece in ((0, block), (1, near), (2, far), (3, far_near)):
        start = [0] * block.ndim
        start[axis] = (me ^ flip) * extent
        whole = lax.dynamic_update_slice(whole, piece, start)
    return whole


def scatter_wsh(partial, axis, me):
    extent = partial.shape[axis] // 4

    def piece(flip):
        return lax.dynamic_slice_in_dim(partial, (me ^ flip) * extent, extent, axis)

    far = piece(2).astype(F32) + swap_core(piece(3)).astype(F32)
    far = swap_chip(far.astype(BF16))
    near = piece(0).astype(F32) + swap_core(piece(1)).astype(F32)
    return near + far.astype(F32)


def rotate(values, cosine, sine_part):
    half = HEAD_DIM // 2
    first, second = values[..., :half], values[..., half:]
    return jnp.concatenate(
        [first * cosine - second * sine_part, second * cosine + first * sine_part], axis=-1
    )


def per_device(
    tokens,
    out_grad,
    attn_weight,
    mlp_weight,
    norm_gains,
    adapt_model,
    adapt_hidden,
    lengths,
    adapter_pick,
    block_order,
):
    own_rows = tokens[0]
    rows, model_dim = own_rows.shape
    block_rows = rows // 2
    ctx_size = lax.axis_size("ctx")
    seqs = lax.axis_size("wsh")
    width = model_dim // seqs
    local_heads = width // HEAD_DIM
    me = lax.axis_index("wsh")
    ctx_index = lax.axis_index("ctx")
    pairs = seqs * local_heads
    members = math.gcd(ctx_size, pairs)
    groups = ctx_size // members
    per_member = pairs // members
    splits = local_heads // per_member
    group_rows = members * rows
    member = ctx_index % members
    group = ctx_index // members
    ctx_groups = [[g * members + i for i in range(members)] for g in range(groups)]
    key_groups = [[g * members + i for g in range(groups)] for i in range(members)]
    score_scale = HEAD_DIM ** (-0.5)
    all_rows = seqs * rows

    def columns(matrix):
        return lax.dynamic_slice_in_dim(matrix, me * width, width, 1)

    orders = gather_wsh(block_order, 0, me)
    positions = (orders[:, :, None] * block_rows + jnp.arange(block_rows)[None, None, :]).reshape(
        seqs, -1
    )
    row_positions = lax.dynamic_slice_in_dim(positions, ctx_index * rows, rows, 1)
    own_positions = lax.dynamic_index_in_dim(row_positions, me, keepdims=False)
    own_length = lax.dynamic_index_in_dim(lengths, me, keepdims=False)
    valid_rows = (own_positions < own_length).astype(F32)[:, None]
    half_dim = HEAD_DIM // 2
    frequency = ROPE_BASE ** (-(jnp.arange(half_dim, dtype=F32) * 2.0) / HEAD_DIM)
    angles = row_positions.reshape(-1).astype(F32)[:, None] * frequency[None, :]
    cosine, sine_part = jnp.cos(angles)[:, None, :], jnp.sin(angles)[:, None, :]
    picked = (jnp.arange(ADAPTERS * RANK)[None, :] // RANK == adapter_pick[:, None]).astype(F32)
    row_mask = jnp.broadcast_to(picked[:, None, :], (seqs, rows, ADAPTERS * RANK)).reshape(
        all_rows, -1
    )

    def low(product):
        return (product * row_mask).astype(BF16)

    def low_sum(partial):
        narrow = (partial * row_mask).reshape(all_rows, ADAPTERS, RANK).sum(1)
        total = jnp.tile(sum_wsh(narrow), (1, ADAPTERS))
        return (total * row_mask).astype(BF16)

    gains = norm_gains.astype(F32)
    last_gain = gather_wsh(norm_gains[3:4], 1, me).astype(F32)

    hidden = gather_wsh(own_rows, 0, me)
    rows_a = gather_wsh(jnp.concatenate([adapt_model[:6], adapt_model[10:11]], 0), 2, me)
    low_in = [low(mm_t(hidden, rows_a[k])) for k in range(3)]
    proj = [
        mm(hidden, attn_weight[k]) + ADAPTER_SCALE * mm(low_in[k], adapt_model[6 + k])
        for k in range(3)
    ]
    squares = jnp.stack([jnp.sum(proj[0] * proj[0], -1), jnp.sum(proj[1] * proj[1], -1)])
    scales = lax.rsqrt(sum_wsh(squares) / model_dim + NORM_EPS)[:, :, None]

    def heads(values):
        return values.reshape(all_rows, local_heads, HEAD_DIM)

    turned = [
        rotate(heads(proj[k] * scales[k] * gains[k]), cosine, sine_part).astype(BF16)
        for k in range(2)
    ]
    packed = jnp.stack([turned[0], turned[1], heads(proj[2].astype(BF16))])

    def to_heads(values):
        count = values.shape[0]
        shaped = values.reshape(count, seqs, rows, splits, per_member * HEAD_DIM)
        shaped = shaped.transpose(1, 3, 0, 2, 4).reshape(
            members, count, rows, per_member * HEAD_DIM
        )
        moved = lax.all_to_all(shaped, "ctx", 0, 0, tiled=True, axis_index_groups=ctx_groups)
        moved = moved.transpose(1, 0, 2, 3).reshape(count, group_rows, per_member, HEAD_DIM)
        return moved.transpose(0, 2, 1, 3)

    def to_rows(values):
        count = values.shape[0]
        shaped = values.transpose(0, 2, 1, 3).reshape(
            count, members, rows, per_member * HEAD_DIM
        )
        moved = lax.all_to_all(
            shaped.transpose(1, 0, 2, 3),
            "ctx",
            0,
            0,
            tiled=True,
            axis_index_groups=ctx_groups,
        )
        moved = moved.reshape(seqs, splits, count, rows, per_member * HEAD_DIM)
        return moved.transpose(2, 0, 3, 1, 4).reshape(count, all_rows, width)

    queries, keys, values = to_heads(packed)
    if groups > 1:
        keys, values = (
            lax.all_gather(part, "ctx", axis=1, tiled=True, axis_index_groups=key_groups)
            for part in (keys, values)
        )
    seq_here = (member * per_member) // local_heads
    key_positions = lax.dynamic_index_in_dim(positions, seq_here, keepdims=False)
    query_positions = lax.dynamic_slice_in_dim(key_positions, group * group_rows, group_rows)
    length_here = lax.dynamic_index_in_dim(lengths, seq_here, keepdims=False)
    allowed = (key_positions[None, :] <= query_positions[:, None]) & (
        key_positions[None, :] < length_here
    )

    def batched(left, right, lc, rc):
        return lax.dot_general(
            left, right, (((lc,), (rc,)), ((0,), (0,))), preferred_element_type=F32
        )

    scores = jnp.where(allowed[None], batched(queries, keys, 2, 2) * score_scale, -jnp.inf)
    row_max = jnp.max(scores, axis=-1, keepdims=True)
    log_total = row_max + jnp.log(jnp.sum(jnp.exp(scores - row_max), axis=-1, keepdims=True))
    weights = jnp.exp(scores - log_total).astype(BF16)
    attended = batched(weights, values, 2, 1).astype(BF16)
    attended = to_rows(attended[None])[0]

    attended_full = gather_wsh(attended, 1, me)
    low_out = low(mm_t(attended_full, rows_a[3]))
    branch = mm(attended_full, attn_weight[3]) + ADAPTER_SCALE * mm(low_out, adapt_model[9])
    branch_scale = lax.rsqrt(
        sum_wsh(jnp.sum(branch * branch, -1, keepdims=True)) / model_dim + NORM_EPS
    )
    mid = columns(hidden).astype(F32) + branch * branch_scale * gains[2]
    mid_low = mid.astype(BF16)
    mid_full = gather_wsh(mid_low, 1, me)

    low_gate = low(mm_t(mid_full, rows_a[4]))
    low_up = low(mm_t(mid_full, rows_a[5]))
    gate = mm(mid_full, mlp_weight[0]) + ADAPTER_SCALE * mm(low_gate, adapt_hidden[0])
    up = mm(mid_full, mlp_weight[1]) + ADAPTER_SCALE * mm(low_up, adapt_hidden[1])
    sigmoid_gate = jax.nn.sigmoid(gate)
    silu_gate = gate * sigmoid_gate
    product = (silu_gate * up).astype(BF16)
    low_down_part = mm_t(product, adapt_hidden[2])
    down_part = mm_t(product, mlp_weight[2]) + ADAPTER_SCALE * mm(low(low_down_part), rows_a[6])
    down = scatter_wsh(down_part.astype(BF16), 0, me)
    low_down = low_sum(low_down_part)
    down_scale = lax.rsqrt(jnp.mean(down * down, axis=-1, keepdims=True) + NORM_EPS)
    mid_rows = lax.dynamic_slice_in_dim(mid_full, me * rows, rows, 0).astype(F32)
    result = mid_rows + down * down_scale * last_gain

    upstream = out_grad[0].astype(F32) * valid_rows
    scaled = upstream * last_gain
    grad_down = (
        down_scale * scaled
        - down * down_scale**3 * jnp.mean(scaled * down, axis=-1, keepdims=True)
    ).astype(BF16)
    grad_down = gather_wsh(grad_down, 0, me)
    grad_low_down = low(ADAPTER_SCALE * mm_t(grad_down, rows_a[6]))
    grad_product = mm(grad_down, mlp_weight[2]) + mm(grad_low_down, adapt_hidden[2])
    grad_gate = (
        grad_product * up * sigmoid_gate * (1.0 + gate * (1.0 - sigmoid_gate))
    ).astype(BF16)
    grad_up = (grad_product * silu_gate).astype(BF16)
    low_gate_part = ADAPTER_SCALE * mm_t(grad_gate, adapt_hidden[0])
    low_up_part = ADAPTER_SCALE * mm_t(grad_up, adapt_hidden[1])
    own_block = (jnp.arange(seqs) == me).astype(F32)[:, None, None]
    mid_part = (
        mm_t(grad_gate, mlp_weight[0])
        + mm_t(grad_up, mlp_weight[1])
        + mm(low(low_gate_part), rows_a[4])
        + mm(low(low_up_part), rows_a[5])
        + (own_block * upstream[None]).reshape(all_rows, model_dim)
    )
    grad_mid = scatter_wsh(mid_part.astype(BF16), 1, me)
    grad_low_gate = low_sum(low_gate_part)
    grad_low_up = low_sum(low_up_part)
    hidden_grads = jnp.stack(
        [
            ADAPTER_SCALE * tmm(low_gate, grad_gate),
            ADAPTER_SCALE * tmm(low_up, grad_up),
            tmm(grad_low_down, product),
        ]
    )
    grad_a_gate = tmm(grad_low_gate, mid_low)
    grad_a_up = tmm(grad_low_up, mid_low)
    grad_b_down = ADAPTER_SCALE * tmm(low_down, columns(grad_down))

    scaled = grad_mid * gains[2]
    mean = sum_wsh(jnp.sum(scaled * branch, axis=-1, keepdims=True)) / model_dim
    grad_branch = (branch_scale * scaled - branch * branch_scale**3 * mean).astype(BF16)
    low_out_part = ADAPTER_SCALE * mm_t(grad_branch, adapt_model[9])
    attended_part = mm_t(grad_branch, attn_weight[3]) + mm(low(low_out_part), rows_a[3])
    grad_attended = scatter_wsh(attended_part.astype(BF16), 1, me).astype(BF16)
    grad_low_out = low_sum(low_out_part)
    grad_b_out = ADAPTER_SCALE * tmm(low_out, grad_branch)
    grad_a_out = tmm(grad_low_out, attended)

    grad_heads = to_heads(grad_attended[None])[0]
    scores = jnp.where(allowed[None], batched(queries, keys, 2, 2) * score_scale, -jnp.inf)
    weights_full = jnp.exp(scores - log_total)
    grad_probs = batched(grad_heads, values, 2, 2)
    delta = jnp.sum(weights_full * grad_probs, axis=-1, keepdims=True)
    grad_scores = (weights_full * (grad_probs - delta)).astype(BF16)
    grad_queries = batched(grad_scores, keys, 2, 1) * score_scale
    grad_keys = batched(grad_scores, queries, 1, 1) * score_scale
    grad_values = batched(weights_full.astype(BF16), grad_heads, 1, 1)
    if groups > 1:
        grad_keys, grad_values = (
            lax.psum_scatter(
                part, "ctx", scatter_dimension=1, tiled=True, axis_index_groups=key_groups
            )
            for part in (grad_keys, grad_values)
        )
    grads = to_rows(jnp.stack([grad_queries, grad_keys, grad_values]).astype(BF16))
    turned = [
        rotate(heads(grads[k].astype(F32)), cosine, -sine_part).reshape(all_rows, width) * gains[k]
        for k in range(2)
    ]
    sums = jnp.stack([jnp.sum(turned[k] * proj[k], -1) for k in range(2)])
    means = (sum_wsh(sums) / model_dim)[:, :, None]
    grad_proj = [
        (scales[k] * turned[k] - proj[k] * scales[k] ** 3 * means[k]).astype(BF16)
        for k in range(2)
    ] + [grads[2]]
    low_parts = [ADAPTER_SCALE * mm_t(grad_proj[k], adapt_model[6 + k]) for k in range(3)]
    own_column = (jnp.arange(seqs) == me).astype(F32)[None, :, None]
    input_part = (
        mm_t(grad_proj[0], attn_weight[0])
        + mm_t(grad_proj[1], attn_weight[1])
        + mm_t(grad_proj[2], attn_weight[2])
        + mm(low(low_parts[0]), rows_a[0])
        + mm(low(low_parts[1]), rows_a[1])
        + mm(low(low_parts[2]), rows_a[2])
        + (own_column * grad_mid[:, None, :]).reshape(all_rows, model_dim)
    )
    grad_inputs = scatter_wsh(input_part.astype(BF16), 0, me)
    own_hidden = columns(hidden)
    grad_a_in = [tmm(low_sum(low_parts[k]), own_hidden) for k in range(3)]
    grad_b_in = [ADAPTER_SCALE * tmm(low_in[k], grad_proj[k]) for k in range(3)]
    model_grads = jnp.stack(
        grad_a_in + [grad_a_out, grad_a_gate, grad_a_up] + grad_b_in + [grad_b_out, grad_b_down]
    )
    model_grads = lax.psum(model_grads, "ctx")
    hidden_grads = lax.psum(hidden_grads, "ctx")
    return (result.astype(BF16)[None], grad_inputs[None], model_grads, hidden_grads)


def solution(mesh):
    in_specs = (
        P("wsh", "ctx", None),
        P("wsh", "ctx", None),
        P(None, None, "wsh"),
        P(None, None, "wsh"),
        P(None, "wsh"),
        P(None, None, "wsh"),
        P(None, None, "wsh"),
        P(),
        P(),
        P("wsh", None),
    )
    out_specs = (
        P("wsh", "ctx", None),
        P("wsh", "ctx", None),
        P(None, None, "wsh"),
        P(None, None, "wsh"),
    )
    return jax.shard_map(
        per_device, mesh=mesh, in_specs=in_specs, out_specs=out_specs, check_vma=False
    )
```

time: 1720 us -> 666 us (0.39)
  waiting for transfers between devices: 1390 us -> 250 us
  matrix products: 217 us -> 167 us
  starting transfers between devices: 0.66 us -> 46.8 us
  local copies, waits for them, and re-layouts: 42.7 us -> 87.8 us
  blocking collectives: 6.39 us -> 37 us
  other arithmetic: 33.2 us -> 51.1 us
    all_gather x6 -> x0, waiting for transfers between devices: 908 us -> none  [the longest x1 566 us: per_device(): weight_piece = lax.all_gather(mlp_weight, 'wsh', axis=2, tiled=True)]
    reduce_scatter x4 -> x0, waiting for transfers between devices: 365 us -> none  [the longest x1 133 us: per_device(): lax.psum_scatter(value_full, 'ctx', scatter_dimension=0, tiled=True)]
    ppermute x0 -> x55, waiting for transfers between devices: none -> 117 us  [the longest x22 102 us: swap_chip(): return lax.ppermute(values, 'wsh', CHIP_SWAP)]
    dot_general x45 -> x62, matrix products: 217 us -> 167 us  [the longest x56 145 us: dot(): lax.dot_general(left, right, (dims, ((), ())), preferred_element_type=F32)]
    all_to_all x0 -> x2, waiting for transfers between devices: none -> 38.7 us  [the longest x1 34 us: to_heads(): lax.all_to_all(shaped, 'ctx', 0, 0, tiled=True, axis_index_groups=ctx_gro...]
    all_to_all x0 -> x2, blocking collectives: none -> 37 us  [the longest x1 18.6 us: to_heads(): lax.all_to_all(shaped, 'ctx', 0, 0, tiled=True, axis_index_groups=ctx_gro...]
    ppermute x0 -> x55, starting transfers between devices: none -> 35.7 us  [the longest x22 30 us: swap_chip(): return lax.ppermute(values, 'wsh', CHIP_SWAP)]
    psum x1, waiting for transfers between devices: 117 us -> 93.8 us  [per_device(): model_grads = lax.psum(model_grads, 'ctx')]
  transfers between devices with their start and end apart: 11 -> 58, of which waited for: 10 -> 27; matrix products, arithmetic and copies ran while one was open for 8% -> 15% of each run, Pallas kernels for 0% -> 0%
where the time goes in v1:
time: 666 us; the launch traced here: 656 us
  waiting for transfers between devices  250 us (38%)
  matrix products  167 us (25%)
  local copies, waits for them, and re-layouts  87.8 us (13%)
  other arithmetic  51.1 us (8%)
  starting transfers between devices  46.8 us (7%)
  blocking collectives  37 us (6%)
  between operations  16.2 us (2%)
    dot_general x56, matrix products, dot(): lax.dot_general(left, right, (dims, ((), ())), preferred_element_type=F32)  145 us
    ppermute x22, waiting for transfers between devices, swap_chip(): return lax.ppermute(values, 'wsh', CHIP_SWAP)  102 us
    psum x1, waiting for transfers between devices, per_device(): model_grads = lax.psum(model_grads, 'ctx')  93.8 us
    all_to_all x1, waiting for transfers between devices, to_heads(): lax.all_to_all(shaped, 'ctx', 0, 0, tiled=True, axis_index_groups=ctx_gro...  34 us
    ppermute x22, starting transfers between devices, swap_chip(): return lax.ppermute(values, 'wsh', CHIP_SWAP)  30 us
    unnamed x222, local copies, waits for them, and re-layouts  22.5 us
    dot_general x6, matrix products, batched(): lax.dot_general(left, right, (((lc,), (rc,)), ((0,), (0,))), preferred_el...  21.8 us
    all_to_all x1, blocking collectives, to_heads(): lax.all_to_all(shaped, 'ctx', 0, 0, tiled=True, axis_index_groups=ctx_gro...  18.6 us
  transfers between devices with their start and end apart: 58, of which 27 were waited for; matrix products, arithmetic and copies ran while one was open for 15% of the time, Pallas kernels for 0%

profile of v1, /device:TPU:0, one launch (start us, length us, event | category | flops | bytes accessed | tf_op | source)
XLA Modules:
  0.0 655.7 jit_solution(950616927271443762)
XLA Ops:
  20.7 15.3 %collective-permute-done.7 = bf16[7,64,512]{2,1,0:T(8,128)(2,1)} collective-permute-done((bf16[7,64,512]{2,1,0:T(8,128)(2,1)}, bf16[7,64,512]{2,1,0:T(8,128)(2,1)}, u32[]{:S(2)}, u32[]{:S(2)}) %collective-permute-start.7) | collective-permute-done | bytes 458784 | tf_op jit(solution)/shard_map/ppermute | solution.py:42
  68.4 3.7 copy.160
  72.2 6.4 all-to-all-start
  81.7 34.0 %all-to-all-done = bf16[8,3,128,256]{3,2,1,0:T(8,128)(2,1)} async-done(((bf16[8,3,128,256]{3,2,1,0:T(8,128)(2,1)}), bf16[8,3,128,256]{3,2,1,0:T(8,128)(2,1)}, u32[]{:S(2)}, u32[]{:S(2)}) %all-to-all-start) | async-done | bytes 1572896 | tf_op jit(solution)/shard_map/all_to_all | solution.py:175
  131.0 4.8 fusion.75
  139.1 18.4 %all_to_all.20 = bf16[8,1,128,256]{2,3,1,0:T(8,128)(2,1)} all-to-all(bf16[8,1,128,256]{2,3,1,0:T(8,128)(2,1)S(1)} %copy.165), channel_id=1, replica_groups={{0,4,8,12,16,20,24,28},{1,5,9,13,17,21,25,29},{2,6,10,14,18,22,26,30},{..., dimensions={0} | all-to-all | bytes 1048576 | tf_op jit(solution)/shard_map/all_to_all | solution.py:184
  164.5 11.0 %collective-permute-done.12 = bf16[512,512]{0,1:T(8,128)(2,1)S(1)} collective-permute-done((bf16[512,512]{0,1:T(8,128)(2,1)S(1)}, bf16[512,512]{0,1:T(8,128)(2,1)S(1)}, u32[]{:S(2)}, u32[]{:S(2)}) %collective-permute-start.12) | collective-permute-done | bytes 524320 | tf_op jit(solution)/shard_map/ppermute | solution.py:42
  189.8 11.3 %collective-permute-done.17 = bf16[512,512]{0,1:T(8,128)(2,1)S(1)} collective-permute-done((bf16[512,512]{0,1:T(8,128)(2,1)S(1)}, bf16[512,512]{0,1:T(8,128)(2,1)S(1)}, u32[]{:S(2)}, u32[]{:S(2)}) %collective-permute-start.17) | collective-permute-done | bytes 524320 | tf_op jit(solution)/shard_map/ppermute | solution.py:42
  207.7 11.6 %multiply_add_fusion.1 = f32[512,2048]{0,1:T(8,128)} fusion(f32[512,2048]{0,1:T(8,128)S(1)} %fusion.137, bf16[512,2048]{0,1:T(8,128)(2,1)S(1)} %constant_dynamic-update-slice_fusion.4, bf16[3,2048,2048]{2,1,0:T(8,128)(2,1)} %param.13), kind=kOutput, calls=%fused_computation.37 | convolution fusion | flops 4297064448 | bytes 18874368 | tf_op jit(solution)/shard_map/dot_general | solution.py:22
  219.3 13.1 %multiply_convert_fusion.3 = (bf16[512,2048]{0,1:T(8,128)(2,1)S(1)}, f32[512,2048]{0,1:T(8,128)}) fusion(f32[512,2048]{0,1:T(8,128)} %multiply_add_fusion.1, f32[512,2048]{0,1:T(8,128)S(1)} %fusion.134, bf16[512,2048]{0,1:T(8,128)(2,1)S(1)} %constant_dynamic-update-slice_fusion.4, bf16[3,2048,2048]{2,1,0:T(8,128)(2,1)} %param.13), kind=kOutput, calls=%fused_computation.33 | convolution fusion | flops 4303355904 | bytes 25165824 | tf_op jit(solution)/shard_map/dot_general | solution.py:22
  232.9 7.1 %fusion.2 = f32[512,2048]{0,1:T(8,128)S(1)} fusion(bf16[512,2048]{0,1:T(8,128)(2,1)S(1)} %get-tuple-element.95, bf16[3,2048,2048]{2,1,0:T(8,128)(2,1)} %param.13), kind=kOutput, calls=%fused_computation.2 | convolution fusion | flops 4294967296 | bytes 14680064 | tf_op jit(solution)/shard_map/dot_general | solution.py:22
  250.0 10.0 %collective-permute-done.23 = bf16[1,512]{1,0:T(2,128)(2,1)S(1)} collective-permute-done((bf16[1,512]{1,0:T(2,128)(2,1)S(1)}, bf16[1,512]{1,0:T(2,128)(2,1)S(1)}, u32[]{:S(2)}, u32[]{:S(2)}) %collective-permute-start.23) | collective-permute-done | bytes 1056 | tf_op jit(solution)/shard_map/ppermute | solution.py:42
  268.0 12.4 %collective-permute-done.26 = bf16[128,2048]{0,1:T(8,128)(2,1)S(1)} collective-permute-done((bf16[128,2048]{0,1:T(8,128)(2,1)S(1)}, bf16[128,2048]{0,1:T(8,128)(2,1)S(1)}, u32[]{:S(2)}, u32[]{:S(2)}) %collective-permute-start.26) | collective-permute-done | bytes 524320 | tf_op jit(solution)/shard_map/ppermute | solution.py:42
  284.9 10.0 %multiply_convert_fusion.1 = (bf16[512,2048]{0,1:T(8,128)(2,1)S(1)}, bf16[512,2048]{0,1:T(8,128)(2,1)S(1)}) fusion(f32[512,2048]{0,1:T(8,128)} %multiply_add_fusion.1, f32[512,2048]{0,1:T(8,128)} %get-tuple-element.96, f32[512,2048]{0,1:T(8,128)S(1)} %fusion.130, bf16[512,2048]{0,1:T(8,128)(2,1)S(1)} %constant_dynamic-update-slice_fusion, ...), kind=kOutput, calls=%fused_computation.30 | convolution fusion | flops 4309647360 | bytes 27262976 | tf_op jit(solution)/shard_map/dot_general | solution.py:22
  295.4 7.9 %fusion.8 = f32[512,2048]{0,1:T(8,128)S(1)} fusion(bf16[512,2048]{0,1:T(8,128)(2,1)S(1)} %get-tuple-element.39, bf16[3,2048,2048]{2,1,0:T(8,128)(2,1)} %param.13), kind=kOutput, calls=%fused_computation.8 | convolution fusion | flops 4294967296 | bytes 14680064 | tf_op jit(solution)/shard_map/dot_general | solution.py:22
  303.8 6.9 %fusion.4 = f32[512,2048]{0,1:T(8,128)S(1)} fusion(bf16[512,2048]{0,1:T(8,128)(2,1)S(1)} %get-tuple-element.38, bf16[3,2048,2048]{2,1,0:T(8,128)(2,1)} %param.13), kind=kOutput, calls=%fused_computation.4 | convolution fusion | flops 4294967296 | bytes 14680064 | tf_op jit(solution)/shard_map/dot_general | solution.py:22
  319.4 12.4 %collective-permute-done.30 = bf16[512,512]{0,1:T(8,128)(2,1)S(1)} collective-permute-done((bf16[512,512]{0,1:T(8,128)(2,1)S(1)}, bf16[512,512]{0,1:T(8,128)(2,1)S(1)}, u32[]{:S(2)}, u32[]{:S(2)}) %collective-permute-start.30) | collective-permute-done | bytes 524320 | tf_op jit(solution)/shard_map/ppermute | solution.py:42
  346.0 12.4 %collective-permute-done.35 = bf16[512,512]{1,0:T(8,128)(2,1)S(1)} collective-permute-done((bf16[512,512]{1,0:T(8,128)(2,1)S(1)}, bf16[512,512]{1,0:T(8,128)(2,1)S(1)}, u32[]{:S(2)}, u32[]{:S(2)}) %collective-permute-start.35) | collective-permute-done | bytes 524320 | tf_op jit(solution)/shard_map/ppermute | solution.py:42
  362.5 18.6 %all_to_all.21 = bf16[8,1,128,256]{3,2,1,0:T(8,128)(2,1)} all-to-all(bf16[8,1,128,256]{3,2,1,0:T(8,128)(2,1)S(1)} %bitcast.544), channel_id=1, replica_groups={{0,4,8,12,16,20,24,28},{1,5,9,13,17,21,25,29},{2,6,10,14,18,22,26,30},{..., dimensions={0} | all-to-all | bytes 1048576 | tf_op jit(solution)/shard_map/all_to_all | solution.py:175
  383.1 5.5 fusion.76
  388.6 5.5 multiply_reduce_fusion
  407.2 4.5 all-to-all-start.3
  438.5 4.0 copy.219
  443.1 4.7 all-to-all-done.3
  470.0 5.0 fusion.36
  481.6 5.1 fusion.40
  488.7 4.9 fusion.44
  496.2 3.8 fusion.139
  505.3 3.7 fusion.140
  520.6 10.5 %add_convert_fusion = bf16[512,2048]{1,0:T(8,128)(2,1)S(1)} fusion(f32[512,2048]{1,0:T(8,128)} %bitcast.518, f32[512,2048]{1,0:T(8,128)} %fusion.140, f32[512,2048]{1,0:T(8,128)} %fusion.139, f32[512,2048]{1,0:T(8,128)} %fusion.36, f32[512,2048]{1,0:T(8,128)} %fusion.44, f32[512,2048]{1,0:T(8,128)} %fusion.40, f32[2048]{0:T(1024)S(1)} %bitcast.557, ...), kind=kOutput, calls=%fused_computation.28 | convolution fusion | flops 142639104 | bytes 27664384 | tf_op jit(solution)/shard_map/dot_general | solution.py:22
  537.7 10.7 %collective-permute-done.40 = bf16[128,2048]{1,0:T(8,128)(2,1)} collective-permute-done((bf16[128,2048]{1,0:T(8,128)(2,1)S(1)}, bf16[128,2048]{1,0:T(8,128)(2,1)}, u32[]{:S(2)}, u32[]{:S(2)}) %collective-permute-start.40) | collective-permute-done | bytes 524320 | tf_op jit(solution)/shard_map/ppermute | solution.py:42
  551.0 93.8 %all-reduce.3.cloned.1.call-done = (f32[11,64,512]{2,1,0:T(8,128)}, f32[3,64,2048]{2,1,0:T(8,128)}) async-done(((f32[11,64,512]{2,1,0:T(8,128)}, f32[3,64,2048]{2,1,0:T(8,128)}), (f32[11,64,512]{2,1,0:T(8,128)}, f32[3,64,2048]{2,1,0:T(8,128)})) %all-reduce.3.cloned.1.call-update) | async-done | bytes 3014672 | tf_op jit(solution)/shard_map/psum | solution.py:338
  (535 shorter events, 250.6 us)
Async XLA Ops:
  7.2 10.8 %collective-permute-start.4 = (s32[1,16]{1,0:T(1,128)}, s32[1,16]{1,0:T(1,128)S(1)}, u32[]{:S(2)}, u32[]{:S(2)}) collective-permute-start(s32[1,16]{1,0:T(1,128)} %param.19), channel_id=1, source_target_pairs={{0,2},{2,0},{1,3},{3,1},{4,6},{6,4},{5,7},{7,5},{8,10},{10,8},{9,1... | collective-permute-start | bytes 200 | tf_op jit(solution)/shard_map/ppermute | solution.py:42
  10.2 5.8 collective-permute-start.3
  11.5 27.8 %collective-permute-start = (bf16[128,2048]{0,1:T(8,128)(2,1)S(1)}, bf16[128,2048]{0,1:T(8,128)(2,1)}, u32[]{:S(2)}, u32[]{:S(2)}) collective-permute-start(bf16[128,2048]{0,1:T(8,128)(2,1)S(1)} %bitcast.539), channel_id=1, source_target_pairs={{0,1},{1,0},{2,3},{3,2},{4,5},{5,4},{6,7},{7,6},{8,9},{9,8},{10,11... | collective-permute-start | bytes 1572872 | tf_op jit(solution)/shard_map/ppermute | solution.py:38
  12.1 26.7 %collective-permute-start.1 = (bf16[128,2048]{0,1:T(8,128)(2,1)S(1)}, bf16[128,2048]{0,1:T(8,128)(2,1)}, u32[]{:S(2)}, u32[]{:S(2)}) collective-permute-start(bf16[128,2048]{0,1:T(8,128)(2,1)S(1)} %bitcast.540), channel_id=1, source_target_pairs={{0,2},{2,0},{1,3},{3,1},{4,6},{6,4},{5,7},{7,5},{8,10},{10,8},{9,1... | collective-permute-start | bytes 1572872 | tf_op jit(solution)/shard_map/ppermute | solution.py:42
  14.7 21.3 %collective-permute-start.6 = (bf16[7,64,512]{2,1,0:T(8,128)(2,1)}, bf16[7,64,512]{2,1,0:T(8,128)(2,1)S(1)}, u32[]{:S(2)}, u32[]{:S(2)}) collective-permute-start(bf16[7,64,512]{2,1,0:T(8,128)(2,1)} %get-tuple-element.59), channel_id=1, source_target_pairs={{0,1},{1,0},{2,3},{3,2},{4,5},{5,4},{6,7},{7,6},{8,9},{9,8},{10,11... | collective-permute-start | bytes 1376264 | tf_op jit(solution)/shard_map/ppermute | solution.py:38
  16.0 20.0 %collective-permute-start.7 = (bf16[7,64,512]{2,1,0:T(8,128)(2,1)}, bf16[7,64,512]{2,1,0:T(8,128)(2,1)}, u32[]{:S(2)}, u32[]{:S(2)}) collective-permute-start(bf16[7,64,512]{2,1,0:T(8,128)(2,1)} %get-tuple-element.59), channel_id=1, source_target_pairs={{0,2},{2,0},{1,3},{3,1},{4,6},{6,4},{5,7},{7,5},{8,10},{10,8},{9,1... | collective-permute-start | bytes 1376264 | tf_op jit(solution)/shard_map/ppermute | solution.py:42
  36.0 5.8 collective-permute-start.8
  72.2 43.5 %all-to-all-start = ((bf16[8,3,128,256]{3,2,1,0:T(8,128)(2,1)}), bf16[8,3,128,256]{3,2,1,0:T(8,128)(2,1)}, u32[]{:S(2)}, u32[]{:S(2)}) async-start(bf16[8,3,128,256]{3,2,1,0:T(8,128)(2,1)} %bitcast.528), calls=%async_computation | async-start | bytes 3145728 | tf_op jit(solution)/shard_map/all_to_all | solution.py:175
  162.8 12.7 %collective-permute-start.12 = (bf16[512,512]{0,1:T(8,128)(2,1)S(1)}, bf16[512,512]{0,1:T(8,128)(2,1)S(1)}, u32[]{:S(2)}, u32[]{:S(2)}) collective-permute-start(bf16[512,512]{0,1:T(8,128)(2,1)S(1)} %bitcast.553), channel_id=1, source_target_pairs={{0,2},{2,0},{1,3},{3,1},{4,6},{6,4},{5,7},{7,5},{8,10},{10,8},{9,1... | collective-permute-start | bytes 1572872 | tf_op jit(solution)/shard_map/ppermute | solution.py:42
  164.5 11.3 %collective-permute-start.11 = (bf16[512,512]{0,1:T(8,128)(2,1)S(1)}, bf16[512,512]{0,1:T(8,128)(2,1)S(1)}, u32[]{:S(2)}, u32[]{:S(2)}) collective-permute-start(bf16[512,512]{0,1:T(8,128)(2,1)S(1)} %bitcast.554), channel_id=1, source_target_pairs={{0,1},{1,0},{2,3},{3,2},{4,5},{5,4},{6,7},{7,6},{8,9},{9,8},{10,11... | collective-permute-start | bytes 1572872 | tf_op jit(solution)/shard_map/ppermute | solution.py:38
  188.2 12.8 %collective-permute-start.17 = (bf16[512,512]{0,1:T(8,128)(2,1)S(1)}, bf16[512,512]{0,1:T(8,128)(2,1)S(1)}, u32[]{:S(2)}, u32[]{:S(2)}) collective-permute-start(bf16[512,512]{0,1:T(8,128)(2,1)S(1)} %get-tuple-element.35), channel_id=1, source_target_pairs={{0,2},{2,0},{1,3},{3,1},{4,6},{6,4},{5,7},{7,5},{8,10},{10,8},{9,1... | collective-permute-start | bytes 1572872 | tf_op jit(solution)/shard_map/ppermute | solution.py:42
  189.8 11.3 %collective-permute-start.16 = (bf16[512,512]{0,1:T(8,128)(2,1)S(1)}, bf16[512,512]{0,1:T(8,128)(2,1)S(1)}, u32[]{:S(2)}, u32[]{:S(2)}) collective-permute-start(bf16[512,512]{0,1:T(8,128)(2,1)S(1)} %get-tuple-element.35), channel_id=1, source_target_pairs={{0,1},{1,0},{2,3},{3,2},{4,5},{5,4},{6,7},{7,6},{8,9},{9,8},{10,11... | collective-permute-start | bytes 1572872 | tf_op jit(solution)/shard_map/ppermute | solution.py:38
  242.9 19.3 %collective-permute-start.19 = (bf16[128,2048]{0,1:T(8,128)(2,1)}, bf16[128,2048]{0,1:T(8,128)(2,1)}, u32[]{:S(2)}, u32[]{:S(2)}) collective-permute-start(bf16[128,2048]{0,1:T(8,128)(2,1)} %get-tuple-element.46), channel_id=1, source_target_pairs={{0,1},{1,0},{2,3},{3,2},{4,5},{5,4},{6,7},{7,6},{8,9},{9,8},{10,11... | collective-permute-start | bytes 1572872 | tf_op jit(solution)/shard_map/ppermute | solution.py:38
  245.6 16.6 %collective-permute-start.21 = (bf16[128,2048]{0,1:T(8,128)(2,1)}, bf16[128,2048]{0,1:T(8,128)(2,1)}, u32[]{:S(2)}, u32[]{:S(2)}) collective-permute-start(bf16[128,2048]{0,1:T(8,128)(2,1)} %add_convert_fusion.8), channel_id=1, source_target_pairs={{0,2},{2,0},{1,3},{3,1},{4,6},{6,4},{5,7},{7,5},{8,10},{10,8},{9,1... | collective-permute-start | bytes 1572872 | tf_op jit(solution)/shard_map/ppermute | solution.py:42
  247.2 12.7 %collective-permute-start.23 = (bf16[1,512]{1,0:T(2,128)(2,1)S(1)}, bf16[1,512]{1,0:T(2,128)(2,1)S(1)}, u32[]{:S(2)}, u32[]{:S(2)}) collective-permute-start(bf16[1,512]{1,0:T(2,128)(2,1)S(1)} %get-tuple-element.78), channel_id=1, source_target_pairs={{0,2},{2,0},{1,3},{3,1},{4,6},{6,4},{5,7},{7,5},{8,10},{10,8},{9,1... | collective-permute-start | bytes 3080 | tf_op jit(solution)/shard_map/ppermute | solution.py:42
  247.7 13.6 %collective-permute-start.22 = (bf16[1,512]{1,0:T(2,128)(2,1)S(1)}, bf16[1,512]{1,0:T(2,128)(2,1)S(1)}, u32[]{:S(2)}, u32[]{:S(2)}) collective-permute-start(bf16[1,512]{1,0:T(2,128)(2,1)S(1)} %get-tuple-element.78), channel_id=1, source_target_pairs={{0,1},{1,0},{2,3},{3,2},{4,5},{5,4},{6,7},{7,6},{8,9},{9,8},{10,11... | collective-permute-start | bytes 3080 | tf_op jit(solution)/shard_map/ppermute | solution.py:38
  266.0 14.4 %collective-permute-start.26 = (bf16[128,2048]{0,1:T(8,128)(2,1)S(1)}, bf16[128,2048]{0,1:T(8,128)(2,1)S(1)}, u32[]{:S(2)}, u32[]{:S(2)}) collective-permute-start(bf16[128,2048]{0,1:T(8,128)(2,1)S(1)} %get-tuple-element.33), channel_id=1, source_target_pairs={{0,2},{2,0},{1,3},{3,1},{4,6},{6,4},{5,7},{7,5},{8,10},{10,8},{9,1... | collective-permute-start | bytes 1572872 | tf_op jit(solution)/shard_map/ppermute | solution.py:42
  267.7 12.8 %collective-permute-start.25 = (bf16[128,2048]{0,1:T(8,128)(2,1)S(1)}, bf16[128,2048]{0,1:T(8,128)(2,1)S(1)}, u32[]{:S(2)}, u32[]{:S(2)}) collective-permute-start(bf16[128,2048]{0,1:T(8,128)(2,1)S(1)} %get-tuple-element.33), channel_id=1, source_target_pairs={{0,1},{1,0},{2,3},{3,2},{4,5},{5,4},{6,7},{7,6},{8,9},{9,8},{10,11... | collective-permute-start | bytes 1572872 | tf_op jit(solution)/shard_map/ppermute | solution.py:38
  317.7 14.0 %collective-permute-start.30 = (bf16[512,512]{0,1:T(8,128)(2,1)S(1)}, bf16[512,512]{0,1:T(8,128)(2,1)S(1)}, u32[]{:S(2)}, u32[]{:S(2)}) collective-permute-start(bf16[512,512]{0,1:T(8,128)(2,1)S(1)} %add_convert_fusion.6), channel_id=1, source_target_pairs={{0,2},{2,0},{1,3},{3,1},{4,6},{6,4},{5,7},{7,5},{8,10},{10,8},{9,1... | collective-permute-start | bytes 1572872 | tf_op jit(solution)/shard_map/ppermute | solution.py:42
  344.4 14.0 %collective-permute-start.35 = (bf16[512,512]{1,0:T(8,128)(2,1)S(1)}, bf16[512,512]{1,0:T(8,128)(2,1)S(1)}, u32[]{:S(2)}, u32[]{:S(2)}) collective-permute-start(bf16[512,512]{1,0:T(8,128)(2,1)S(1)} %add_convert_fusion.5), channel_id=1, source_target_pairs={{0,2},{2,0},{1,3},{3,1},{4,6},{6,4},{5,7},{7,5},{8,10},{10,8},{9,1... | collective-permute-start | bytes 1572872 | tf_op jit(solution)/shard_map/ppermute | solution.py:42
  407.2 40.6 %all-to-all-start.3 = ((bf16[8,3,128,256]{2,3,1,0:T(8,128)(2,1)}), bf16[8,3,128,256]{2,3,1,0:T(8,128)(2,1)}, u32[]{:S(2)}, u32[]{:S(2)}) async-start(bf16[8,3,128,256]{2,3,1,0:T(8,128)(2,1)} %copy.187), calls=%async_computation.3 | async-start | bytes 3145728 | tf_op jit(solution)/shard_map/all_to_all | solution.py:184
  411.7 233.1 %all-reduce.3.cloned.1.call-start = ((), (), s32[]{:S(2)}) async-start(), calls=%async_computation.4 | async-start | bytes 6029312 | tf_op jit(solution)/shard_map/psum | solution.py:338
  419.1 7.9 %collective-permute-start.51 = (f32[512,16]{0,1:T(8,128)}, f32[512,16]{0,1:T(8,128)}, u32[]{:S(2)}, u32[]{:S(2)}) collective-permute-start(f32[512,16]{0,1:T(8,128)} %reduce_sum.168), channel_id=1, source_target_pairs={{0,1},{1,0},{2,3},{3,2},{4,5},{5,4},{6,7},{7,6},{8,9},{9,8},{10,11... | collective-permute-start | bytes 98312 | tf_op jit(solution)/shard_map/ppermute | solution.py:38
  419.1 10.3 %collective-permute-start.49 = (f32[512,16]{0,1:T(8,128)S(1)}, f32[512,16]{0,1:T(8,128)S(1)}, u32[]{:S(2)}, u32[]{:S(2)}) collective-permute-start(f32[512,16]{0,1:T(8,128)S(1)} %reduce_sum.167), channel_id=1, source_target_pairs={{0,1},{1,0},{2,3},{3,2},{4,5},{5,4},{6,7},{7,6},{8,9},{9,8},{10,11... | collective-permute-start | bytes 98312 | tf_op jit(solution)/shard_map/ppermute | solution.py:38
  427.9 6.1 collective-permute-start.52
  430.0 12.5 %collective-permute-start.48 = (f32[512,16]{0,1:T(8,128)S(1)}, f32[512,16]{0,1:T(8,128)S(1)}, u32[]{:S(2)}, u32[]{:S(2)}) collective-permute-start(f32[512,16]{0,1:T(8,128)S(1)} %add.424), channel_id=1, source_target_pairs={{0,2},{2,0},{1,3},{3,1},{4,6},{6,4},{5,7},{7,5},{8,10},{10,8},{9,1... | collective-permute-start | bytes 98312 | tf_op jit(solution)/shard_map/ppermute | solution.py:42
  477.6 22.5 %collective-permute-start.45 = (f32[512,16]{0,1:T(8,128)}, f32[512,16]{0,1:T(8,128)}, u32[]{:S(2)}, u32[]{:S(2)}) collective-permute-start(f32[512,16]{0,1:T(8,128)} %reduce_sum.165), channel_id=1, source_target_pairs={{0,1},{1,0},{2,3},{3,2},{4,5},{5,4},{6,7},{7,6},{8,9},{9,8},{10,11... | collective-permute-start | bytes 98312 | tf_op jit(solution)/shard_map/ppermute | solution.py:38
  494.2 8.2 %collective-permute-start.43 = (f32[512,16]{0,1:T(8,128)}, f32[512,16]{0,1:T(8,128)}, u32[]{:S(2)}, u32[]{:S(2)}) collective-permute-start(f32[512,16]{0,1:T(8,128)} %reduce_sum.164), channel_id=1, source_target_pairs={{0,1},{1,0},{2,3},{3,2},{4,5},{5,4},{6,7},{7,6},{8,9},{9,8},{10,11... | collective-permute-start | bytes 98312 | tf_op jit(solution)/shard_map/ppermute | solution.py:38
  495.7 7.9 %collective-permute-start.41 = (f32[512,16]{0,1:T(8,128)}, f32[512,16]{0,1:T(8,128)S(1)}, u32[]{:S(2)}, u32[]{:S(2)}) collective-permute-start(f32[512,16]{0,1:T(8,128)} %reduce_sum.163), channel_id=1, source_target_pairs={{0,1},{1,0},{2,3},{3,2},{4,5},{5,4},{6,7},{7,6},{8,9},{9,8},{10,11... | collective-permute-start | bytes 98312 | tf_op jit(solution)/shard_map/ppermute | solution.py:38
  500.8 8.2 %collective-permute-start.46 = (f32[512,16]{0,1:T(8,128)S(1)}, f32[512,16]{0,1:T(8,128)S(1)}, u32[]{:S(2)}, u32[]{:S(2)}) collective-permute-start(f32[512,16]{0,1:T(8,128)S(1)} %add.422), channel_id=1, source_target_pairs={{0,2},{2,0},{1,3},{3,1},{4,6},{6,4},{5,7},{7,5},{8,10},{10,8},{9,1... | collective-permute-start | bytes 98312 | tf_op jit(solution)/shard_map/ppermute | solution.py:42
  503.1 5.9 collective-permute-start.44
  534.3 14.1 %collective-permute-start.40 = (bf16[128,2048]{1,0:T(8,128)(2,1)S(1)}, bf16[128,2048]{1,0:T(8,128)(2,1)}, u32[]{:S(2)}, u32[]{:S(2)}) collective-permute-start(bf16[128,2048]{1,0:T(8,128)(2,1)S(1)} %add_convert_fusion.3), channel_id=1, source_target_pairs={{0,2},{2,0},{1,3},{3,1},{4,6},{6,4},{5,7},{7,5},{8,10},{10,8},{9,1... | collective-permute-start | bytes 1572872 | tf_op jit(solution)/shard_map/ppermute | solution.py:42
  (133 other events, 1117.5 us)
Sparse Core Ops, SparseCore 0:
  520.7 124.0 all-reduce.2

commit v2 on v1

v2 whole, which is shorter than its diff:
```python
import math

import jax
import jax.numpy as jnp
from jax import lax
from jax.experimental import pallas as pl
from jax.experimental.pallas import tpu as pltpu
from jax.sharding import PartitionSpec as P

HEADS = 16
HEAD_DIM = 128
RANK = 16
ADAPTERS = 4
LOW = RANK * ADAPTERS
NORM_EPS = 1e-06
SCALE = 4.0
ROPE_BASE = 500000.0
MASKED = -1e30
FAR_POSITION = 1e9
F32 = jnp.float32
BF16 = jnp.bfloat16
CORE_SWAP = ((0, 1), (1, 0), (2, 3), (3, 2))
CHIP_SWAP = ((0, 2), (2, 0), (1, 3), (3, 1))


def dot(left, right, lc, rc, precision=None):
    return lax.dot_general(
        left, right, (((lc,), (rc,)), ((), ())), precision=precision, preferred_element_type=F32
    )


def mm(left, right):
    return dot(left, right, 1, 0)


def mm_t(left, right):
    return dot(left, right, 1, 1)


def tmm(left, right):
    return dot(left, right, 0, 0)


def row_sums(values, row):
    picked = lax.broadcasted_iota(jnp.int32, (8, values.shape[1]), 0) == row
    return dot(picked.astype(F32), values, 1, 1, lax.Precision.HIGHEST)


def column(block, row):
    return jnp.transpose(block)[:, row : row + 1]


def window(index, extent):
    return pl.ds(pl.multiple_of(index * extent, extent), extent)


def narrow(wide):
    return sum(wide[a * RANK : (a + 1) * RANK] for a in range(ADAPTERS))


def widen(thin, mask):
    return (jnp.concatenate([thin] * ADAPTERS, axis=0) * mask).astype(BF16)


def swap_core(values):
    return lax.ppermute(values, "wsh", CORE_SWAP)


def swap_chip(values):
    return lax.ppermute(values, "wsh", CHIP_SWAP)


def sum_wsh(values):
    values = values + swap_core(values)
    return values + swap_chip(values)


def pieces_wsh(block):
    far = swap_chip(block)
    return block, swap_core(block), far, swap_core(far)


def gather_wsh(block, axis, me):
    extent = block.shape[axis]
    shape = list(block.shape)
    shape[axis] = 4 * extent
    whole = jnp.zeros(shape, block.dtype)
    for flip, piece in enumerate(pieces_wsh(block)):
        start = [0] * block.ndim
        start[axis] = (me ^ flip) * extent
        whole = lax.dynamic_update_slice(whole, piece, start)
    return whole


def scatter_wsh(own, near, far, far_near):
    far = (far.astype(F32) + swap_core(far_near).astype(F32)).astype(BF16)
    return own, swap_core(near), swap_chip(far)


def total(refs):
    return refs[0][...].astype(F32) + refs[1][...].astype(F32) + refs[2][...].astype(F32)


def whole(array):
    rank = len(array.shape)
    return pl.BlockSpec(array.shape, lambda *_: (0,) * rank)


def kernel_call(body, name, grid, ins, outs, scratch=(), me=None, flops=0):
    arrays = [i[0] if isinstance(i, tuple) else i for i in ins]
    in_specs = [i[1] if isinstance(i, tuple) else whole(i) for i in ins]
    shapes = [o[0] if isinstance(o, tuple) else o for o in outs]
    out_specs = [o[1] if isinstance(o, tuple) else whole(o) for o in outs]
    moved = sum(math.prod(s.block_shape) * a.dtype.itemsize for s, a in zip(in_specs, arrays))
    moved += sum(math.prod(s.shape) * s.dtype.itemsize for s in shapes)
    return pl.pallas_call(
        body,
        name=name,
        out_shape=shapes,
        grid_spec=pltpu.PrefetchScalarGridSpec(
            num_scalar_prefetch=1,
            grid=grid,
            in_specs=in_specs,
            out_specs=out_specs,
            scratch_shapes=list(scratch),
        ),
        compiler_params=pltpu.CompilerParams(dimension_semantics=("arbitrary",) * len(grid)),
        cost_estimate=pl.CostEstimate(
            flops=int(flops), bytes_accessed=int(moved), transcendentals=0
        ),
    )(me, *arrays)


def shape(dims, dtype):
    return jax.ShapeDtypeStruct(dims, dtype)


def qkv_body(me, p0, p1, p2, p3, w, a, b, mask, proj, low_ref, squares, own_ref, rows_scr, low_scr):
    step = pl.program_id(0)
    rows = p0.shape[0]

    @pl.when(step == 0)
    def _():
        for flip, piece in enumerate((p0, p1, p2, p3)):
            rows_scr[window(me[0] ^ flip, rows), :] = piece[...]
        own_ref[...] = rows_scr[:, window(me[0], own_ref.shape[1])]
        squares[...] = jnp.zeros_like(squares)
        stacked = a[...].reshape(-1, a.shape[2])
        low_scr[...] = mm_t(stacked, rows_scr[...])

    low = (low_scr[pl.ds(pl.multiple_of(step * LOW, LOW), LOW), :] * mask[...]).astype(BF16)
    low_ref[0] = low
    out = mm(rows_scr[...], w[0]) + SCALE * tmm(low, b[0])
    proj[0] = out
    squares[...] += row_sums(out * out, step)


def rope_body(model_dim, per_member, me, proj, squares, gain, cosine, sine, out):
    inverse = lax.rsqrt(squares[...] * (1.0 / model_dim) + NORM_EPS)
    for k in range(3):
        scale = column(inverse, k)
        for h in range(proj.shape[2] // HEAD_DIM):
            lanes = slice(h * HEAD_DIM, (h + 1) * HEAD_DIM)
            part = proj[k, :, lanes]
            if k < 2:
                part = part * scale * gain[k : k + 1, lanes]
                part = part * cosine[...] + pltpu.roll(part, HEAD_DIM // 2, 1) * sine[...]
            spot = (h % per_member) * HEAD_DIM
            out[h // per_member, k, :, spot : spot + HEAD_DIM] = part.astype(BF16)


def probabilities(q, k, q_pos, k_pos):
    queries = q[...].reshape(-1, HEAD_DIM)
    keys = k[...].reshape(-1, HEAD_DIM)
    scores = mm_t(queries, keys) * (HEAD_DIM**-0.5)
    scores = jnp.where(k_pos[0:1, :] <= column(q_pos[...], 0), scores, MASKED)
    weights = jnp.exp(scores - jnp.max(scores, axis=-1, keepdims=True))
    return queries, keys, weights * (1.0 / jnp.sum(weights, axis=-1, keepdims=True))


def attention_body(me, q, k, v, q_pos, k_pos, out):
    _, _, weights = probabilities(q, k, q_pos, k_pos)
    mixed = mm(weights.astype(BF16), v[...].reshape(-1, HEAD_DIM))
    out[...] = mixed.astype(BF16).reshape(out.shape)


def attention_back_body(joint, me, q, k, v, g, q_pos, k_pos, *outs):
    key_scr, value_scr = outs[-2:]
    step = pl.program_id(1)
    queries, keys, weights = probabilities(q, k, q_pos, k_pos)
    grads = g[...].reshape(-1, HEAD_DIM)
    grad_probs = mm_t(grads, v[...].reshape(-1, HEAD_DIM))
    delta = jnp.sum(weights * grad_probs, axis=-1, keepdims=True)
    grad_scores = (weights * (grad_probs - delta)).astype(BF16)
    grad_queries = mm(grad_scores, keys) * (HEAD_DIM**-0.5)
    grad_keys = tmm(grad_scores, queries)
    grad_values = tmm(weights.astype(BF16), grads)
    blocks, rows = q.shape[0], q.shape[2]
    grad_queries = grad_queries.astype(BF16).reshape(blocks, rows, HEAD_DIM)
    if joint:
        outs[0][pl.ds(step * blocks, blocks), 0] = grad_queries
    else:
        outs[0][...] = grad_queries

    @pl.when(step == 0)
    def _():
        key_scr[...] = grad_keys
        value_scr[...] = grad_values

    @pl.when(step > 0)
    def _():
        key_scr[...] += grad_keys
        value_scr[...] += grad_values

    @pl.when(step == pl.num_programs(1) - 1)
    def _():
        target = outs[0] if joint else outs[1]
        first = 1 if joint else 0
        extent = (target.shape[0],) + target.shape[2:]
        target[:, first] = (key_scr[...] * (HEAD_DIM**-0.5)).astype(target.dtype).reshape(extent)
        target[:, first + 1] = value_scr[...].astype(target.dtype).reshape(extent)


def branch_body(me, p0, p1, p2, p3, w, a, b, mask, branch, low_ref, squares):
    out = None
    low = None
    splits, rows, extent = p0.shape[1:]
    for flip, piece in enumerate((p0, p1, p2, p3)):
        for part in range(splits):
            at = window((me[0] ^ flip) * splits + part, extent)
            left = piece[:, part].reshape(-1, extent)
            term = mm(left, w[0, at, :])
            low_term = mm_t(a[0, :, at], left)
            out = term if out is None else out + term
            low = low_term if low is None else low + low_term
    low = (low * mask[...]).astype(BF16)
    low_ref[...] = low
    out = out + SCALE * tmm(low, b[0])
    branch[...] = out
    squares[...] = row_sums(out * out, 0)


def mid_body(model_dim, me, own, branch, squares, gain, out):
    scale = lax.rsqrt(column(squares[...], 0) * (1.0 / model_dim) + NORM_EPS)
    out[...] = (own[...].astype(F32) + branch[...] * scale * gain[2:3, :]).astype(BF16)


def mlp_body(
    me, p0, p1, p2, p3, wg, wu, wd, a, bg, bu, ad, b_down, mask,
    gate_ref, up_ref, product_ref, low_ref, low_down, mid_rows, o0, o1, o2, o3,
    rows_scr, low_scr, acc,
):
    step = pl.program_id(0)
    width = p0.shape[1]

    @pl.when(step == 0)
    def _():
        for flip, piece in enumerate((p0, p1, p2, p3)):
            rows_scr[:, window(me[0] ^ flip, width)] = piece[...]
        mid_rows[...] = rows_scr[window(me[0], mid_rows.shape[0]), :]
        stacked = mm_t(a[...].reshape(-1, a.shape[2]), rows_scr[...])
        for k in range(2):
            low_ref[k] = (stacked[k * LOW : (k + 1) * LOW] * mask[...]).astype(BF16)
        low_scr[...] = jnp.zeros_like(low_scr)

    gate = mm(rows_scr[...], wg[0]) + SCALE * tmm(low_ref[0], bg[0])
    up = mm(rows_scr[...], wu[0]) + SCALE * tmm(low_ref[1], bu[0])
    gate_ref[...] = gate
    up_ref[...] = up
    product = (gate * jax.nn.sigmoid(gate) * up).astype(BF16)
    product_ref[...] = product
    low_scr[...] += mm_t(ad[0], product)
    part = mm_t(product, wd[0])

    @pl.when(step == 0)
    def _():
        acc[...] = part

    @pl.when(step > 0)
    def _():
        acc[...] += part

    @pl.when(step == pl.num_programs(0) - 1)
    def _():
        low = low_scr[...] * mask[...]
        low_down[...] = narrow(low)
        acc[...] += SCALE * tmm(low.astype(BF16), b_down[0])
        for flip, out in enumerate((o0, o1, o2, o3)):
            out[...] = acc[window(me[0] ^ flip, out.shape[0]), :].astype(BF16)


def turn_body(me, y0, y1, y2, mid_rows, upstream_ref, valid, gain, result, grad, masked):
    down = total((y0, y1, y2))
    scale = lax.rsqrt(jnp.mean(down * down, axis=-1, keepdims=True) + NORM_EPS)
    result[...] = (mid_rows[...].astype(F32) + down * scale * gain[0:1, :]).astype(BF16)
    upstream = upstream_ref[0].astype(F32) * column(valid[...], 0)
    masked[...] = upstream.astype(BF16)
    scaled = upstream * gain[0:1, :]
    mean = jnp.mean(scaled * down, axis=-1, keepdims=True)
    grad[...] = (scale * scaled - down * (scale * scale * scale) * mean).astype(BF16)


def mlp_back_body(
    me, p0, p1, p2, p3, masked, wg, wu, wd, a, bg, bu, ad, b_down, mask,
    gate_ref, up_ref, product_ref, low_ref, low_down,
    grads, grad_b_down, low_parts, o0, o1, o2, o3,
    rows_scr, low_scr, part_scr, acc,
):
    step = pl.program_id(0)
    rows = p0.shape[0]
    width = o0.shape[1]

    @pl.when(step == 0)
    def _():
        for flip, piece in enumerate((p0, p1, p2, p3)):
            rows_scr[window(me[0] ^ flip, rows), :] = piece[...]
        low_scr[...] = (SCALE * mm_t(b_down[0], rows_scr[...]) * mask[...]).astype(BF16)
        wide = widen(low_down[...], mask[...])
        grad_b_down[...] = SCALE * mm(wide, rows_scr[:, window(me[0], width)])
        part_scr[...] = jnp.zeros_like(part_scr)
        acc[...] = jnp.zeros_like(acc)
        acc[window(me[0], rows), :] = masked[...].astype(F32)

    grad_product = mm(rows_scr[...], wd[0]) + tmm(low_scr[...], ad[0])
    gate = gate_ref[...]
    sigmoid = jax.nn.sigmoid(gate)
    silu = gate * sigmoid
    grad_up = (grad_product * silu).astype(BF16)
    grad_gate = (
        grad_product * up_ref[...] * sigmoid * (1.0 + gate * (1.0 - sigmoid))
    ).astype(BF16)
    grads[0] = SCALE * mm(low_ref[0], grad_gate)
    grads[1] = SCALE * mm(low_ref[1], grad_up)
    grads[2] = mm(low_scr[...], product_ref[...])
    part_scr[0] += SCALE * mm_t(bg[0], grad_gate)
    part_scr[1] += SCALE * mm_t(bu[0], grad_up)
    acc[...] += mm_t(grad_gate, wg[0]) + mm_t(grad_up, wu[0])

    @pl.when(step == pl.num_programs(0) - 1)
    def _():
        for k in range(2):
            low = part_scr[k] * mask[...]
            low_parts[k] = narrow(low)
            acc[...] += tmm(low.astype(BF16), a[k])
        for flip, out in enumerate((o0, o1, o2, o3)):
            out[...] = acc[:, window(me[0] ^ flip, width)].astype(BF16)


def mid_sum_body(me, y0, y1, y2, branch, gain, grad_mid, sums):
    grad = total((y0, y1, y2))
    grad_mid[...] = grad
    sums[...] = row_sums(grad * gain[2:3, :] * branch[...], 0)


def branch_back_body(
    model_dim, me, grad_mid, branch, squares, sums, gain, w, a, b, mask, low_out, low_sums, mid,
    grad_b, grad_a, low_parts, o0, o1, o2, o3,
):
    scale = lax.rsqrt(column(squares[...], 0) * (1.0 / model_dim) + NORM_EPS)
    mean = column(sums[...], 0) * (1.0 / model_dim)
    scaled = grad_mid[...] * gain[2:3, :]
    grad = (scale * scaled - branch[...] * (scale * scale * scale) * mean).astype(BF16)
    low = SCALE * mm_t(b[0], grad) * mask[...]
    low_parts[...] = narrow(low)
    low = low.astype(BF16)
    width = o0.shape[1]
    for flip, out in enumerate((o0, o1, o2, o3)):
        at = window(me[0] ^ flip, width)
        out[...] = (mm_t(grad, w[0, at, :]) + tmm(low, a[0, :, at])).astype(BF16)
    grad_b[...] = SCALE * mm(low_out[...], grad)
    for k in range(2):
        grad_a[k] = mm(widen(low_sums[k], mask[...]), mid[...])


def heads_body(y0, y1, y2):
    return total((y0, y1, y2))


def split_body(per_member, me, y0, y1, y2, out):
    grad = total((y0, y1, y2)).astype(BF16)
    extent = per_member * HEAD_DIM
    for part in range(out.shape[0]):
        out[part] = grad[:, part * extent : (part + 1) * extent]


def turn_back_body(per_member, me, grads, proj, gain, cosine, sine, turned, sums):
    result = None
    for k in range(3):
        dots = None
        for h in range(proj.shape[2] // HEAD_DIM):
            lanes = slice(h * HEAD_DIM, (h + 1) * HEAD_DIM)
            spot = (h % per_member) * HEAD_DIM
            part = grads[h // per_member, k, :, spot : spot + HEAD_DIM].astype(F32)
            if k < 2:
                part = part * cosine[...] - pltpu.roll(part, HEAD_DIM // 2, 1) * sine[...]
                part = part * gain[k : k + 1, lanes]
                term = row_sums(part * proj[k, :, lanes], k)
                result = term if result is None else result + term
            turned[k, :, lanes] = part
    sums[...] = result


def qkv_back_body(
    model_dim, me, turned, proj, squares, sums, grad_mid, w, a, b, mask, low_ref,
    grad_b, low_parts, o0, o1, o2, o3, acc,
):
    step = pl.program_id(0)

    @pl.when(step == 0)
    def _():
        acc[...] = jnp.zeros_like(acc)
        acc[:, window(me[0], grad_mid.shape[1])] = grad_mid[...]

    here = lax.broadcasted_iota(jnp.int32, squares.shape, 0) == step

    def chosen(values):
        row = jnp.sum(jnp.where(here, values, 0.0), axis=0, keepdims=True)
        return column(jnp.broadcast_to(row, values.shape), 0)

    scale = chosen(lax.rsqrt(squares[...] * (1.0 / model_dim) + NORM_EPS))
    mean = chosen(sums[...]) * (1.0 / model_dim)
    scale = jnp.where(step == 2, 1.0, scale)
    mean = jnp.where(step == 2, 0.0, mean)
    grad = (scale * turned[0] - proj[0] * (scale * scale * scale) * mean).astype(BF16)
    low = SCALE * mm_t(b[0], grad) * mask[...]
    low_parts[0] = narrow(low)
    grad_b[0] = SCALE * mm(low_ref[0], grad)
    acc[...] += mm_t(grad, w[0]) + tmm(low.astype(BF16), a[0])

    @pl.when(step == pl.num_programs(0) - 1)
    def _():
        for flip, out in enumerate((o0, o1, o2, o3)):
            out[...] = acc[window(me[0] ^ flip, out.shape[0]), :].astype(BF16)


def last_grads_body(me, low_in, low_out, own, attended, mask, grad_in, grad_out):
    for k in range(3):
        grad_in[k] = mm(widen(low_in[k], mask[...]), own[...])
    wide = widen(low_out[...], mask[...])
    splits, rows, extent = attended.shape[1:]
    for part in range(splits):
        grad_out[:, part * extent : (part + 1) * extent] = mm(
            wide, attended[:, part].reshape(-1, extent)
        )


def per_device(
    tokens,
    out_grad,
    attn_weight,
    mlp_weight,
    norm_gains,
    adapt_model,
    adapt_hidden,
    lengths,
    adapter_pick,
    block_order,
):
    own_rows = tokens[0]
    rows, model_dim = own_rows.shape
    block_rows = rows // 2
    ctx_size = lax.axis_size("ctx")
    seqs = lax.axis_size("wsh")
    width = model_dim // seqs
    hidden_width = mlp_weight.shape[2]
    local_heads = width // HEAD_DIM
    me = lax.axis_index("wsh")
    here = me.astype(jnp.int32).reshape(1)
    ctx_index = lax.axis_index("ctx")
    pairs = seqs * local_heads
    members = math.gcd(ctx_size, pairs)
    groups = ctx_size // members
    per_member = pairs // members
    splits = local_heads // per_member
    span = per_member * HEAD_DIM
    group_rows = members * rows
    member = ctx_index % members
    group = ctx_index // members
    ctx_groups = [[g * members + i for i in range(members)] for g in range(groups)]
    key_groups = [[g * members + i for g in range(groups)] for i in range(members)]
    all_rows = seqs * rows

    def call(body, name, grid, ins, outs, scratch=(), flops=0):
        return kernel_call(body, name, grid, ins, outs, scratch, here, flops)

    def bind(body, *fixed):
        def bound(*refs):
            return body(*fixed, *refs)

        return bound

    orders = gather_wsh(block_order, 0, me)
    positions = (orders[:, :, None] * block_rows + jnp.arange(block_rows)[None, None, :]).reshape(
        seqs, -1
    )
    row_positions = lax.dynamic_slice_in_dim(positions, ctx_index * rows, rows, 1)
    own_positions = lax.dynamic_index_in_dim(row_positions, me, keepdims=False)
    own_length = lax.dynamic_index_in_dim(lengths, me, keepdims=False)
    valid = jnp.broadcast_to((own_positions < own_length).astype(F32)[None], (8, rows))
    half = HEAD_DIM // 2
    frequency = ROPE_BASE ** (-(jnp.arange(half, dtype=F32) * 2.0) / HEAD_DIM)
    angles = row_positions.reshape(-1).astype(F32)[:, None] * frequency[None, :]
    cosine, sine = jnp.cos(angles), jnp.sin(angles)
    cosine = jnp.concatenate([cosine, cosine], 1)
    sine = jnp.concatenate([-sine, sine], 1)
    picked = jnp.arange(LOW)[:, None] // RANK == adapter_pick[None, :]
    mask = jnp.repeat(picked.astype(F32), rows, axis=1)
    seq_here = (member * per_member) // local_heads
    key_positions = lax.dynamic_index_in_dim(positions, seq_here, keepdims=False)
    query_positions = lax.dynamic_slice_in_dim(key_positions, group * group_rows, group_rows)
    length_here = lax.dynamic_index_in_dim(lengths, seq_here, keepdims=False)
    key_positions = jnp.where(
        key_positions < length_here, key_positions.astype(F32), FAR_POSITION
    )
    k_pos = jnp.broadcast_to(key_positions[None], (8, key_positions.shape[0]))
    q_pos = jnp.broadcast_to(query_positions.astype(F32)[None], (8, group_rows))
    gains = norm_gains.astype(F32)

    hidden = pieces_wsh(own_rows)
    rows_a = gather_wsh(jnp.concatenate([adapt_model[:6], adapt_model[10:11]], 0), 2, me)
    last_gain = jnp.broadcast_to(
        gather_wsh(norm_gains[3:4], 1, me).astype(F32), (8, model_dim)
    )

    def stack_block(index):
        return pl.BlockSpec((1, all_rows, width), lambda k, *_: (k, 0, 0))

    w_qkv = (attn_weight, pl.BlockSpec((1, model_dim, width), lambda k, *_: (k, 0, 0)))
    w_out = (attn_weight, pl.BlockSpec((1, model_dim, width), lambda *_: (3, 0, 0)))
    a_qkv = (rows_a, pl.BlockSpec((3, LOW, model_dim), lambda *_: (0, 0, 0)))
    a_step = (rows_a, pl.BlockSpec((1, LOW, model_dim), lambda k, *_: (k, 0, 0)))
    a_out = (rows_a, pl.BlockSpec((1, LOW, model_dim), lambda *_: (3, 0, 0)))
    a_mlp = (rows_a, pl.BlockSpec((2, LOW, model_dim), lambda *_: (2, 0, 0)))
    b_down = (rows_a, pl.BlockSpec((1, LOW, model_dim), lambda *_: (6, 0, 0)))
    b_step = (adapt_model, pl.BlockSpec((1, LOW, width), lambda k, *_: (6 + k, 0, 0)))
    b_out = (adapt_model, pl.BlockSpec((1, LOW, width), lambda *_: (9, 0, 0)))
    step_rows = pl.BlockSpec((1, all_rows, width), lambda k, *_: (k, 0, 0))
    step_low = pl.BlockSpec((1, LOW, all_rows), lambda k, *_: (k, 0, 0))

    matmul = 2.0 * all_rows * model_dim * width

    proj, low_in, squares, own_columns = call(
        qkv_body,
        "qkv",
        (3,),
        [*hidden, w_qkv, a_qkv, b_step, mask],
        [
            (shape((3, all_rows, width), F32), step_rows),
            (shape((3, LOW, all_rows), BF16), step_low),
            shape((8, all_rows), F32),
            shape((all_rows, width), BF16),
        ],
        [pltpu.VMEM((all_rows, model_dim), BF16), pltpu.VMEM((3 * LOW, all_rows), F32)],
        3 * matmul,
    )
    squares = sum_wsh(squares)
    proj_rows = (proj, pl.BlockSpec((3, rows, width), lambda s, *_: (0, s, 0)))
    tables = [(t, pl.BlockSpec((rows, HEAD_DIM), lambda s, *_: (s, 0))) for t in (cosine, sine)]
    lane_rows = pl.BlockSpec((8, rows), lambda s, *_: (0, s))
    member_rows = pl.BlockSpec((splits, 3, rows, span), lambda s, *_: (s, 0, 0, 0))
    (packed,) = call(
        bind(rope_body, model_dim, per_member),
        "rope",
        (seqs,),
        [proj_rows, (squares, lane_rows), gains, *tables],
        [(shape((members, 3, rows, span), BF16), member_rows)],
    )

    def exchange(values):
        return lax.all_to_all(values, "ctx", 0, 0, tiled=True, axis_index_groups=ctx_groups)

    heads = exchange(packed)
    if groups > 1:
        keyed = lax.all_gather(
            heads[:, 1:], "ctx", axis=0, tiled=True, axis_index_groups=key_groups
        )
        first = 0
    else:
        keyed, first = heads, 1
    key_blocks = keyed.shape[0]
    query_blocks = 2
    query_rows = query_blocks * rows
    attention_ins = [
        (heads, pl.BlockSpec((query_blocks, 1, rows, HEAD_DIM), lambda p, i, *_: (i, 0, 0, p))),
        (keyed, pl.BlockSpec((key_blocks, 1, rows, HEAD_DIM), lambda p, i, *_: (0, first, 0, p))),
        (
            keyed,
            pl.BlockSpec((key_blocks, 1, rows, HEAD_DIM), lambda p, i, *_: (0, first + 1, 0, p)),
        ),
    ]
    position_ins = [(q_pos, pl.BlockSpec((8, query_rows), lambda p, i, *_: (0, i))), k_pos]
    row_block = pl.BlockSpec((query_blocks, rows, HEAD_DIM), lambda p, i, *_: (i, 0, p))
    attention_grid = (per_member, members // query_blocks)
    score_flops = 2.0 * per_member * group_rows * key_blocks * rows * HEAD_DIM
    (attended,) = call(
        attention_body,
        "attention",
        attention_grid,
        attention_ins + position_ins,
        [(shape((members, rows, span), BF16), row_block)],
        flops=2 * score_flops,
    )
    attended = exchange(attended).reshape(seqs, splits, rows, span)

    attended_pieces = pieces_wsh(attended)
    branch, low_out, branch_squares = call(
        branch_body,
        "branch",
        (1,),
        [*attended_pieces, w_out, a_out, b_out, mask],
        [shape((all_rows, width), F32), shape((LOW, all_rows), BF16), shape((8, all_rows), F32)],
        flops=matmul,
    )
    branch_squares = sum_wsh(branch_squares)
    (mid,) = call(
        bind(mid_body, model_dim),
        "mid",
        (1,),
        [own_columns, branch, branch_squares, gains],
        [shape((all_rows, width), BF16)],
    )

    tile = 256
    steps = hidden_width // tile

    def w_mlp(index):
        return (mlp_weight, pl.BlockSpec((1, model_dim, tile), lambda j, *_: (index, 0, j)))

    def hidden_low(index):
        return (adapt_hidden, pl.BlockSpec((1, LOW, tile), lambda j, *_: (index, 0, j)))

    tile_rows = pl.BlockSpec((all_rows, tile), lambda j, *_: (0, j))
    mid_pieces = pieces_wsh(mid)
    weights = [w_mlp(0), w_mlp(1), w_mlp(2), a_mlp]
    weights += [hidden_low(0), hidden_low(1), hidden_low(2), b_down, mask]
    wide = shape((all_rows, hidden_width), F32)
    gate, up, product, low_mid, low_down, mid_rows, *parts = call(
        mlp_body,
        "mlp",
        (steps,),
        [*mid_pieces, *weights],
        [
            (wide, tile_rows),
            (wide, tile_rows),
            (shape((all_rows, hidden_width), BF16), tile_rows),
            shape((2, LOW, all_rows), BF16),
            shape((RANK, all_rows), F32),
            shape((rows, model_dim), BF16),
        ]
        + [shape((rows, model_dim), BF16)] * 4,
        [
            pltpu.VMEM((all_rows, model_dim), BF16),
            pltpu.VMEM((LOW, all_rows), F32),
            pltpu.VMEM((all_rows, model_dim), F32),
        ],
        12 * matmul,
    )
    down_parts = scatter_wsh(*parts)
    low_down = sum_wsh(low_down)
    result, grad_down, masked = call(
        turn_body,
        "turn",
        (1,),
        [*down_parts, mid_rows, out_grad, valid, last_gain],
        [shape((rows, model_dim), BF16)] * 3,
    )

    grad_pieces = pieces_wsh(grad_down)
    hidden_grads, grad_b_down, low_parts, *parts = call(
        mlp_back_body,
        "mlp_back",
        (steps,),
        [*grad_pieces, masked, *weights]
        + [(gate, tile_rows), (up, tile_rows), (product, tile_rows), low_mid, low_down],
        [
            (shape((3, LOW, hidden_width), F32), pl.BlockSpec((3, LOW, tile), lambda j, *_: (0, 0, j))),
            shape((LOW, width), F32),
            shape((2, RANK, all_rows), F32),
        ]
        + [shape((all_rows, width), BF16)] * 4,
        [
            pltpu.VMEM((all_rows, model_dim), BF16),
            pltpu.VMEM((LOW, all_rows), BF16),
            pltpu.VMEM((2, LOW, all_rows), F32),
            pltpu.VMEM((all_rows, model_dim), F32),
        ],
        12 * matmul,
    )
    mid_parts = scatter_wsh(*parts)
    low_parts = sum_wsh(low_parts)

    grad_mid, mid_sums = call(
        mid_sum_body,
        "mid_sum",
        (1,),
        [*mid_parts, branch, gains],
        [shape((all_rows, width), F32), shape((8, all_rows), F32)],
    )
    mid_sums = sum_wsh(mid_sums)
    grad_b_out, grad_a_mid, low_out_parts, *parts = call(
        bind(branch_back_body, model_dim),
        "branch_back",
        (1,),
        [grad_mid, branch, branch_squares, mid_sums, gains, w_out, a_out, b_out, mask]
        + [low_out, low_parts, mid],
        [
            shape((LOW, width), F32),
            shape((2, LOW, width), F32),
            shape((RANK, all_rows), F32),
        ]
        + [shape((all_rows, width), BF16)] * 4,
        flops=matmul,
    )
    early_grads = jnp.stack([grad_a_mid[0], grad_a_mid[1], grad_b_out, grad_b_down])
    early_grads, hidden_grads = lax.psum((early_grads, hidden_grads), "ctx")
    low_out_parts = sum_wsh(low_out_parts)
    attended_parts = scatter_wsh(*parts)
    seq_rows = pl.BlockSpec((rows, width), lambda s, *_: (s, 0))
    (grad_attended,) = call(
        bind(split_body, per_member),
        "split",
        (seqs,),
        [(part, seq_rows) for part in attended_parts],
        [(shape((members, rows, span), BF16), pl.BlockSpec((splits, rows, span), lambda s, *_: (s, 0, 0)))],
    )

    grad_heads = exchange(grad_attended)
    back_ins = attention_ins + [(grad_heads, row_block)] + position_ins
    key_scratch = [pltpu.VMEM((key_blocks * rows, HEAD_DIM), F32)] * 2
    if groups == 1:
        (grads,) = call(
            bind(attention_back_body, True),
            "attention_back",
            attention_grid,
            back_ins,
            [
                (
                    shape((members, 3, rows, span), BF16),
                    pl.BlockSpec((members, 3, rows, HEAD_DIM), lambda p, i, *_: (0, 0, 0, p)),
                )
            ],
            key_scratch,
            5 * score_flops,
        )
    else:
        grad_queries, grad_keyed = call(
            bind(attention_back_body, False),
            "attention_back",
            attention_grid,
            back_ins,
            [
                (shape((members, rows, span), BF16), row_block),
                (
                    shape((key_blocks, 2, rows, span), F32),
                    pl.BlockSpec((key_blocks, 2, rows, HEAD_DIM), lambda p, i, *_: (0, 0, 0, p)),
                ),
            ],
            key_scratch,
            5 * score_flops,
        )
        grad_keyed = lax.psum_scatter(
            grad_keyed, "ctx", scatter_dimension=0, tiled=True, axis_index_groups=key_groups
        )
        grads = jnp.concatenate([grad_queries[:, None], grad_keyed.astype(BF16)], 1)
    grads = exchange(grads)
    turned, sums = call(
        bind(turn_back_body, per_member),
        "turn_back",
        (seqs,),
        [(grads, member_rows), proj_rows, gains, *tables],
        [
            (shape((3, all_rows, width), F32), pl.BlockSpec((3, rows, width), lambda s, *_: (0, s, 0))),
            (shape((8, all_rows), F32), lane_rows),
        ],
    )
    sums = sum_wsh(sums)
    grad_b_in, low_in_parts, *parts = call(
        bind(qkv_back_body, model_dim),
        "qkv_back",
        (3,),
        [(turned, step_rows), (proj, step_rows), squares, sums, grad_mid]
        + [w_qkv, a_step, b_step, mask, (low_in, step_low)],
        [
            (shape((3, LOW, width), F32), pl.BlockSpec((1, LOW, width), lambda k, *_: (k, 0, 0))),
            (shape((3, RANK, all_rows), F32), pl.BlockSpec((1, RANK, all_rows), lambda k, *_: (k, 0, 0))),
        ]
        + [shape((rows, model_dim), BF16)] * 4,
        [pltpu.VMEM((all_rows, model_dim), F32)],
        3 * matmul,
    )
    low_in_parts = sum_wsh(low_in_parts)
    input_parts = scatter_wsh(*parts)
    grad_inputs = sum(part.astype(F32) for part in input_parts)
    grad_a_in, grad_a_out = call(
        last_grads_body,
        "last_grads",
        (1,),
        [low_in_parts, low_out_parts, own_columns, attended, mask],
        [shape((3, LOW, width), F32), shape((LOW, width), F32)],
    )
    late = jnp.concatenate([grad_a_in, grad_a_out[None], grad_b_in], 0).astype(BF16)
    count = late.shape[0]
    late = late.reshape(ctx_size, -1, width)
    late = lax.all_to_all(late, "ctx", 0, 0, tiled=True).astype(F32).sum(0).astype(BF16)
    late = jnp.broadcast_to(late[None], (ctx_size,) + late.shape)
    late = lax.all_to_all(late, "ctx", 0, 0, tiled=True).astype(F32).reshape(count, LOW, width)
    model_grads = jnp.concatenate(
        [late[:4], early_grads[:2], late[4:7], early_grads[2:]], 0
    )
    return (result[None], grad_inputs[None], model_grads, hidden_grads)


def solution(mesh):
    in_specs = (
        P("wsh", "ctx", None),
        P("wsh", "ctx", None),
        P(None, None, "wsh"),
        P(None, None, "wsh"),
        P(None, "wsh"),
        P(None, None, "wsh"),
        P(None, None, "wsh"),
        P(),
        P(),
        P("wsh", None),
    )
    out_specs = (
        P("wsh", "ctx", None),
        P("wsh", "ctx", None),
        P(None, None, "wsh"),
        P(None, None, "wsh"),
    )
    return jax.shard_map(
        per_device, mesh=mesh, in_specs=in_specs, out_specs=out_specs, check_vma=False
    )
```

time: 666 us -> 542 us (0.81); the launches traced: 656 us -> 540 us
  matrix products: 167 us -> 0 us
  Pallas kernels: 0 us -> 151 us
  local copies, waits for them, and re-layouts: 87.8 us -> 16.8 us
  other arithmetic: 51.1 us -> 25.3 us
  starting transfers between devices: 46.8 us -> 39.2 us
  waiting for transfers between devices: 250 us -> 257 us
    dot_general x62 -> x0, matrix products: 167 us -> none  [the longest x56 145 us: dot(): lax.dot_general(left, right, (dims, ((), ())), preferred_element_type=F32)]
    pallas_call x0 -> x15, Pallas kernels: none -> 151 us  [kernel_call(): pl.pallas_call(body, name=name, out_shape=shapes, grid_spec=pltpu.Prefetc...]
    psum x1, waiting for transfers between devices: 93.8 us -> 0.52 us  [per_device(): early_grads, hidden_grads = lax.psum((early_grads, hidden_grads), 'ctx')]
    all_to_all x2 -> x4, waiting for transfers between devices: 38.7 us -> 127 us  [the longest x2 93.2 us: exchange(): lax.all_to_all(values, 'ctx', 0, 0, tiled=True, axis_index_groups=ctx_gro...]
    transpose x6 -> x0, local copies, waits for them, and re-layouts: 14.7 us -> none  [the longest x2 4.66 us: to_rows(): values.transpose(0, 2, 1, 3)]
    convert_element_type x7 -> x1, local copies, waits for them, and re-layouts: 14 us -> 0.1 us  [per_device(): mask = jnp.repeat(picked.astype(F32), rows, axis=1)]
    unnamed x222 -> x70, local copies, waits for them, and re-layouts: 22.5 us -> 8.73 us
    ppermute x22 -> x19, starting transfers between devices: 30 us -> 17.5 us  [swap_chip(): return lax.ppermute(values, 'wsh', CHIP_SWAP)]
  transfers between devices with their start and end apart: 58 -> 54, of which waited for: 27 -> 34; matrix products, arithmetic and copies ran while one was open for 15% -> 5% of each run, Pallas kernels for 0% -> 5%
where the time goes in v2:
time: 542 us; the launch traced here: 540 us
  waiting for transfers between devices  257 us (47%)
  Pallas kernels  151 us (28%)
  starting transfers between devices  39.2 us (7%)
  blocking collectives  36.6 us (7%)
  other arithmetic  25.3 us (5%)
  local copies, waits for them, and re-layouts  16.8 us (3%)
  between operations  14.6 us (3%)
    pallas_call x15, Pallas kernels, kernel_call(): pl.pallas_call(body, name=name, out_shape=shapes, grid_spec=pltpu.Prefetc...  151 us
    ppermute x19, waiting for transfers between devices, swap_chip(): return lax.ppermute(values, 'wsh', CHIP_SWAP)  108 us
    all_to_all x2, waiting for transfers between devices, exchange(): lax.all_to_all(values, 'ctx', 0, 0, tiled=True, axis_index_groups=ctx_gro...  93.2 us
    all_to_all x2, blocking collectives, exchange(): lax.all_to_all(values, 'ctx', 0, 0, tiled=True, axis_index_groups=ctx_gro...  36.6 us
    all_to_all x1, waiting for transfers between devices, per_device(): lax.all_to_all(late, 'ctx', 0, 0, tiled=True).astype(F32).sum(0)  24.8 us
    ppermute x30, waiting for transfers between devices, swap_core(): return lax.ppermute(values, 'wsh', CORE_SWAP)  21.4 us
    ppermute x19, starting transfers between devices, swap_chip(): return lax.ppermute(values, 'wsh', CHIP_SWAP)  17.5 us
  transfers between devices with their start and end apart: 54, of which 34 were waited for; matrix products, arithmetic and copies ran while one was open for 5% of the time, Pallas kernels for 5%

profile of v2, /device:TPU:0, one launch (start us, length us, event | category | flops | bytes accessed | tf_op | source)
XLA Modules:
  0.0 540.4 jit_solution(13458945583511066972)
XLA Ops:
  17.6 17.1 %collective-permute-done.4 = bf16[7,64,512]{2,1,0:T(8,128)(2,1)} collective-permute-done((bf16[7,64,512]{2,1,0:T(8,128)(2,1)}, bf16[7,64,512]{2,1,0:T(8,128)(2,1)}, u32[]{:S(2)}, u32[]{:S(2)}) %collective-permute-start.4) | collective-permute-done | bytes 458784 | tf_op jit(solution)/shard_map/ppermute | solution.py:70
  38.4 11.2 %qkv.1 = (f32[3,512,512]{2,1,0:T(8,128)}, bf16[3,64,512]{2,1,0:T(8,128)(2,1)}, f32[8,512]{1,0:T(8,128)}, bf16[512,512]{1,0:T(8,128)(2,1)}) custom-call(s32[1]{0:T(128)} %bitcast.me.refs_0_, bf16[128,2048]{1,0:T(8,128)(2,1)} %bitcast.54, bf16[128,2048]{1,0:T(8,128)(2,1)} %copy-done.12, bf16[128,2048]{1,0:T(8,128)(2,1)} %copy-done.11, ...), custom_call_target="tpu_custom_call" | custom-call | flops 3221225472 | bytes 9060352 | tf_op jit(solution)/shard_map/qkv/pallas_call | solution.py:116
  56.1 4.6 rope.1
  60.6 6.0 %all-to-all-start = ((bf16[8,3,128,256]{3,2,1,0:T(8,128)(2,1)}), bf16[8,3,128,256]{3,2,1,0:T(8,128)(2,1)S(1)}, u32[]{:S(2)}, u32[]{:S(2)}) async-start(bf16[8,3,128,256]{3,2,1,0:T(8,128)(2,1)} %rope.1), calls=%async_computation | async-start | bytes 3145728 | tf_op jit(solution)/shard_map/all_to_all | solution.py:570
  67.9 34.9 %all-to-all-done.q.k.v.refs_1_.refs_2_.refs_3_ = bf16[8,3,128,256]{3,2,1,0:T(8,128)(2,1)S(1)} async-done(((bf16[8,3,128,256]{3,2,1,0:T(8,128)(2,1)}), bf16[8,3,128,256]{3,2,1,0:T(8,128)(2,1)S(1)}, u32[]{:S(2)}, u32[]{:S(2)}) %all-to-all-start) | async-done | bytes 1572896 | tf_op jit(solution)/shard_map/all_to_all | solution.py:570
  104.1 9.0 %attention.1 = bf16[8,128,256]{2,1,0:T(8,128)(2,1)} custom-call(s32[1]{0:T(128)} %bitcast.me.refs_0_, bf16[8,3,128,256]{3,2,1,0:T(8,128)(2,1)} %copy-done.1, bf16[8,3,128,256]{3,2,1,0:T(8,128)(2,1)} %copy-done.1, bf16[8,3,128,256]{3,2,1,0:T(8,128)(2,1)} %copy-done.1, f32[8,1024]{1,0:T(8,128)} %broadcast_in_dim.97.q_pos.refs_5_, ...), custom_call_target="tpu_custom_call" | custom-call | flops 1073741824 | bytes 1155072 | tf_op jit(solution)/shard_map/attention/pallas_call | solution.py:116
  113.1 18.2 %all_to_all.30 = bf16[8,128,256]{2,1,0:T(8,128)(2,1)S(1)} all-to-all(bf16[8,128,256]{2,1,0:T(8,128)(2,1)} %attention.1), channel_id=1, replica_groups={{0,4,8,12,16,20,24,28},{1,5,9,13,17,21,25,29},{2,6,10,14,18,22,26,30},{..., dimensions={0} | all-to-all | bytes 1048576 | tf_op jit(solution)/shard_map/all_to_all | solution.py:570
  131.8 12.1 %collective-permute-done.12.p2 = bf16[4,2,128,256]{3,2,1,0:T(8,128)(2,1)S(1)} collective-permute-done((bf16[4,2,128,256]{3,2,1,0:T(8,128)(2,1)S(1)}, bf16[4,2,128,256]{3,2,1,0:T(8,128)(2,1)S(1)}, u32[]{:S(2)}, u32[]{:S(2)}) %collective-permute-start.12) | collective-permute-done | bytes 524320 | tf_op jit(solution)/shard_map/ppermute | solution.py:70
  146.6 5.8 %branch.1 = (f32[512,512]{1,0:T(8,128)}, bf16[64,512]{1,0:T(8,128)(2,1)}, f32[8,512]{1,0:T(8,128)}) custom-call(s32[1]{0:T(128)} %bitcast.me.refs_0_, bf16[4,2,128,256]{3,2,1,0:T(8,128)(2,1)} %bitcast.48, bf16[4,2,128,256]{3,2,1,0:T(8,128)(2,1)} %copy-done.18, bf16[4,2,128,256]{3,2,1,0:T(8,128)(2,1)} %copy-done.16, bf16[4,2,128,256]{3,2,1,0:T(8,128)(2,1)} %copy-done.19, ...), custom_call_target="tpu_custom_call" | custom-call | flops 1073741824 | bytes 5783552 | tf_op jit(solution)/shard_map/branch/pallas_call | solution.py:116
  155.0 3.2 collective-permute-done.15
  161.9 12.5 %collective-permute-done.17.p2 = bf16[512,512]{1,0:T(8,128)(2,1)S(1)} collective-permute-done((bf16[512,512]{1,0:T(8,128)(2,1)}, bf16[512,512]{1,0:T(8,128)(2,1)S(1)}, u32[]{:S(2)}, u32[]{:S(2)}) %collective-permute-start.17) | collective-permute-done | bytes 524320 | tf_op jit(solution)/shard_map/ppermute | solution.py:70
  177.1 28.6 %mlp.1 = (f32[512,2048]{1,0:T(8,128)}, f32[512,2048]{1,0:T(8,128)}, bf16[512,2048]{1,0:T(8,128)(2,1)}, bf16[2,64,512]{2,1,0:T(8,128)(2,1)}, f32[16,512]{1,0:T(8,...) custom-call(s32[1]{0:T(128)} %bitcast.me.refs_0_, ...), custom_call_target="tpu_custom_call" | custom-call | flops 12884901888 | bytes 19529728 | tf_op jit(solution)/shard_map/mlp/pallas_call | solution.py:116
  211.5 11.7 %collective-permute-done.23 = bf16[1,512]{1,0:T(2,128)(2,1)S(1)} collective-permute-done((bf16[1,512]{1,0:T(2,128)(2,1)S(1)}, bf16[1,512]{1,0:T(2,128)(2,1)S(1)}, u32[]{:S(2)}, u32[]{:S(2)}) %collective-permute-start.23) | collective-permute-done | bytes 1056 | tf_op jit(solution)/shard_map/ppermute | solution.py:70
  225.9 3.6 turn.1
  230.3 13.8 %collective-permute-done.26.p2 = bf16[128,2048]{1,0:T(8,128)(2,1)S(1)} collective-permute-done((bf16[128,2048]{1,0:T(8,128)(2,1)}, bf16[128,2048]{1,0:T(8,128)(2,1)S(1)}, u32[]{:S(2)}, u32[]{:S(2)}) %collective-permute-start.26) | collective-permute-done | bytes 524320 | tf_op jit(solution)/shard_map/ppermute | solution.py:70
  246.6 3.4 collective-permute-done.29
  251.6 37.1 %mlp_back.1 = (f32[3,64,2048]{2,1,0:T(8,128)}, f32[64,512]{1,0:T(8,128)}, f32[2,16,512]{2,1,0:T(8,128)}, bf16[512,512]{1,0:T(8,128)(2,1)}, bf16[512,512]{1,0:T(8...) custom-call(s32[1]{0:T(128)} %bitcast.me.refs_0_, bf16[128,2048]{1,0:T(8,128)(2,1)} %get-tuple-element.61.p0, ...), custom_call_target="tpu_custom_call" | custom-call | flops 12884901888 | bytes 12124160 | tf_op jit(solution)/shard_map/mlp_back/pallas_call | solution.py:116
  296.5 10.3 %collective-permute-done.32.y2 = bf16[512,512]{1,0:T(8,128)(2,1)S(1)} collective-permute-done((bf16[512,512]{1,0:T(8,128)(2,1)S(1)}, bf16[512,512]{1,0:T(8,128)(2,1)S(1)}, u32[]{:S(2)}, u32[]{:S(2)}) %collective-permute-start.32) | collective-permute-done | bytes 524320 | tf_op jit(solution)/shard_map/ppermute | solution.py:70
  307.6 3.3 mid_sum.1
  317.3 6.0 %branch_back.1 = (f32[64,512]{1,0:T(8,128)}, f32[2,64,512]{2,1,0:T(8,128)}, f32[16,512]{1,0:T(8,128)}, bf16[512,512]{1,0:T(8,128)(2,1)}, bf16[512,512]{1,0:T(8,1...) custom-call(s32[1]{0:T(128)} %bitcast.me.refs_0_, f32[512,512]{1,0:T(8,128)} %get-tuple-element.72.refs_1_.refs_5_, ...), custom_call_target="tpu_custom_call" | custom-call | flops 1073741824 | bytes 7872512 | tf_op jit(solution)/shard_map/branch_back/pallas_call | solution.py:116
  327.3 13.4 %collective-permute-done.39.refs_3_ = bf16[512,512]{1,0:T(8,128)(2,1)S(1)} collective-permute-done((bf16[512,512]{1,0:T(8,128)(2,1)S(1)}, bf16[512,512]{1,0:T(8,128)(2,1)S(1)}, u32[]{:S(2)}, u32[]{:S(2)}) %collective-permute-start.39) | collective-permute-done | bytes 524320 | tf_op jit(solution)/shard_map/ppermute | solution.py:70
  341.5 3.5 split.1
  345.0 18.4 %all_to_all.31.refs_4_ = bf16[8,128,256]{2,1,0:T(8,128)(2,1)} all-to-all(bf16[8,128,256]{2,1,0:T(8,128)(2,1)} %split.1), channel_id=1, replica_groups={{0,4,8,12,16,20,24,28},{1,5,9,13,17,21,25,29},{2,6,10,14,18,22,26,30},{..., dimensions={0} | all-to-all | bytes 1048576 | tf_op jit(solution)/shard_map/all_to_all | solution.py:570
  363.4 13.5 %attention_back.1 = bf16[8,3,128,256]{3,2,1,0:T(8,128)(2,1)} custom-call(s32[1]{0:T(128)} %bitcast.me.refs_0_, bf16[8,3,128,256]{3,2,1,0:T(8,128)(2,1)} %copy-done.1, bf16[8,3,128,256]{3,2,1,0:T(8,128)(2,1)} %copy-done.1, bf16[8,3,128,256]{3,2,1,0:T(8,128)(2,1)} %copy-done.1, bf16[8,128,256]{2,1,0:T(8,128)(2,1)} %all_to_all.31.refs_4_, ...), custom_call_target="tpu_custom_call" | custom-call | flops 2684354560 | bytes 2269184 | tf_op jit(solution)/shard_map/attention_back/pallas_call | solution.py:116
  376.9 3.8 all-to-all-start.3
  381.6 58.3 %all-to-all-done.3.refs_1_ = bf16[8,3,128,256]{3,2,1,0:T(8,128)(2,1)S(1)} async-done(((bf16[8,3,128,256]{3,2,1,0:T(8,128)(2,1)}), bf16[8,3,128,256]{3,2,1,0:T(8,128)(2,1)S(1)}, u32[]{:S(2)}, u32[]{:S(2)}) %all-to-all-start.3) | async-done | bytes 1572896 | tf_op jit(solution)/shard_map/all_to_all | solution.py:570
  441.0 6.9 %turn_back.1 = (f32[3,512,512]{2,1,0:T(8,128)}, f32[8,512]{1,0:T(8,128)}) custom-call(s32[1]{0:T(128)} %bitcast.me.refs_0_, bf16[8,3,128,256]{3,2,1,0:T(8,128)(2,1)} %copy-done.2, f32[3,512,512]{2,1,0:T(8,128)} %get-tuple-element.51.refs_1_.refs_2_, f32[4,512]{1,0:T(4,128)} %convert_element_type.79.refs_3_.refs_4_.gain.refs_5_, ...), custom_call_target="tpu_custom_call" | custom-call | bytes 4481024 | tf_op jit(solution)/shard_map/turn_back/pallas_call | solution.py:116
  454.3 12.6 %qkv_back.1 = (f32[3,64,512]{2,1,0:T(8,128)}, f32[3,16,512]{2,1,0:T(8,128)}, bf16[128,2048]{1,0:T(8,128)(2,1)}, bf16[128,2048]{1,0:T(8,128)(2,1)}, bf16[128,2048]{1,0:T(8,128)(2,1)}, /*index=5*/bf16[128,2048]{1,0:T(8,128)(2,1)}) custom-call(s32[1]{0:T(128)} %bitcast.me.refs_0_, f32[3,512,512]{2,1,0:T(8,128)} %get-tuple-element.80.refs_1_, ...), custom_call_target="tpu_custom_call" | custom-call | flops 3221225472 | bytes 8388608 | tf_op jit(solution)/shard_map/qkv_back/pallas_call | solution.py:116
  483.8 3.5 all-to-all-start.4
  489.0 24.8 %all-to-all-done.4 = bf16[8,56,512]{2,1,0:T(8,128)(2,1)S(1)} async-done(((bf16[8,56,512]{2,1,0:T(8,128)(2,1)}), bf16[8,56,512]{2,1,0:T(8,128)(2,1)S(1)}, u32[]{:S(2)}, u32[]{:S(2)}) %all-to-all-start.4) | async-done | bytes 458784 | tf_op jit(solution)/shard_map/all_to_all | solution.py:804
  514.8 3.5 all-to-all-start.5
  521.0 9.4 %all-to-all-done.5 = bf16[8,56,512]{2,1,0:T(8,128)(2,1)S(1)} async-done(((bf16[8,56,512]{2,1,0:T(8,128)(2,1)}), bf16[8,56,512]{2,1,0:T(8,128)(2,1)S(1)}, u32[]{:S(2)}, u32[]{:S(2)}) %all-to-all-start.5) | async-done | bytes 458784 | tf_op jit(solution)/shard_map/all_to_all | solution.py:806
  (242 shorter events, 102.1 us)
Async XLA Ops:
  7.2 8.3 %collective-permute-start.9 = (s32[1,16]{1,0:T(1,128)}, s32[1,16]{1,0:T(1,128)S(1)}, u32[]{:S(2)}, u32[]{:S(2)}) collective-permute-start(s32[1,16]{1,0:T(1,128)} %param.19), channel_id=1, source_target_pairs={{0,2},{2,0},{1,3},{3,1},{4,6},{6,4},{5,7},{7,5},{8,10},{10,8},{9,1... | collective-permute-start | bytes 200 | tf_op jit(solution)/shard_map/ppermute | solution.py:70
  10.2 5.1 collective-permute-start.8
  10.2 24.5 %collective-permute-start.1 = (bf16[128,2048]{1,0:T(8,128)(2,1)}, bf16[128,2048]{1,0:T(8,128)(2,1)S(1)}, u32[]{:S(2)}, u32[]{:S(2)}) collective-permute-start(bf16[128,2048]{1,0:T(8,128)(2,1)} %bitcast.52), channel_id=1, source_target_pairs={{0,2},{2,0},{1,3},{3,1},{4,6},{6,4},{5,7},{7,5},{8,10},{10,8},{9,1... | collective-permute-start | bytes 1572872 | tf_op jit(solution)/shard_map/ppermute | solution.py:70
  10.4 26.4 %collective-permute-start = (bf16[128,2048]{1,0:T(8,128)(2,1)}, bf16[128,2048]{1,0:T(8,128)(2,1)S(1)}, u32[]{:S(2)}, u32[]{:S(2)}) collective-permute-start(bf16[128,2048]{1,0:T(8,128)(2,1)} %bitcast.53), channel_id=1, source_target_pairs={{0,1},{1,0},{2,3},{3,2},{4,5},{5,4},{6,7},{7,6},{8,9},{9,8},{10,11... | collective-permute-start | bytes 1572872 | tf_op jit(solution)/shard_map/ppermute | solution.py:66
  11.8 22.9 %collective-permute-start.4 = (bf16[7,64,512]{2,1,0:T(8,128)(2,1)}, bf16[7,64,512]{2,1,0:T(8,128)(2,1)}, u32[]{:S(2)}, u32[]{:S(2)}) collective-permute-start(bf16[7,64,512]{2,1,0:T(8,128)(2,1)} %get-tuple-element.100), channel_id=1, source_target_pairs={{0,2},{2,0},{1,3},{3,1},{4,6},{6,4},{5,7},{7,5},{8,10},{10,8},{9,1... | collective-permute-start | bytes 1376264 | tf_op jit(solution)/shard_map/ppermute | solution.py:70
  15.3 19.9 %collective-permute-start.3 = (bf16[7,64,512]{2,1,0:T(8,128)(2,1)}, bf16[7,64,512]{2,1,0:T(8,128)(2,1)S(1)}, u32[]{:S(2)}, u32[]{:S(2)}) collective-permute-start(bf16[7,64,512]{2,1,0:T(8,128)(2,1)} %get-tuple-element.100), channel_id=1, source_target_pairs={{0,1},{1,0},{2,3},{3,2},{4,5},{5,4},{6,7},{7,6},{8,9},{9,8},{10,11... | collective-permute-start | bytes 1376264 | tf_op jit(solution)/shard_map/ppermute | solution.py:66
  60.6 42.2 %all-to-all-start = ((bf16[8,3,128,256]{3,2,1,0:T(8,128)(2,1)}), bf16[8,3,128,256]{3,2,1,0:T(8,128)(2,1)S(1)}, u32[]{:S(2)}, u32[]{:S(2)}) async-start(bf16[8,3,128,256]{3,2,1,0:T(8,128)(2,1)} %rope.1), calls=%async_computation | async-start | bytes 3145728 | tf_op jit(solution)/shard_map/all_to_all | solution.py:570
  131.3 12.6 %collective-permute-start.12 = (bf16[4,2,128,256]{3,2,1,0:T(8,128)(2,1)S(1)}, bf16[4,2,128,256]{3,2,1,0:T(8,128)(2,1)S(1)}, u32[]{:S(2)}, u32[]{:S(2)}) collective-permute-start(bf16[4,2,128,256]{3,2,1,0:T(8,128)(2,1)S(1)} %bitcast.46), channel_id=1, source_target_pairs={{0,2},{2,0},{1,3},{3,1},{4,6},{6,4},{5,7},{7,5},{8,10},{10,8},{9,1... | collective-permute-start | bytes 1572872 | tf_op jit(solution)/shard_map/ppermute | solution.py:70
  131.8 12.1 %collective-permute-start.11 = (bf16[4,2,128,256]{3,2,1,0:T(8,128)(2,1)S(1)}, bf16[4,2,128,256]{3,2,1,0:T(8,128)(2,1)S(1)}, u32[]{:S(2)}, u32[]{:S(2)}) collective-permute-start(bf16[4,2,128,256]{3,2,1,0:T(8,128)(2,1)S(1)} %bitcast.47), channel_id=1, source_target_pairs={{0,1},{1,0},{2,3},{3,2},{4,5},{5,4},{6,7},{7,6},{8,9},{9,8},{10,11... | collective-permute-start | bytes 1572872 | tf_op jit(solution)/shard_map/ppermute | solution.py:66
  161.3 13.1 %collective-permute-start.17 = (bf16[512,512]{1,0:T(8,128)(2,1)}, bf16[512,512]{1,0:T(8,128)(2,1)S(1)}, u32[]{:S(2)}, u32[]{:S(2)}) collective-permute-start(bf16[512,512]{1,0:T(8,128)(2,1)} %mid.1.p0.refs_12_), channel_id=1, source_target_pairs={{0,2},{2,0},{1,3},{3,1},{4,6},{6,4},{5,7},{7,5},{8,10},{10,8},{9,1... | collective-permute-start | bytes 1572872 | tf_op jit(solution)/shard_map/ppermute | solution.py:70
  161.9 12.5 %collective-permute-start.16 = (bf16[512,512]{1,0:T(8,128)(2,1)}, bf16[512,512]{1,0:T(8,128)(2,1)S(1)}, u32[]{:S(2)}, u32[]{:S(2)}) collective-permute-start(bf16[512,512]{1,0:T(8,128)(2,1)} %mid.1.p0.refs_12_), channel_id=1, source_target_pairs={{0,1},{1,0},{2,3},{3,2},{4,5},{5,4},{6,7},{7,6},{8,9},{9,8},{10,11... | collective-permute-start | bytes 1572872 | tf_op jit(solution)/shard_map/ppermute | solution.py:66
  205.9 18.7 %collective-permute-start.19 = (bf16[128,2048]{1,0:T(8,128)(2,1)}, bf16[128,2048]{1,0:T(8,128)(2,1)S(1)}, u32[]{:S(2)}, u32[]{:S(2)}) collective-permute-start(bf16[128,2048]{1,0:T(8,128)(2,1)} %get-tuple-element.56), channel_id=1, source_target_pairs={{0,1},{1,0},{2,3},{3,2},{4,5},{5,4},{6,7},{7,6},{8,9},{9,8},{10,11... | collective-permute-start | bytes 1572872 | tf_op jit(solution)/shard_map/ppermute | solution.py:66
  209.1 15.5 %collective-permute-start.21 = (bf16[128,2048]{1,0:T(8,128)(2,1)S(1)}, bf16[128,2048]{1,0:T(8,128)(2,1)S(1)}, u32[]{:S(2)}, u32[]{:S(2)}) collective-permute-start(bf16[128,2048]{1,0:T(8,128)(2,1)S(1)} %add_convert_fusion.3), channel_id=1, source_target_pairs={{0,2},{2,0},{1,3},{3,1},{4,6},{6,4},{5,7},{7,5},{8,10},{10,8},{9,1... | collective-permute-start | bytes 1572872 | tf_op jit(solution)/shard_map/ppermute | solution.py:70
  209.7 13.5 %collective-permute-start.23 = (bf16[1,512]{1,0:T(2,128)(2,1)S(1)}, bf16[1,512]{1,0:T(2,128)(2,1)S(1)}, u32[]{:S(2)}, u32[]{:S(2)}) collective-permute-start(bf16[1,512]{1,0:T(2,128)(2,1)S(1)} %get-tuple-element.102), channel_id=1, source_target_pairs={{0,2},{2,0},{1,3},{3,1},{4,6},{6,4},{5,7},{7,5},{8,10},{10,8},{9,1... | collective-permute-start | bytes 3080 | tf_op jit(solution)/shard_map/ppermute | solution.py:70
  211.3 12.5 %collective-permute-start.22 = (bf16[1,512]{1,0:T(2,128)(2,1)S(1)}, bf16[1,512]{1,0:T(2,128)(2,1)S(1)}, u32[]{:S(2)}, u32[]{:S(2)}) collective-permute-start(bf16[1,512]{1,0:T(2,128)(2,1)S(1)} %get-tuple-element.102), channel_id=1, source_target_pairs={{0,1},{1,0},{2,3},{3,2},{4,5},{5,4},{6,7},{7,6},{8,9},{9,8},{10,11... | collective-permute-start | bytes 3080 | tf_op jit(solution)/shard_map/ppermute | solution.py:66
  229.5 14.5 %collective-permute-start.26 = (bf16[128,2048]{1,0:T(8,128)(2,1)}, bf16[128,2048]{1,0:T(8,128)(2,1)S(1)}, u32[]{:S(2)}, u32[]{:S(2)}) collective-permute-start(bf16[128,2048]{1,0:T(8,128)(2,1)} %get-tuple-element.61.p0), channel_id=1, source_target_pairs={{0,2},{2,0},{1,3},{3,1},{4,6},{6,4},{5,7},{7,5},{8,10},{10,8},{9,1... | collective-permute-start | bytes 1572872 | tf_op jit(solution)/shard_map/ppermute | solution.py:70
  230.1 20.5 %collective-permute-start.25 = (bf16[128,2048]{1,0:T(8,128)(2,1)}, bf16[128,2048]{1,0:T(8,128)(2,1)S(1)}, u32[]{:S(2)}, u32[]{:S(2)}) collective-permute-start(bf16[128,2048]{1,0:T(8,128)(2,1)} %get-tuple-element.61.p0), channel_id=1, source_target_pairs={{0,1},{1,0},{2,3},{3,2},{4,5},{5,4},{6,7},{7,6},{8,9},{9,8},{10,11... | collective-permute-start | bytes 1572872 | tf_op jit(solution)/shard_map/ppermute | solution.py:66
  244.1 6.5 %collective-permute-start.27 = (bf16[128,2048]{1,0:T(8,128)(2,1)S(1)}, bf16[128,2048]{1,0:T(8,128)(2,1)S(1)}, u32[]{:S(2)}, u32[]{:S(2)}) collective-permute-start(bf16[128,2048]{1,0:T(8,128)(2,1)S(1)} %collective-permute-done.26.p2), channel_id=1, source_target_pairs={{0,1},{1,0},{2,3},{3,2},{4,5},{5,4},{6,7},{7,6},{8,9},{9,8},{10,11... | collective-permute-start | bytes 1572872 | tf_op jit(solution)/shard_map/ppermute | solution.py:66
  246.0 3.9 collective-permute-start.29
  288.7 7.8 %collective-permute-start.30 = (bf16[512,512]{1,0:T(8,128)(2,1)}, bf16[512,512]{1,0:T(8,128)(2,1)S(1)}, u32[]{:S(2)}, u32[]{:S(2)}) collective-permute-start(bf16[512,512]{1,0:T(8,128)(2,1)} %get-tuple-element.69), channel_id=1, source_target_pairs={{0,1},{1,0},{2,3},{3,2},{4,5},{5,4},{6,7},{7,6},{8,9},{9,8},{10,11... | collective-permute-start | bytes 1572872 | tf_op jit(solution)/shard_map/ppermute | solution.py:66
  292.0 14.7 %collective-permute-start.32 = (bf16[512,512]{1,0:T(8,128)(2,1)S(1)}, bf16[512,512]{1,0:T(8,128)(2,1)S(1)}, u32[]{:S(2)}, u32[]{:S(2)}) collective-permute-start(bf16[512,512]{1,0:T(8,128)(2,1)S(1)} %add_convert_fusion.2), channel_id=1, source_target_pairs={{0,2},{2,0},{1,3},{3,1},{4,6},{6,4},{5,7},{7,5},{8,10},{10,8},{9,1... | collective-permute-start | bytes 1572872 | tf_op jit(solution)/shard_map/ppermute | solution.py:70
  295.0 18.6 %collective-permute-start.36 = (f32[2,16,512]{2,1,0:T(8,128)S(1)}, f32[2,16,512]{2,1,0:T(8,128)S(1)}, u32[]{:S(2)}, u32[]{:S(2)}) collective-permute-start(f32[2,16,512]{2,1,0:T(8,128)S(1)} %add.175), channel_id=1, source_target_pairs={{0,2},{2,0},{1,3},{3,1},{4,6},{6,4},{5,7},{7,5},{8,10},{10,8},{9,1... | collective-permute-start | bytes 196616 | tf_op jit(solution)/shard_map/ppermute | solution.py:70
  326.7 14.0 %collective-permute-start.39 = (bf16[512,512]{1,0:T(8,128)(2,1)S(1)}, bf16[512,512]{1,0:T(8,128)(2,1)S(1)}, u32[]{:S(2)}, u32[]{:S(2)}) collective-permute-start(bf16[512,512]{1,0:T(8,128)(2,1)S(1)} %add_convert_fusion.1), channel_id=1, source_target_pairs={{0,2},{2,0},{1,3},{3,1},{4,6},{6,4},{5,7},{7,5},{8,10},{10,8},{9,1... | collective-permute-start | bytes 1572872 | tf_op jit(solution)/shard_map/ppermute | solution.py:70
  376.9 63.0 %all-to-all-start.3 = ((bf16[8,3,128,256]{3,2,1,0:T(8,128)(2,1)}), bf16[8,3,128,256]{3,2,1,0:T(8,128)(2,1)S(1)}, u32[]{:S(2)}, u32[]{:S(2)}) async-start(bf16[8,3,128,256]{3,2,1,0:T(8,128)(2,1)} %attention_back.1), calls=%async_computation.3 | async-start | bytes 3145728 | tf_op jit(solution)/shard_map/all_to_all | solution.py:570
  380.6 138.1 %all-reduce.3.cloned.1.call-start = ((), (), s32[]{:S(2)}) async-start(), calls=%async_computation.6 | async-start | bytes 4194304 | tf_op jit(solution)/shard_map/psum | solution.py:715
  469.5 8.4 %collective-permute-start.46 = (f32[3,16,512]{2,1,0:T(8,128)S(1)}, f32[3,16,512]{2,1,0:T(8,128)S(1)}, u32[]{:S(2)}, u32[]{:S(2)}) collective-permute-start(f32[3,16,512]{2,1,0:T(8,128)S(1)} %add.183), channel_id=1, source_target_pairs={{0,2},{2,0},{1,3},{3,1},{4,6},{6,4},{5,7},{7,5},{8,10},{10,8},{9,1... | collective-permute-start | bytes 294920 | tf_op jit(solution)/shard_map/ppermute | solution.py:70
  470.1 17.2 %collective-permute-start.43 = (bf16[128,2048]{1,0:T(8,128)(2,1)}, bf16[128,2048]{1,0:T(8,128)(2,1)S(1)}, u32[]{:S(2)}, u32[]{:S(2)}) collective-permute-start(bf16[128,2048]{1,0:T(8,128)(2,1)} %get-tuple-element.86), channel_id=1, source_target_pairs={{0,1},{1,0},{2,3},{3,2},{4,5},{5,4},{6,7},{7,6},{8,9},{9,8},{10,11... | collective-permute-start | bytes 1572872 | tf_op jit(solution)/shard_map/ppermute | solution.py:66
  472.3 3.9 collective-permute-start.48
  483.8 30.1 %all-to-all-start.4 = ((bf16[8,56,512]{2,1,0:T(8,128)(2,1)}), bf16[8,56,512]{2,1,0:T(8,128)(2,1)S(1)}, u32[]{:S(2)}, u32[]{:S(2)}) async-start(bf16[8,56,512]{2,1,0:T(8,128)(2,1)} %bitcast.21), calls=%async_computation.4 | async-start | bytes 917504 | tf_op jit(solution)/shard_map/all_to_all | solution.py:804
  487.2 32.6 %collective-permute-start.42 = (bf16[128,2048]{1,0:T(8,128)(2,1)}, bf16[128,2048]{1,0:T(8,128)(2,1)S(1)}, u32[]{:S(2)}, u32[]{:S(2)}) collective-permute-start(bf16[128,2048]{1,0:T(8,128)(2,1)} %get-tuple-element.84), channel_id=1, source_target_pairs={{0,1},{1,0},{2,3},{3,2},{4,5},{5,4},{6,7},{7,6},{8,9},{9,8},{10,11... | collective-permute-start | bytes 1572872 | tf_op jit(solution)/shard_map/ppermute | solution.py:66
  487.5 32.3 %collective-permute-start.44 = (bf16[128,2048]{1,0:T(8,128)(2,1)S(1)}, bf16[128,2048]{1,0:T(8,128)(2,1)S(1)}, u32[]{:S(2)}, u32[]{:S(2)}) collective-permute-start(bf16[128,2048]{1,0:T(8,128)(2,1)S(1)} %add_convert_fusion), channel_id=1, source_target_pairs={{0,2},{2,0},{1,3},{3,1},{4,6},{6,4},{5,7},{7,5},{8,10},{10,8},{9,1... | collective-permute-start | bytes 1572872 | tf_op jit(solution)/shard_map/ppermute | solution.py:70
  514.8 15.7 %all-to-all-start.5 = ((bf16[8,56,512]{2,1,0:T(8,128)(2,1)}), bf16[8,56,512]{2,1,0:T(8,128)(2,1)S(1)}, u32[]{:S(2)}, u32[]{:S(2)}) async-start(bf16[8,56,512]{2,1,0:T(8,128)(2,1)} %broadcast_in_dim.114), calls=%async_computation.5 | async-start | bytes 917504 | tf_op jit(solution)/shard_map/all_to_all | solution.py:806
  (58 other events, 251.1 us)
Sparse Core Ops, SparseCore 0:
  385.2 133.5 all-reduce.2

commit v3 on v2

--- a/solution.py
+++ b/solution.py
@@ -106,43 +106,52 @@
     return pl.BlockSpec(array.shape, lambda *_: (0,) * rank)
 
 
-def kernel_call(body, name, grid, ins, outs, scratch=(), me=None, flops=0):
+def kernel_call(body, name, grid, ins, outs, scratch, me, flops, keep, after, grant):
     arrays = [i[0] if isinstance(i, tuple) else i for i in ins]
     in_specs = [i[1] if isinstance(i, tuple) else whole(i) for i in ins]
     shapes = [o[0] if isinstance(o, tuple) else o for o in outs]
     out_specs = [o[1] if isinstance(o, tuple) else whole(o) for o in outs]
     moved = sum(math.prod(s.block_shape) * a.dtype.itemsize for s, a in zip(in_specs, arrays))
-    moved += sum(math.prod(s.shape) * s.dtype.itemsize for s in shapes)
+    moved += sum(math.prod(s.block_shape) * a.dtype.itemsize for s, a in zip(out_specs, shapes))
+    first = 1 + len(arrays)
+    extra = [array for array, _ in keep] + list(after)
+
+    def run(*refs):
+        return body(*refs[:first], *refs[first + len(extra) :])
+
     return pl.pallas_call(
-        body,
+        run,
         name=name,
         out_shape=shapes,
         grid_spec=pltpu.PrefetchScalarGridSpec(
             num_scalar_prefetch=1,
             grid=grid,
-            in_specs=in_specs,
+            in_specs=in_specs + [pl.BlockSpec(memory_space=pl.ANY)] * len(extra),
             out_specs=out_specs,
             scratch_shapes=list(scratch),
         ),
-        compiler_params=pltpu.CompilerParams(dimension_semantics=("arbitrary",) * len(grid)),
+        input_output_aliases={first + i: out for i, (_, out) in enumerate(keep)},
+        compiler_params=pltpu.CompilerParams(
+            dimension_semantics=("arbitrary",) * len(grid), vmem_limit_bytes=grant << 20
+        ),
         cost_estimate=pl.CostEstimate(
-            flops=int(flops), bytes_accessed=int(moved), transcendentals=0
+            flops=int(flops), bytes_accessed=int(moved * math.prod(grid)), transcendentals=0
         ),
-    )(me, *arrays)
+    )(me, *arrays, *extra)
 
 
 def shape(dims, dtype):
     return jax.ShapeDtypeStruct(dims, dtype)
 
 
-def qkv_body(me, p0, p1, p2, p3, w, a, b, mask, proj, low_ref, squares, own_ref, rows_scr, low_scr):
+def qkv_body(me, p0, p1, w, a, b, mask, proj, low_ref, squares, own_ref, rows_scr, low_scr):
     step = pl.program_id(0)
     rows = p0.shape[0]
 
     @pl.when(step == 0)
     def _():
-        for flip, piece in enumerate((p0, p1, p2, p3)):
-            rows_scr[window(me[0] ^ flip, rows), :] = piece[...]
+        rows_scr[window(me[1], rows), :] = p0[...]
+        rows_scr[window(1 - me[1], rows), :] = p1[...]
         own_ref[...] = rows_scr[:, window(me[0], own_ref.shape[1])]
         squares[...] = jnp.zeros_like(squares)
         stacked = a[...].reshape(-1, a.shape[2])
@@ -246,10 +255,11 @@
 
 
 def mlp_body(
-    me, p0, p1, p2, p3, wg, wu, wd, a, bg, bu, ad, b_down, mask,
-    gate_ref, up_ref, product_ref, low_ref, low_down, mid_rows, o0, o1, o2, o3,
-    rows_scr, low_scr, acc,
+    near, me, p0, p1, p2, p3, wg, wu, wd, a, bg, bu, ad, b_down, mask, *refs
 ):
+    gate_ref, up_ref, product_ref, low_ref, low_down, *refs = refs
+    rows_scr, low_scr, acc = refs[-3:]
+    parts = refs[:2]
     step = pl.program_id(0)
     width = p0.shape[1]
 
@@ -257,11 +267,14 @@
     def _():
         for flip, piece in enumerate((p0, p1, p2, p3)):
             rows_scr[:, window(me[0] ^ flip, width)] = piece[...]
-        mid_rows[...] = rows_scr[window(me[0], mid_rows.shape[0]), :]
+        if near:
+            mid_rows = refs[2]
+            mid_rows[...] = rows_scr[window(me[1], mid_rows.shape[0]), :]
         stacked = mm_t(a[...].reshape(-1, a.shape[2]), rows_scr[...])
         for k in range(2):
             low_ref[k] = (stacked[k * LOW : (k + 1) * LOW] * mask[...]).astype(BF16)
         low_scr[...] = jnp.zeros_like(low_scr)
+        acc[...] = jnp.zeros_like(acc)
 
     gate = mm(rows_scr[...], wg[0]) + SCALE * tmm(low_ref[0], bg[0])
     up = mm(rows_scr[...], wu[0]) + SCALE * tmm(low_ref[1], bu[0])
@@ -270,23 +283,15 @@
     product = (gate * jax.nn.sigmoid(gate) * up).astype(BF16)
     product_ref[...] = product
     low_scr[...] += mm_t(ad[0], product)
-    part = mm_t(product, wd[0])
-
-    @pl.when(step == 0)
-    def _():
-        acc[...] = part
-
-    @pl.when(step > 0)
-    def _():
-        acc[...] += part
+    acc[...] += mm_t(product, wd[0])
 
     @pl.when(step == pl.num_programs(0) - 1)
     def _():
         low = low_scr[...] * mask[...]
         low_down[...] = narrow(low)
         acc[...] += SCALE * tmm(low.astype(BF16), b_down[0])
-        for flip, out in enumerate((o0, o1, o2, o3)):
-            out[...] = acc[window(me[0] ^ flip, out.shape[0]), :].astype(BF16)
+        for flip, out in enumerate(parts):
+            out[...] = acc[window(me[1] ^ flip, out.shape[0]), :].astype(BF16)
 
 
 def turn_body(me, y0, y1, y2, mid_rows, upstream_ref, valid, gain, result, grad, masked):
@@ -301,9 +306,9 @@
 
 
 def mlp_back_body(
-    me, p0, p1, p2, p3, masked, wg, wu, wd, a, bg, bu, ad, b_down, mask,
-    gate_ref, up_ref, product_ref, low_ref, low_down,
-    grads, grad_b_down, low_parts, o0, o1, o2, o3,
+    near, me, p0, p1, seed, wg, wu, wd, a, bg, bu, ad, b_down, mask,
+    gate_ref, up_ref, product_ref, low_ref,
+    grads, own_ref, low_parts, o0, o1, o2, o3,
     rows_scr, low_scr, part_scr, acc,
 ):
     step = pl.program_id(0)
@@ -312,14 +317,14 @@
 
     @pl.when(step == 0)
     def _():
-        for flip, piece in enumerate((p0, p1, p2, p3)):
-            rows_scr[window(me[0] ^ flip, rows), :] = piece[...]
+        rows_scr[window(me[1], rows), :] = p0[...]
+        rows_scr[window(1 - me[1], rows), :] = p1[...]
+        own_ref[...] = rows_scr[:, window(me[0], width)]
         low_scr[...] = (SCALE * mm_t(b_down[0], rows_scr[...]) * mask[...]).astype(BF16)
-        wide = widen(low_down[...], mask[...])
-        grad_b_down[...] = SCALE * mm(wide, rows_scr[:, window(me[0], width)])
         part_scr[...] = jnp.zeros_like(part_scr)
         acc[...] = jnp.zeros_like(acc)
-        acc[window(me[0], rows), :] = masked[...].astype(F32)
+        if near:
+            acc[window(me[1], rows), :] = seed[...].astype(F32)
 
     grad_product = mm(rows_scr[...], wd[0]) + tmm(low_scr[...], ad[0])
     gate = gate_ref[...]
@@ -329,9 +334,13 @@
     grad_gate = (
         grad_product * up_ref[...] * sigmoid * (1.0 + gate * (1.0 - sigmoid))
     ).astype(BF16)
-    grads[0] = SCALE * mm(low_ref[0], grad_gate)
-    grads[1] = SCALE * mm(low_ref[1], grad_up)
-    grads[2] = mm(low_scr[...], product_ref[...])
+    terms = (
+        SCALE * mm(low_ref[0], grad_gate),
+        SCALE * mm(low_ref[1], grad_up),
+        mm(low_scr[...], product_ref[...]),
+    )
+    for k, term in enumerate(terms):
+        grads[k] = term if near else term + seed[k]
     part_scr[0] += SCALE * mm_t(bg[0], grad_gate)
     part_scr[1] += SCALE * mm_t(bu[0], grad_up)
     acc[...] += mm_t(grad_gate, wg[0]) + mm_t(grad_up, wu[0])
@@ -346,15 +355,17 @@
             out[...] = acc[:, window(me[0] ^ flip, width)].astype(BF16)
 
 
-def mid_sum_body(me, y0, y1, y2, branch, gain, grad_mid, sums):
-    grad = total((y0, y1, y2))
-    grad_mid[...] = grad
-    sums[...] = row_sums(grad * gain[2:3, :] * branch[...], 0)
+def mid_sum_body(me, y0, y1, y2, z0, z1, z2, branch, gain, grad_mid, sums):
+    half = y0.shape[0]
+    chip = me[0] // 2
+    grad_mid[window(chip, half), :] = total((y0, y1, y2))
+    grad_mid[window(1 - chip, half), :] = total((z0, z1, z2))
+    sums[...] = row_sums(grad_mid[...] * gain[2:3, :] * branch[...], 0)
 
 
 def branch_back_body(
     model_dim, me, grad_mid, branch, squares, sums, gain, w, a, b, mask, low_out, low_sums, mid,
-    grad_b, grad_a, low_parts, o0, o1, o2, o3,
+    low_down, grad_down, grads, low_parts, o0, o1, o2, o3,
 ):
     scale = lax.rsqrt(column(squares[...], 0) * (1.0 / model_dim) + NORM_EPS)
     mean = column(sums[...], 0) * (1.0 / model_dim)
@@ -363,24 +374,17 @@
     low = SCALE * mm_t(b[0], grad) * mask[...]
     low_parts[...] = narrow(low)
     low = low.astype(BF16)
-    width = o0.shape[1]
+    width = grad.shape[1]
+    seqs, splits, rows, span = o0.shape
     for flip, out in enumerate((o0, o1, o2, o3)):
         at = window(me[0] ^ flip, width)
-        out[...] = (mm_t(grad, w[0, at, :]) + tmm(low, a[0, :, at])).astype(BF16)
-    grad_b[...] = SCALE * mm(low_out[...], grad)
+        part = (mm_t(grad, w[0, at, :]) + tmm(low, a[0, :, at])).astype(BF16)
+        for i in range(splits):
+            out[:, i] = part[:, i * span : (i + 1) * span].reshape(seqs, rows, span)
     for k in range(2):
-        grad_a[k] = mm(widen(low_sums[k], mask[...]), mid[...])
-
-
-def heads_body(y0, y1, y2):
-    return total((y0, y1, y2))
-
-
-def split_body(per_member, me, y0, y1, y2, out):
-    grad = total((y0, y1, y2)).astype(BF16)
-    extent = per_member * HEAD_DIM
-    for part in range(out.shape[0]):
-        out[part] = grad[:, part * extent : (part + 1) * extent]
+        grads[k] = mm(widen(low_sums[k], mask[...]), mid[...]).astype(BF16)
+    grads[2] = (SCALE * mm(low_out[...], grad)).astype(BF16)
+    grads[3] = (SCALE * mm(widen(low_down[...], mask[...]), grad_down[...])).astype(BF16)
 
 
 def turn_back_body(per_member, me, grads, proj, gain, cosine, sine, turned, sums):
@@ -400,17 +404,10 @@
     sums[...] = result
 
 
-def qkv_back_body(
-    model_dim, me, turned, proj, squares, sums, grad_mid, w, a, b, mask, low_ref,
-    grad_b, low_parts, o0, o1, o2, o3, acc,
+def qkv_grad_body(
+    model_dim, me, turned, proj, squares, sums, b, mask, low_ref, grad_ref, grad_b, low_wide, low_parts
 ):
     step = pl.program_id(0)
-
-    @pl.when(step == 0)
-    def _():
-        acc[...] = jnp.zeros_like(acc)
-        acc[:, window(me[0], grad_mid.shape[1])] = grad_mid[...]
-
     here = lax.broadcasted_iota(jnp.int32, squares.shape, 0) == step
 
     def chosen(values):
@@ -422,26 +419,38 @@
     scale = jnp.where(step == 2, 1.0, scale)
     mean = jnp.where(step == 2, 0.0, mean)
     grad = (scale * turned[0] - proj[0] * (scale * scale * scale) * mean).astype(BF16)
+    grad_ref[0] = grad
     low = SCALE * mm_t(b[0], grad) * mask[...]
     low_parts[0] = narrow(low)
-    grad_b[0] = SCALE * mm(low_ref[0], grad)
-    acc[...] += mm_t(grad, w[0]) + tmm(low.astype(BF16), a[0])
+    low_wide[0] = low.astype(BF16)
+    grad_b[0] = (SCALE * mm(low_ref[0], grad)).astype(BF16)
+
+
+def qkv_back_body(me, grad, low, grad_mid, w, a, o0, o1, acc):
+    step = pl.program_id(0)
+
+    @pl.when(step == 0)
+    def _():
+        acc[...] = jnp.zeros_like(acc)
+        acc[:, window(me[0], grad_mid.shape[1])] = grad_mid[...]
+
+    acc[...] += mm_t(grad[0], w[0]) + tmm(low[0], a[0])
 
     @pl.when(step == pl.num_programs(0) - 1)
     def _():
-        for flip, out in enumerate((o0, o1, o2, o3)):
-            out[...] = acc[window(me[0] ^ flip, out.shape[0]), :].astype(BF16)
-
-
-def last_grads_body(me, low_in, low_out, own, attended, mask, grad_in, grad_out):
+        for flip, out in enumerate((o0, o1)):
+            out[...] = acc[window(me[1] ^ flip, out.shape[0]), :].astype(BF16)
+
+
+def last_grads_body(me, low_in, low_out, own, attended, mask, grads):
     for k in range(3):
-        grad_in[k] = mm(widen(low_in[k], mask[...]), own[...])
+        grads[k] = mm(widen(low_in[k], mask[...]), own[...]).astype(BF16)
     wide = widen(low_out[...], mask[...])
     splits, rows, extent = attended.shape[1:]
     for part in range(splits):
-        grad_out[:, part * extent : (part + 1) * extent] = mm(
+        grads[3, :, part * extent : (part + 1) * extent] = mm(
             wide, attended[:, part].reshape(-1, extent)
-        )
+        ).astype(BF16)
 
 
 def per_device(
@@ -465,7 +474,7 @@
     hidden_width = mlp_weight.shape[2]
     local_heads = width // HEAD_DIM
     me = lax.axis_index("wsh")
-    here = me.astype(jnp.int32).reshape(1)
+    here = jnp.stack([me, me % 2, me // 2]).astype(jnp.int32)
     ctx_index = lax.axis_index("ctx")
     pairs = seqs * local_heads
     members = math.gcd(ctx_size, pairs)
@@ -480,14 +489,24 @@
     key_groups = [[g * members + i for g in range(groups)] for i in range(members)]
     all_rows = seqs * rows
 
-    def call(body, name, grid, ins, outs, scratch=(), flops=0):
-        return kernel_call(body, name, grid, ins, outs, scratch, here, flops)
+    def call(body, name, grid, ins, outs, scratch=(), flops=0, keep=(), after=(), grant=40):
+        return kernel_call(
+            body, name, grid, ins, outs, scratch, here, flops, keep, after, grant
+        )
 
     def bind(body, *fixed):
         def bound(*refs):
             return body(*fixed, *refs)
 
         return bound
+
+    rows_qkv = gather_wsh(adapt_model[:3], 2, me)
+    hidden = pieces_wsh(own_rows)
+    rest = lax.optimization_barrier(
+        (jnp.concatenate([adapt_model[3:6], adapt_model[10:11]], 0), norm_gains, hidden[2])
+    )
+    rows_a = gather_wsh(rest[0], 2, me)
+    last_gain = jnp.broadcast_to(gather_wsh(rest[1][3:4], 1, me).astype(F32), (8, model_dim))
 
     orders = gather_wsh(block_order, 0, me)
     positions = (orders[:, :, None] * block_rows + jnp.arange(block_rows)[None, None, :]).reshape(
@@ -516,22 +535,14 @@
     q_pos = jnp.broadcast_to(query_positions.astype(F32)[None], (8, group_rows))
     gains = norm_gains.astype(F32)
 
-    hidden = pieces_wsh(own_rows)
-    rows_a = gather_wsh(jnp.concatenate([adapt_model[:6], adapt_model[10:11]], 0), 2, me)
-    last_gain = jnp.broadcast_to(
-        gather_wsh(norm_gains[3:4], 1, me).astype(F32), (8, model_dim)
-    )
-
-    def stack_block(index):
-        return pl.BlockSpec((1, all_rows, width), lambda k, *_: (k, 0, 0))
-
     w_qkv = (attn_weight, pl.BlockSpec((1, model_dim, width), lambda k, *_: (k, 0, 0)))
     w_out = (attn_weight, pl.BlockSpec((1, model_dim, width), lambda *_: (3, 0, 0)))
-    a_qkv = (rows_a, pl.BlockSpec((3, LOW, model_dim), lambda *_: (0, 0, 0)))
-    a_step = (rows_a, pl.BlockSpec((1, LOW, model_dim), lambda k, *_: (k, 0, 0)))
-    a_out = (rows_a, pl.BlockSpec((1, LOW, model_dim), lambda *_: (3, 0, 0)))
-    a_mlp = (rows_a, pl.BlockSpec((2, LOW, model_dim), lambda *_: (2, 0, 0)))
-    b_down = (rows_a, pl.BlockSpec((1, LOW, model_dim), lambda *_: (6, 0, 0)))
+    a_qkv = (rows_qkv, pl.BlockSpec((3, LOW, model_dim), lambda *_: (0, 0, 0)))
+    a_step = (rows_qkv, pl.BlockSpec((1, LOW, model_dim), lambda k, *_: (k, 0, 0)))
+    a_out = (rows_a, pl.BlockSpec((1, LOW, model_dim), lambda *_: (0, 0, 0)))
+    a_gate = (rows_a, pl.BlockSpec((1, LOW, model_dim), lambda *_: (1, 0, 0)))
+    a_up = (rows_a, pl.BlockSpec((1, LOW, model_dim), lambda *_: (2, 0, 0)))
+    b_down = (rows_a, pl.BlockSpec((1, LOW, model_dim), lambda *_: (3, 0, 0)))
     b_step = (adapt_model, pl.BlockSpec((1, LOW, width), lambda k, *_: (6 + k, 0, 0)))
     b_out = (adapt_model, pl.BlockSpec((1, LOW, width), lambda *_: (9, 0, 0)))
     step_rows = pl.BlockSpec((1, all_rows, width), lambda k, *_: (k, 0, 0))
@@ -539,20 +550,45 @@
 
     matmul = 2.0 * all_rows * model_dim * width
 
-    proj, low_in, squares, own_columns = call(
-        qkv_body,
-        "qkv",
-        (3,),
-        [*hidden, w_qkv, a_qkv, b_step, mask],
-        [
-            (shape((3, all_rows, width), F32), step_rows),
-            (shape((3, LOW, all_rows), BF16), step_low),
-            shape((8, all_rows), F32),
-            shape((all_rows, width), BF16),
-        ],
-        [pltpu.VMEM((all_rows, model_dim), BF16), pltpu.VMEM((3 * LOW, all_rows), F32)],
-        3 * matmul,
-    )
+    pair_rows = 2 * rows
+
+    def half_rows(side, dims):
+        def block(*args):
+            half = args[-1][2] ^ side
+            return tuple(half if d == -1 else (args[d] if d < 9 else 0) for d in dims)
+
+        return block
+
+    NONE = 9
+
+    state = ()
+    for side, pieces in ((0, hidden[:2]), (1, hidden[2:])):
+        state = call(
+            qkv_body,
+            "qkv",
+            (3,),
+            [*pieces, w_qkv, a_qkv, b_step]
+            + [(mask, pl.BlockSpec((LOW, pair_rows), half_rows(side, (NONE, -1))))],
+            [
+                (
+                    shape((3, all_rows, width), F32),
+                    pl.BlockSpec((1, pair_rows, width), half_rows(side, (0, -1, NONE))),
+                ),
+                (
+                    shape((3, LOW, all_rows), BF16),
+                    pl.BlockSpec((1, LOW, pair_rows), half_rows(side, (0, NONE, -1))),
+                ),
+                (shape((8, all_rows), F32), pl.BlockSpec((8, pair_rows), half_rows(side, (NONE, -1)))),
+                (
+                    shape((all_rows, width), BF16),
+                    pl.BlockSpec((pair_rows, width), half_rows(side, (-1, NONE))),
+                ),
+            ],
+            [pltpu.VMEM((pair_rows, model_dim), BF16), pltpu.VMEM((3 * LOW, pair_rows), F32)],
+            1.5 * matmul,
+            keep=[(array, i) for i, array in enumerate(state)],
+        )
+    proj, low_in, squares, own_columns = state
     squares = sum_wsh(squares)
     proj_rows = (proj, pl.BlockSpec((3, rows, width), lambda s, *_: (0, s, 0)))
     tables = [(t, pl.BlockSpec((rows, HEAD_DIM), lambda s, *_: (s, 0))) for t in (cosine, sine)]
@@ -620,7 +656,7 @@
         [shape((all_rows, width), BF16)],
     )
 
-    tile = 256
+    tile = 512
     steps = hidden_width // tile
 
     def w_mlp(index):
@@ -629,100 +665,136 @@
     def hidden_low(index):
         return (adapt_hidden, pl.BlockSpec((1, LOW, tile), lambda j, *_: (index, 0, j)))
 
-    tile_rows = pl.BlockSpec((all_rows, tile), lambda j, *_: (0, j))
+    def side_weights(side):
+        return [w_mlp(0), w_mlp(1), w_mlp(2), a_pair, hidden_low(0), hidden_low(1)] + [
+            hidden_low(2),
+            b_down,
+            (mask, pl.BlockSpec((LOW, pair_rows), half_rows(side, (NONE, -1)))),
+        ]
+
+    a_pair = (rows_a[1:3], pl.BlockSpec((2, LOW, model_dim), lambda *_: (0, 0, 0)))
     mid_pieces = pieces_wsh(mid)
-    weights = [w_mlp(0), w_mlp(1), w_mlp(2), a_mlp]
-    weights += [hidden_low(0), hidden_low(1), hidden_low(2), b_down, mask]
-    wide = shape((all_rows, hidden_width), F32)
-    gate, up, product, low_mid, low_down, mid_rows, *parts = call(
-        mlp_body,
-        "mlp",
-        (steps,),
-        [*mid_pieces, *weights],
-        [
-            (wide, tile_rows),
-            (wide, tile_rows),
-            (shape((all_rows, hidden_width), BF16), tile_rows),
-            shape((2, LOW, all_rows), BF16),
-            shape((RANK, all_rows), F32),
-            shape((rows, model_dim), BF16),
-        ]
-        + [shape((rows, model_dim), BF16)] * 4,
-        [
-            pltpu.VMEM((all_rows, model_dim), BF16),
-            pltpu.VMEM((LOW, all_rows), F32),
-            pltpu.VMEM((all_rows, model_dim), F32),
-        ],
-        12 * matmul,
-    )
-    down_parts = scatter_wsh(*parts)
-    low_down = sum_wsh(low_down)
-    result, grad_down, masked = call(
+    state = ()
+    parts = {}
+    for side in (1, 0):
+        tile_rows = pl.BlockSpec((pair_rows, tile), half_rows(side, (-1, 0)))
+        rows_here = pl.BlockSpec((pair_rows, width), half_rows(side, (-1, NONE)))
+        result = call(
+            bind(mlp_body, side == 0),
+            "mlp",
+            (steps,),
+            [(piece, rows_here) for piece in mid_pieces] + side_weights(side),
+            [
+                (shape((all_rows, hidden_width), F32), tile_rows),
+                (shape((all_rows, hidden_width), F32), tile_rows),
+                (shape((all_rows, hidden_width), BF16), tile_rows),
+                (
+                    shape((2, LOW, all_rows), BF16),
+                    pl.BlockSpec((2, LOW, pair_rows), half_rows(side, (NONE, NONE, -1))),
+                ),
+                (
+                    shape((RANK, all_rows), F32),
+                    pl.BlockSpec((RANK, pair_rows), half_rows(side, (NONE, -1))),
+                ),
+            ]
+            + [shape((rows, model_dim), BF16)] * (3 - side),
+            [
+                pltpu.VMEM((pair_rows, model_dim), BF16),
+                pltpu.VMEM((LOW, pair_rows), F32),
+                pltpu.VMEM((pair_rows, model_dim), F32),
+            ],
+            6 * matmul,
+            keep=[(array, i) for i, array in enumerate(state)],
+        )
+        state, parts[side] = result[:5], result[5:]
+    gate, up, product, low_mid, low_down = state
+    far = (parts[1][0].astype(F32) + swap_core(parts[1][1]).astype(F32)).astype(BF16)
+    mid_rows = parts[0][2]
+    result_rows, grad_down, masked = call(
         turn_body,
         "turn",
         (1,),
-        [*down_parts, mid_rows, out_grad, valid, last_gain],
+        [parts[0][0], swap_core(parts[0][1]), swap_chip(far), mid_rows, out_grad, valid, last_gain],
         [shape((rows, model_dim), BF16)] * 3,
+        grant=20,
     )
 
     grad_pieces = pieces_wsh(grad_down)
-    hidden_grads, grad_b_down, low_parts, *parts = call(
-        mlp_back_body,
-        "mlp_back",
-        (steps,),
-        [*grad_pieces, masked, *weights]
-        + [(gate, tile_rows), (up, tile_rows), (product, tile_rows), low_mid, low_down],
-        [
-            (shape((3, LOW, hidden_width), F32), pl.BlockSpec((3, LOW, tile), lambda j, *_: (0, 0, j))),
-            shape((LOW, width), F32),
-            shape((2, RANK, all_rows), F32),
-        ]
-        + [shape((all_rows, width), BF16)] * 4,
-        [
-            pltpu.VMEM((all_rows, model_dim), BF16),
-            pltpu.VMEM((LOW, all_rows), BF16),
-            pltpu.VMEM((2, LOW, all_rows), F32),
-            pltpu.VMEM((all_rows, model_dim), F32),
-        ],
-        12 * matmul,
-    )
-    mid_parts = scatter_wsh(*parts)
+    state = ()
+    seed = masked
+    parts = {}
+    for side, pieces in ((0, grad_pieces[:2]), (1, grad_pieces[2:])):
+        tile_rows = pl.BlockSpec((pair_rows, tile), half_rows(side, (-1, 0)))
+        step_grads = pl.BlockSpec((3, LOW, tile), lambda j, *_: (0, 0, j))
+        hidden_grads, *result = call(
+            bind(mlp_back_body, side == 0),
+            "mlp_back",
+            (steps,),
+            [*pieces, seed if side == 0 else (seed, step_grads), *side_weights(side)]
+            + [(gate, tile_rows), (up, tile_rows), (product, tile_rows)]
+            + [(low_mid, pl.BlockSpec((2, LOW, pair_rows), half_rows(side, (NONE, NONE, -1))))],
+            [
+                (shape((3, LOW, hidden_width), F32), step_grads),
+                (
+                    shape((all_rows, width), BF16),
+                    pl.BlockSpec((pair_rows, width), half_rows(side, (-1, NONE))),
+                ),
+                (
+                    shape((2, RANK, all_rows), F32),
+                    pl.BlockSpec((2, RANK, pair_rows), half_rows(side, (NONE, NONE, -1))),
+                ),
+            ]
+            + [shape((pair_rows, width), BF16)] * 4,
+            [
+                pltpu.VMEM((pair_rows, model_dim), BF16),
+                pltpu.VMEM((LOW, pair_rows), BF16),
+                pltpu.VMEM((2, LOW, pair_rows), F32),
+                pltpu.VMEM((pair_rows, model_dim), F32),
+            ],
+            6 * matmul,
+            keep=[(array, i + 1) for i, array in enumerate(state)],
+        )
+        seed, state, parts[side] = hidden_grads, result[:2], scatter_wsh(*result[2:])
+    grad_down_own, low_parts = state
+
+    def sum_ctx(values):
+        count, lanes = values.shape
+        values = values.astype(BF16).reshape(ctx_size, -1, lanes)
+        values = lax.all_to_all(values, "ctx", 0, 0, tiled=True).astype(F32).sum(0).astype(BF16)
+        values = jnp.broadcast_to(values[None], (ctx_size,) + values.shape)
+        values = lax.all_to_all(values, "ctx", 0, 0, tiled=True)
+        return values.astype(F32).reshape(count, lanes)
+
+    hidden_grads = sum_ctx(hidden_grads.reshape(3 * LOW, hidden_width)).reshape(
+        3, LOW, hidden_width
+    )
+    low_down = sum_wsh(low_down)
     low_parts = sum_wsh(low_parts)
 
+    near, far = parts[0], parts[1]
     grad_mid, mid_sums = call(
         mid_sum_body,
         "mid_sum",
         (1,),
-        [*mid_parts, branch, gains],
+        [near[0], near[1], far[2], far[0], far[1], near[2], branch, gains],
         [shape((all_rows, width), F32), shape((8, all_rows), F32)],
+        grant=20,
     )
     mid_sums = sum_wsh(mid_sums)
-    grad_b_out, grad_a_mid, low_out_parts, *parts = call(
+    pieces_shape = shape((seqs, splits, rows, span), BF16)
+    early_grads, low_out_parts, *parts = call(
         bind(branch_back_body, model_dim),
         "branch_back",
         (1,),
         [grad_mid, branch, branch_squares, mid_sums, gains, w_out, a_out, b_out, mask]
-        + [low_out, low_parts, mid],
-        [
-            shape((LOW, width), F32),
-            shape((2, LOW, width), F32),
-            shape((RANK, all_rows), F32),
-        ]
-        + [shape((all_rows, width), BF16)] * 4,
+        + [low_out, low_parts, mid, low_down, grad_down_own],
+        [shape((4, LOW, width), BF16), shape((RANK, all_rows), F32)] + [pieces_shape] * 4,
         flops=matmul,
     )
-    early_grads = jnp.stack([grad_a_mid[0], grad_a_mid[1], grad_b_out, grad_b_down])
-    early_grads, hidden_grads = lax.psum((early_grads, hidden_grads), "ctx")
     low_out_parts = sum_wsh(low_out_parts)
     attended_parts = scatter_wsh(*parts)
-    seq_rows = pl.BlockSpec((rows, width), lambda s, *_: (s, 0))
-    (grad_attended,) = call(
-        bind(split_body, per_member),
-        "split",
-        (seqs,),
-        [(part, seq_rows) for part in attended_parts],
-        [(shape((members, rows, span), BF16), pl.BlockSpec((splits, rows, span), lambda s, *_: (s, 0, 0)))],
-    )
+    grad_attended = sum(part.astype(F32) for part in attended_parts).astype(BF16)
+    grad_attended = grad_attended.reshape(members, rows, span)
 
     grad_heads = exchange(grad_attended)
     back_ins = attention_ins + [(grad_heads, row_block)] + position_ins
@@ -774,40 +846,61 @@
         ],
     )
     sums = sum_wsh(sums)
-    grad_b_in, low_in_parts, *parts = call(
-        bind(qkv_back_body, model_dim),
-        "qkv_back",
+    half_low = pl.BlockSpec((1, LOW, width), lambda k, *_: (k, 0, 0))
+    grad_proj, grad_b_in, low_wide, low_in_parts = call(
+        bind(qkv_grad_body, model_dim),
+        "qkv_grad",
         (3,),
-        [(turned, step_rows), (proj, step_rows), squares, sums, grad_mid]
-        + [w_qkv, a_step, b_step, mask, (low_in, step_low)],
+        [(turned, step_rows), (proj, step_rows), squares, sums, b_step, mask, (low_in, step_low)],
         [
-            (shape((3, LOW, width), F32), pl.BlockSpec((1, LOW, width), lambda k, *_: (k, 0, 0))),
-            (shape((3, RANK, all_rows), F32), pl.BlockSpec((1, RANK, all_rows), lambda k, *_: (k, 0, 0))),
-        ]
-        + [shape((rows, model_dim), BF16)] * 4,
-        [pltpu.VMEM((all_rows, model_dim), F32)],
-        3 * matmul,
-    )
+            (shape((3, all_rows, width), BF16), step_rows),
+            (shape((3, LOW, width), BF16), half_low),
+            (shape((3, LOW, all_rows), BF16), step_low),
+            (
+                shape((3, RANK, all_rows), F32),
+                pl.BlockSpec((1, RANK, all_rows), lambda k, *_: (k, 0, 0)),
+            ),
+        ],
+        grant=20,
+    )
+
+    def input_grads(side, after):
+        return call(
+            qkv_back_body,
+            "qkv_back",
+            (3,),
+            [
+                (grad_proj, pl.BlockSpec((1, pair_rows, width), half_rows(side, (0, -1, NONE)))),
+                (low_wide, pl.BlockSpec((1, LOW, pair_rows), half_rows(side, (0, NONE, -1)))),
+                (grad_mid, pl.BlockSpec((pair_rows, width), half_rows(side, (-1, NONE)))),
+                w_qkv,
+                a_step,
+            ],
+            [shape((rows, model_dim), BF16)] * 2,
+            [pltpu.VMEM((pair_rows, model_dim), F32)],
+            1.5 * matmul,
+            after=after,
+        )
+
+    far_parts = input_grads(1, ())
     low_in_parts = sum_wsh(low_in_parts)
-    input_parts = scatter_wsh(*parts)
-    grad_inputs = sum(part.astype(F32) for part in input_parts)
-    grad_a_in, grad_a_out = call(
+    (last_grads,) = call(
         last_grads_body,
         "last_grads",
         (1,),
         [low_in_parts, low_out_parts, own_columns, attended, mask],
-        [shape((3, LOW, width), F32), shape((LOW, width), F32)],
-    )
-    late = jnp.concatenate([grad_a_in, grad_a_out[None], grad_b_in], 0).astype(BF16)
-    count = late.shape[0]
-    late = late.reshape(ctx_size, -1, width)
-    late = lax.all_to_all(late, "ctx", 0, 0, tiled=True).astype(F32).sum(0).astype(BF16)
-    late = jnp.broadcast_to(late[None], (ctx_size,) + late.shape)
-    late = lax.all_to_all(late, "ctx", 0, 0, tiled=True).astype(F32).reshape(count, LOW, width)
+        [shape((4, LOW, width), BF16)],
+        after=far_parts[:1],
+        grant=20,
+    )
+    near_parts = input_grads(0, (last_grads,))
+    input_parts = scatter_wsh(*near_parts, *far_parts)
+    grad_inputs = sum(part.astype(F32) for part in input_parts)
     model_grads = jnp.concatenate(
-        [late[:4], early_grads[:2], late[4:7], early_grads[2:]], 0
-    )
-    return (result[None], grad_inputs[None], model_grads, hidden_grads)
+        [last_grads, early_grads[:2], grad_b_in, early_grads[2:]], 0
+    )
+    model_grads = sum_ctx(model_grads.reshape(-1, width)).reshape(-1, LOW, width)
+    return (result_rows[None], grad_inputs[None], model_grads, hidden_grads)
 
 
 def solution(mesh):

time: 542 us -> 519 us (0.958); the launches traced: 540 us -> 512 us
  waiting for transfers between devices: 257 us -> 212 us
  local copies, waits for them, and re-layouts: 16.8 us -> 43.7 us
  starting transfers between devices: 39.2 us -> 61.2 us
  Pallas kernels: 151 us -> 134 us
  between operations: 14.6 us -> 2.22 us
    all_to_all x2, waiting for transfers between devices: 93.2 us -> 68.6 us  [exchange(): lax.all_to_all(values, 'ctx', 0, 0, tiled=True, axis_index_groups=ctx_gro...]
    unnamed x70 -> x163, local copies, waits for them, and re-layouts: 8.73 us -> 31.1 us
    pallas_call x15 -> x19, Pallas kernels: 151 us -> 134 us  [kernel_call(): pl.pallas_call(run, name=name, out_shape=shapes, grid_spec=pltpu.Prefetch...]
    all_to_all x2 -> x4, starting transfers between devices: 6.97 us -> 18.1 us  [the longest x2 10.3 us: sum_ctx(): lax.all_to_all(values, 'ctx', 0, 0, tiled=True).astype(F32).sum(0)]
    ppermute x19 -> x21, starting transfers between devices: 17.5 us -> 26.5 us  [swap_chip(): return lax.ppermute(values, 'wsh', CHIP_SWAP)]
    ppermute x30 -> x34, waiting for transfers between devices: 21.4 us -> 12.7 us  [swap_core(): return lax.ppermute(values, 'wsh', CORE_SWAP)]
    all_to_all x2 -> x4, waiting for transfers between devices: 34.2 us -> 27.7 us  [the longest x2 17.6 us: sum_ctx(): lax.all_to_all(values, 'ctx', 0, 0, tiled=True).astype(F32).sum(0)]
    ppermute x19 -> x21, waiting for transfers between devices: 108 us -> 103 us  [swap_chip(): return lax.ppermute(values, 'wsh', CHIP_SWAP)]
  transfers between devices with their start and end apart: 54 -> 61, of which waited for: 34 -> 30; matrix products, arithmetic and copies ran while one was open for 5% -> 6% of each run, Pallas kernels for 5% -> 15%
where the time goes in v3:
time: 519 us; the launch traced here: 512 us
  waiting for transfers between devices  212 us (41%)
  Pallas kernels  134 us (26%)
  starting transfers between devices  61.2 us (12%)
  local copies, waits for them, and re-layouts  43.7 us (8%)
  blocking collectives  36.6 us (7%)
  other arithmetic  22.1 us (4%)
    pallas_call x19, Pallas kernels, kernel_call(): pl.pallas_call(run, name=name, out_shape=shapes, grid_spec=pltpu.Prefetch...  134 us
    ppermute x21, waiting for transfers between devices, swap_chip(): return lax.ppermute(values, 'wsh', CHIP_SWAP)  103 us
    all_to_all x2, waiting for transfers between devices, exchange(): lax.all_to_all(values, 'ctx', 0, 0, tiled=True, axis_index_groups=ctx_gro...  68.6 us
    all_to_all x2, blocking collectives, exchange(): lax.all_to_all(values, 'ctx', 0, 0, tiled=True, axis_index_groups=ctx_gro...  36.6 us
    unnamed x163, local copies, waits for them, and re-layouts  31.1 us
    ppermute x21, starting transfers between devices, swap_chip(): return lax.ppermute(values, 'wsh', CHIP_SWAP)  26.5 us
    all_to_all x2, waiting for transfers between devices, sum_ctx(): lax.all_to_all(values, 'ctx', 0, 0, tiled=True).astype(F32).sum(0)  17.6 us
    ppermute x34, waiting for transfers between devices, swap_core(): return lax.ppermute(values, 'wsh', CORE_SWAP)  12.7 us
  transfers between devices with their start and end apart: 61, of which 30 were waited for; matrix products, arithmetic and copies ran while one was open for 6% of the time, Pallas kernels for 15%

profile of v3, /device:TPU:0, one launch (start us, length us, event | category | flops | bytes accessed | tf_op | source)
XLA Modules:
  0.0 511.8 jit_solution(13194043993997935156)
XLA Ops:
  9.2 13.3 %collective-permute-done.9 = s32[1,16]{1,0:T(1,128)S(1)} collective-permute-done((s32[1,16]{1,0:T(1,128)S(1)}, s32[1,16]{1,0:T(1,128)S(1)}, u32[]{:S(2)}, u32[]{:S(2)}) %collective-permute-start.9) | collective-permute-done | bytes 96 | tf_op jit(solution)/shard_map/ppermute | solution.py:70
  26.5 7.6 %qkv.2 = (f32[3,512,512]{2,1,0:T(8,128)S(1)}, bf16[3,64,512]{2,1,0:T(8,128)(2,1)S(1)}, f32[8,512]{1,0:T(8,128)S(1)}, bf16[512,512]{1,0:T(8,128)(2,1)S(1)}) custom-call(s32[3]{0:T(128)S(1)} %pad_add_fusion.refs_0_, bf16[128,2048]{1,0:T(8,128)(2,1)S(1)} %bitcast.57, bf16[128,2048]{1,0:T(8,128)(2,1)S(1)} %collective-permute-done.5.refs_2_, ...), custom_call_target="tpu_custom_call" | custom-call | flops 1610612736 | bytes 14671872 | tf_op jit(solution)/shard_map/qkv/pallas_call | solution.py:122
  34.1 7.6 %qkv.3 = (f32[3,512,512]{2,1,0:T(8,128)S(1)}, bf16[3,64,512]{2,1,0:T(8,128)(2,1)S(1)}, f32[8,512]{1,0:T(8,128)S(1)}, bf16[512,512]{1,0:T(8,128)(2,1)S(1)}) custom-call(s32[3]{0:T(128)S(1)} %pad_add_fusion.refs_0_, bf16[128,2048]{1,0:T(8,128)(2,1)S(1)} %collective-permute-done.refs_1_, ...), custom_call_target="tpu_custom_call", output_to_operand_aliasing={{0}: (7, {}), {1}: (8, {}), {2}: (9, {}), {3}: (10, {})} | custom-call | flops 1610612736 | bytes 14671872 | tf_op jit(solution)/shard_map/qkv/pallas_call | solution.py:122
  54.0 6.2 %all-to-all-start = ((bf16[8,3,128,256]{3,2,1,0:T(8,128)(2,1)}), bf16[8,3,128,256]{3,2,1,0:T(8,128)(2,1)S(1)}, u32[]{:S(2)}, u32[]{:S(2)}) async-start(bf16[8,3,128,256]{3,2,1,0:T(8,128)(2,1)} %copy-done.30), calls=%async_computation | async-start | bytes 3145728 | tf_op jit(solution)/shard_map/all_to_all | solution.py:606
  61.6 35.0 %all-to-all-done.refs_1_.refs_2_.refs_3_ = bf16[8,3,128,256]{3,2,1,0:T(8,128)(2,1)S(1)} async-done(((bf16[8,3,128,256]{3,2,1,0:T(8,128)(2,1)}), bf16[8,3,128,256]{3,2,1,0:T(8,128)(2,1)S(1)}, u32[]{:S(2)}, u32[]{:S(2)}) %all-to-all-start) | async-done | bytes 1572896 | tf_op jit(solution)/shard_map/all_to_all | solution.py:606
  96.7 7.8 %attention.1 = bf16[8,128,256]{2,1,0:T(8,128)(2,1)S(1)} custom-call(s32[3]{0:T(128)S(1)} %pad_add_fusion.refs_0_, bf16[8,3,128,256]{3,2,1,0:T(8,128)(2,1)S(1)} %all-to-all-done.refs_1_.refs_2_.refs_3_, bf16[8,3,128,256]{3,2,1,0:T(8,128)(2,1)S(1)} %all-to-all-done.refs_1_.refs_2_.refs_3_, bf16[8,3,128,256]{3,2,1,0:T(8,128)(2,1)S(1)} %all-to-all-done.refs_1_.refs_2_.refs_3_, ...), custom_call_target="tpu_custom_call" | custom-call | flops 1073741824 | bytes 5570560 | tf_op jit(solution)/shard_map/attention/pallas_call | solution.py:122
  104.5 18.3 %all_to_all.40 = bf16[8,128,256]{2,1,0:T(8,128)(2,1)S(1)} all-to-all(bf16[8,128,256]{2,1,0:T(8,128)(2,1)S(1)} %attention.1), channel_id=1, replica_groups={{0,4,8,12,16,20,24,28},{1,5,9,13,17,21,25,29},{2,6,10,14,18,22,26,30},{..., dimensions={0} | all-to-all | bytes 1048576 | tf_op jit(solution)/shard_map/all_to_all | solution.py:606
  125.4 12.2 %collective-permute-done.12.refs_3_ = bf16[4,2,128,256]{3,2,1,0:T(8,128)(2,1)S(1)} collective-permute-done((bf16[4,2,128,256]{3,2,1,0:T(8,128)(2,1)S(1)}, bf16[4,2,128,256]{3,2,1,0:T(8,128)(2,1)S(1)}, u32[]{:S(2)}, u32[]{:S(2)}) %collective-permute-start.12) | collective-permute-done | bytes 524320 | tf_op jit(solution)/shard_map/ppermute | solution.py:70
  156.8 11.4 %collective-permute-done.20.refs_3_ = bf16[512,512]{1,0:T(8,128)(2,1)S(1)} collective-permute-done((bf16[512,512]{1,0:T(8,128)(2,1)S(1)}, bf16[512,512]{1,0:T(8,128)(2,1)S(1)}, u32[]{:S(2)}, u32[]{:S(2)}) %collective-permute-start.20) | collective-permute-done | bytes 524320 | tf_op jit(solution)/shard_map/ppermute | solution.py:70
  170.1 15.5 %mlp.2 = (f32[512,2048]{1,0:T(8,128)S(1)}, f32[512,2048]{1,0:T(8,128)}, bf16[512,2048]{1,0:T(8,128)(2,1)S(1)}, bf16[2,64,512]{2,1,0:T(8,128)(2,1)S(1)}, f32[16,5...) custom-call(s32[3]{0:T(128)S(1)} %pad_add_fusion.refs_0_, ...), custom_call_target="tpu_custom_call" | custom-call | flops 6442450944 | bytes 43319296 | tf_op jit(solution)/shard_map/mlp/pallas_call | solution.py:122
  185.8 15.7 %mlp.3 = (f32[512,2048]{1,0:T(8,128)S(1)}, f32[512,2048]{1,0:T(8,128)}, bf16[512,2048]{1,0:T(8,128)(2,1)S(1)}, bf16[2,64,512]{2,1,0:T(8,128)(2,1)S(1)}, f32[16,5...) custom-call(s32[3]{0:T(128)S(1)} %pad_add_fusion.refs_0_, ...), custom_call_target="tpu_custom_call", output_to_operand_aliasing={{0}: (14, {}), {1}: (15, {}), {2}: (16, {}), {3}: (17, {}),... | custom-call | flops 6442450944 | bytes 45416448 | tf_op jit(solution)/shard_map/mlp/pallas_call | solution.py:122
  210.6 11.1 %collective-permute-done.26 = bf16[1,512]{1,0:T(2,128)(2,1)} collective-permute-done((bf16[1,512]{1,0:T(2,128)(2,1)}, bf16[1,512]{1,0:T(2,128)(2,1)}, u32[]{:S(2)}, u32[]{:S(2)}) %collective-permute-start.26) | collective-permute-done | bytes 1056 | tf_op jit(solution)/shard_map/ppermute | solution.py:70
  239.9 12.6 %collective-permute-done.30.refs_1_ = bf16[128,2048]{1,0:T(8,128)(2,1)S(1)} collective-permute-done((bf16[128,2048]{1,0:T(8,128)(2,1)S(1)}, bf16[128,2048]{1,0:T(8,128)(2,1)S(1)}, u32[]{:S(2)}, u32[]{:S(2)}) %collective-permute-start.30) | collective-permute-done | bytes 524320 | tf_op jit(solution)/shard_map/ppermute | solution.py:70
  254.6 16.0 %mlp_back.2 = (f32[3,64,2048]{2,1,0:T(8,128)S(1)}, bf16[512,512]{1,0:T(8,128)(2,1)S(1)}, f32[2,16,512]{2,1,0:T(8,128)S(1)}, bf16[256,512]{1,0:T(8,128)(2,1)S(1)}...) custom-call(s32[3]{0:T(128)S(1)} %pad_add_fusion.refs_0_, ...), custom_call_target="tpu_custom_call" | custom-call | flops 6442450944 | bytes 48103424 | tf_op jit(solution)/shard_map/mlp_back/pallas_call | solution.py:122
  271.3 16.0 %mlp_back.3 = (f32[3,64,2048]{2,1,0:T(8,128)S(1)}, bf16[512,512]{1,0:T(8,128)(2,1)S(1)}, f32[2,16,512]{2,1,0:T(8,128)S(1)}, bf16[256,512]{1,0:T(8,128)(2,1)S(1)}...) custom-call(s32[3]{0:T(128)S(1)} %pad_add_fusion.refs_0_, ...), custom_call_target="tpu_custom_call", output_to_operand_aliasing={{1}: (17, {}), {2}: (18, {})} | custom-call | flops 6442450944 | bytes 47579136 | tf_op jit(solution)/shard_map/mlp_back/pallas_call | solution.py:122
  297.3 5.6 %collective-permute-done.33.refs_3_ = bf16[256,512]{1,0:T(8,128)(2,1)S(1)} collective-permute-done((bf16[256,512]{1,0:T(8,128)(2,1)S(1)}, bf16[256,512]{1,0:T(8,128)(2,1)S(1)}, u32[]{:S(2)}, u32[]{:S(2)}) %collective-permute-start.33) | collective-permute-done | bytes 262176 | tf_op jit(solution)/shard_map/ppermute | solution.py:70
  309.7 5.0 branch_back.1
  318.9 12.5 %collective-permute-done.45 = bf16[4,2,128,256]{3,2,1,0:T(8,128)(2,1)S(1)} collective-permute-done((bf16[4,2,128,256]{3,2,1,0:T(8,128)(2,1)S(1)}, bf16[4,2,128,256]{3,2,1,0:T(8,128)(2,1)S(1)}, u32[]{:S(2)}, u32[]{:S(2)}) %collective-permute-start.45) | collective-permute-done | bytes 524320 | tf_op jit(solution)/shard_map/ppermute | solution.py:70
  331.6 18.3 %all_to_all.41.refs_4_ = bf16[8,128,256]{2,1,0:T(8,128)(2,1)S(1)} all-to-all(bf16[8,128,256]{2,1,0:T(8,128)(2,1)S(1)} %bitcast.61), channel_id=1, replica_groups={{0,4,8,12,16,20,24,28},{1,5,9,13,17,21,25,29},{2,6,10,14,18,22,26,30},{..., dimensions={0} | all-to-all | bytes 1048576 | tf_op jit(solution)/shard_map/all_to_all | solution.py:606
  349.9 12.9 %attention_back.1 = bf16[8,3,128,256]{3,2,1,0:T(8,128)(2,1)} custom-call(s32[3]{0:T(128)S(1)} %pad_add_fusion.refs_0_, bf16[8,3,128,256]{3,2,1,0:T(8,128)(2,1)S(1)} %all-to-all-done.refs_1_.refs_2_.refs_3_, bf16[8,3,128,256]{3,2,1,0:T(8,128)(2,1)S(1)} %all-to-all-done.refs_1_.refs_2_.refs_3_, ...), custom_call_target="tpu_custom_call" | custom-call | flops 2684354560 | bytes 11862016 | tf_op jit(solution)/shard_map/attention_back/pallas_call | solution.py:122
  362.9 4.3 all-to-all-start.3
  369.8 33.6 %all-to-all-done.3.refs_1_ = bf16[8,3,128,256]{3,2,1,0:T(8,128)(2,1)} async-done(((bf16[8,3,128,256]{3,2,1,0:T(8,128)(2,1)}), bf16[8,3,128,256]{3,2,1,0:T(8,128)(2,1)}, u32[]{:S(2)}, u32[]{:S(2)}) %all-to-all-start.3) | async-done | bytes 1572896 | tf_op jit(solution)/shard_map/all_to_all | solution.py:606
  403.3 4.2 all-to-all-start.6
  408.7 5.8 %turn_back.1 = (f32[3,512,512]{2,1,0:T(8,128)S(1)}, f32[8,512]{1,0:T(8,128)S(1)}) custom-call(s32[3]{0:T(128)S(1)} %pad_add_fusion.refs_0_, bf16[8,3,128,256]{3,2,1,0:T(8,128)(2,1)} %all-to-all-done.3.refs_1_, f32[3,512,512]{2,1,0:T(8,128)S(1)} %copy-done.5, f32[4,512]{1,0:T(4,128)S(1)} %convert_element_type.105.refs_3_.refs_4_.refs_8_.refs_5_, ...), custom_call_target="tpu_custom_call" | custom-call | bytes 8437760 | tf_op jit(solution)/shard_map/turn_back/pallas_call | solution.py:122
  429.0 4.0 qkv_back.2
  436.6 6.1 %all-to-all-start.4 = ((bf16[8,88,512]{2,1,0:T(8,128)(2,1)}), bf16[8,88,512]{2,1,0:T(8,128)(2,1)}, u32[]{:S(2)}, u32[]{:S(2)}) async-start(bf16[8,88,512]{2,1,0:T(8,128)(2,1)} %bitcast.60), calls=%async_computation.4 | async-start | bytes 1441792 | tf_op jit(solution)/shard_map/all_to_all | solution.py:763
  443.9 17.6 %all-to-all-done.4 = bf16[8,88,512]{2,1,0:T(8,128)(2,1)} async-done(((bf16[8,88,512]{2,1,0:T(8,128)(2,1)}), bf16[8,88,512]{2,1,0:T(8,128)(2,1)}, u32[]{:S(2)}, u32[]{:S(2)}) %all-to-all-start.4) | async-done | bytes 720928 | tf_op jit(solution)/shard_map/all_to_all | solution.py:763
  462.5 4.2 all-to-all-start.7
  472.1 4.8 qkv_back.3
  479.5 7.2 %all-to-all-done.7 = bf16[8,24,2048]{2,1,0:T(8,128)(2,1)} async-done(((bf16[8,24,2048]{2,1,0:T(8,128)(2,1)}), bf16[8,24,2048]{2,1,0:T(8,128)(2,1)}, u32[]{:S(2)}, u32[]{:S(2)}) %all-to-all-start.7) | async-done | bytes 786464 | tf_op jit(solution)/shard_map/all_to_all | solution.py:765
  487.6 3.5 all-to-all-start.5
  495.4 10.6 %collective-permute-done.54 = bf16[128,2048]{1,0:T(8,128)(2,1)S(1)} collective-permute-done((bf16[128,2048]{1,0:T(8,128)(2,1)S(1)}, bf16[128,2048]{1,0:T(8,128)(2,1)S(1)}, u32[]{:S(2)}, u32[]{:S(2)}) %collective-permute-start.54) | collective-permute-done | bytes 524320 | tf_op jit(solution)/shard_map/ppermute | solution.py:70
  (358 shorter events, 142.9 us)
Async XLA Ops:
  2.6 21.9 %collective-permute-start.2 = (bf16[3,64,512]{2,1,0:T(8,128)(2,1)S(1)}, bf16[3,64,512]{2,1,0:T(8,128)(2,1)}, u32[]{:S(2)}, u32[]{:S(2)}) collective-permute-start(bf16[3,64,512]{2,1,0:T(8,128)(2,1)S(1)} %get-tuple-element.132), channel_id=1, source_target_pairs={{0,1},{1,0},{2,3},{3,2},{4,5},{5,4},{6,7},{7,6},{8,9},{9,8},{10,11... | collective-permute-start | bytes 589832 | tf_op jit(solution)/shard_map/ppermute | solution.py:66
  3.1 21.0 %collective-permute-start.3 = (bf16[3,64,512]{2,1,0:T(8,128)(2,1)S(1)}, bf16[3,64,512]{2,1,0:T(8,128)(2,1)}, u32[]{:S(2)}, u32[]{:S(2)}) collective-permute-start(bf16[3,64,512]{2,1,0:T(8,128)(2,1)S(1)} %get-tuple-element.132), channel_id=1, source_target_pairs={{0,2},{2,0},{1,3},{3,1},{4,6},{6,4},{5,7},{7,5},{8,10},{10,8},{9,1... | collective-permute-start | bytes 589832 | tf_op jit(solution)/shard_map/ppermute | solution.py:70
  5.6 20.8 %collective-permute-start.5 = (bf16[128,2048]{1,0:T(8,128)(2,1)}, bf16[128,2048]{1,0:T(8,128)(2,1)S(1)}, u32[]{:S(2)}, u32[]{:S(2)}) collective-permute-start(bf16[128,2048]{1,0:T(8,128)(2,1)} %bitcast.55), channel_id=1, source_target_pairs={{0,1},{1,0},{2,3},{3,2},{4,5},{5,4},{6,7},{7,6},{8,9},{9,8},{10,11... | collective-permute-start | bytes 1572872 | tf_op jit(solution)/shard_map/ppermute | solution.py:66
  5.8 18.1 %collective-permute-start = (bf16[128,2048]{1,0:T(8,128)(2,1)}, bf16[128,2048]{1,0:T(8,128)(2,1)S(1)}, u32[]{:S(2)}, u32[]{:S(2)}) collective-permute-start(bf16[128,2048]{1,0:T(8,128)(2,1)} %bitcast.56), channel_id=1, source_target_pairs={{0,2},{2,0},{1,3},{3,1},{4,6},{6,4},{5,7},{7,5},{8,10},{10,8},{9,1... | collective-permute-start | bytes 1572872 | tf_op jit(solution)/shard_map/ppermute | solution.py:70
  7.7 14.8 %collective-permute-start.9 = (s32[1,16]{1,0:T(1,128)S(1)}, s32[1,16]{1,0:T(1,128)S(1)}, u32[]{:S(2)}, u32[]{:S(2)}) collective-permute-start(s32[1,16]{1,0:T(1,128)S(1)} %copy-done.80), channel_id=1, source_target_pairs={{0,2},{2,0},{1,3},{3,1},{4,6},{6,4},{5,7},{7,5},{8,10},{10,8},{9,1... | collective-permute-start | bytes 200 | tf_op jit(solution)/shard_map/ppermute | solution.py:70
  54.0 42.6 %all-to-all-start = ((bf16[8,3,128,256]{3,2,1,0:T(8,128)(2,1)}), bf16[8,3,128,256]{3,2,1,0:T(8,128)(2,1)S(1)}, u32[]{:S(2)}, u32[]{:S(2)}) async-start(bf16[8,3,128,256]{3,2,1,0:T(8,128)(2,1)} %copy-done.30), calls=%async_computation | async-start | bytes 3145728 | tf_op jit(solution)/shard_map/all_to_all | solution.py:606
  122.7 14.8 %collective-permute-start.12 = (bf16[4,2,128,256]{3,2,1,0:T(8,128)(2,1)S(1)}, bf16[4,2,128,256]{3,2,1,0:T(8,128)(2,1)S(1)}, u32[]{:S(2)}, u32[]{:S(2)}) collective-permute-start(bf16[4,2,128,256]{3,2,1,0:T(8,128)(2,1)S(1)} %bitcast.51), channel_id=1, source_target_pairs={{0,2},{2,0},{1,3},{3,1},{4,6},{6,4},{5,7},{7,5},{8,10},{10,8},{9,1... | collective-permute-start | bytes 1572872 | tf_op jit(solution)/shard_map/ppermute | solution.py:70
  124.2 16.7 %collective-permute-start.15 = (bf16[4,64,512]{2,1,0:T(8,128)(2,1)S(1)}, bf16[4,64,512]{2,1,0:T(8,128)(2,1)S(1)}, u32[]{:S(2)}, u32[]{:S(2)}) collective-permute-start(bf16[4,64,512]{2,1,0:T(8,128)(2,1)S(1)} %pad_maximum_fusion.3), channel_id=1, source_target_pairs={{0,2},{2,0},{1,3},{3,1},{4,6},{6,4},{5,7},{7,5},{8,10},{10,8},{9,1... | collective-permute-start | bytes 786440 | tf_op jit(solution)/shard_map/ppermute | solution.py:70
  124.8 16.2 %collective-permute-start.14 = (bf16[4,64,512]{2,1,0:T(8,128)(2,1)S(1)}, bf16[4,64,512]{2,1,0:T(8,128)(2,1)S(1)}, u32[]{:S(2)}, u32[]{:S(2)}) collective-permute-start(bf16[4,64,512]{2,1,0:T(8,128)(2,1)S(1)} %pad_maximum_fusion.3), channel_id=1, source_target_pairs={{0,1},{1,0},{2,3},{3,2},{4,5},{5,4},{6,7},{7,6},{8,9},{9,8},{10,11... | collective-permute-start | bytes 786440 | tf_op jit(solution)/shard_map/ppermute | solution.py:66
  124.9 17.7 %collective-permute-start.11 = (bf16[4,2,128,256]{3,2,1,0:T(8,128)(2,1)S(1)}, bf16[4,2,128,256]{3,2,1,0:T(8,128)(2,1)S(1)}, u32[]{:S(2)}, u32[]{:S(2)}) collective-permute-start(bf16[4,2,128,256]{3,2,1,0:T(8,128)(2,1)S(1)} %bitcast.52), channel_id=1, source_target_pairs={{0,1},{1,0},{2,3},{3,2},{4,5},{5,4},{6,7},{7,6},{8,9},{9,8},{10,11... | collective-permute-start | bytes 1572872 | tf_op jit(solution)/shard_map/ppermute | solution.py:66
  155.3 12.9 %collective-permute-start.20 = (bf16[512,512]{1,0:T(8,128)(2,1)S(1)}, bf16[512,512]{1,0:T(8,128)(2,1)S(1)}, u32[]{:S(2)}, u32[]{:S(2)}) collective-permute-start(bf16[512,512]{1,0:T(8,128)(2,1)S(1)} %mid.1.refs_1_.refs_12_), channel_id=1, source_target_pairs={{0,2},{2,0},{1,3},{3,1},{4,6},{6,4},{5,7},{7,5},{8,10},{10,8},{9,1... | collective-permute-start | bytes 1572872 | tf_op jit(solution)/shard_map/ppermute | solution.py:70
  185.6 20.9 %collective-permute-start.23 = (bf16[128,2048]{1,0:T(8,128)(2,1)S(1)}, bf16[128,2048]{1,0:T(8,128)(2,1)S(1)}, u32[]{:S(2)}, u32[]{:S(2)}) collective-permute-start(bf16[128,2048]{1,0:T(8,128)(2,1)S(1)} %get-tuple-element.85), channel_id=1, source_target_pairs={{0,1},{1,0},{2,3},{3,2},{4,5},{5,4},{6,7},{7,6},{8,9},{9,8},{10,11... | collective-permute-start | bytes 1572872 | tf_op jit(solution)/shard_map/ppermute | solution.py:66
  206.1 24.7 %collective-permute-start.22 = (bf16[128,2048]{1,0:T(8,128)(2,1)}, bf16[128,2048]{1,0:T(8,128)(2,1)}, u32[]{:S(2)}, u32[]{:S(2)}) collective-permute-start(bf16[128,2048]{1,0:T(8,128)(2,1)} %get-tuple-element.83), channel_id=1, source_target_pairs={{0,1},{1,0},{2,3},{3,2},{4,5},{5,4},{6,7},{7,6},{8,9},{9,8},{10,11... | collective-permute-start | bytes 1572872 | tf_op jit(solution)/shard_map/ppermute | solution.py:66
  207.5 23.4 %collective-permute-start.24 = (bf16[128,2048]{1,0:T(8,128)(2,1)}, bf16[128,2048]{1,0:T(8,128)(2,1)}, u32[]{:S(2)}, u32[]{:S(2)}) collective-permute-start(bf16[128,2048]{1,0:T(8,128)(2,1)} %add_convert_fusion.3), channel_id=1, source_target_pairs={{0,2},{2,0},{1,3},{3,1},{4,6},{6,4},{5,7},{7,5},{8,10},{10,8},{9,1... | collective-permute-start | bytes 1572872 | tf_op jit(solution)/shard_map/ppermute | solution.py:70
  210.2 11.6 %collective-permute-start.26 = (bf16[1,512]{1,0:T(2,128)(2,1)}, bf16[1,512]{1,0:T(2,128)(2,1)}, u32[]{:S(2)}, u32[]{:S(2)}) collective-permute-start(bf16[1,512]{1,0:T(2,128)(2,1)} %get-tuple-element.135), channel_id=1, source_target_pairs={{0,2},{2,0},{1,3},{3,1},{4,6},{6,4},{5,7},{7,5},{8,10},{10,8},{9,1... | collective-permute-start | bytes 3080 | tf_op jit(solution)/shard_map/ppermute | solution.py:70
  210.6 14.0 %collective-permute-start.25 = (bf16[1,512]{1,0:T(2,128)(2,1)}, bf16[1,512]{1,0:T(2,128)(2,1)}, u32[]{:S(2)}, u32[]{:S(2)}) collective-permute-start(bf16[1,512]{1,0:T(2,128)(2,1)} %get-tuple-element.135), channel_id=1, source_target_pairs={{0,1},{1,0},{2,3},{3,2},{4,5},{5,4},{6,7},{7,6},{8,9},{9,8},{10,11... | collective-permute-start | bytes 3080 | tf_op jit(solution)/shard_map/ppermute | solution.py:66
  238.1 14.3 %collective-permute-start.30 = (bf16[128,2048]{1,0:T(8,128)(2,1)S(1)}, bf16[128,2048]{1,0:T(8,128)(2,1)S(1)}, u32[]{:S(2)}, u32[]{:S(2)}) collective-permute-start(bf16[128,2048]{1,0:T(8,128)(2,1)S(1)} %get-tuple-element.89.refs_1_), channel_id=1, source_target_pairs={{0,2},{2,0},{1,3},{3,1},{4,6},{6,4},{5,7},{7,5},{8,10},{10,8},{9,1... | collective-permute-start | bytes 1572872 | tf_op jit(solution)/shard_map/ppermute | solution.py:70
  239.6 12.8 %collective-permute-start.28 = (bf16[128,2048]{1,0:T(8,128)(2,1)S(1)}, bf16[128,2048]{1,0:T(8,128)(2,1)S(1)}, u32[]{:S(2)}, u32[]{:S(2)}) collective-permute-start(bf16[128,2048]{1,0:T(8,128)(2,1)S(1)} %get-tuple-element.89.refs_1_), channel_id=1, source_target_pairs={{0,1},{1,0},{2,3},{3,2},{4,5},{5,4},{6,7},{7,6},{8,9},{9,8},{10,11... | collective-permute-start | bytes 1572872 | tf_op jit(solution)/shard_map/ppermute | solution.py:66
  252.4 18.9 %collective-permute-start.31 = (bf16[128,2048]{1,0:T(8,128)(2,1)S(1)}, bf16[128,2048]{1,0:T(8,128)(2,1)S(1)}, u32[]{:S(2)}, u32[]{:S(2)}) collective-permute-start(bf16[128,2048]{1,0:T(8,128)(2,1)S(1)} %collective-permute-done.30.refs_1_), channel_id=1, source_target_pairs={{0,1},{1,0},{2,3},{3,2},{4,5},{5,4},{6,7},{7,6},{8,9},{9,8},{10,11... | collective-permute-start | bytes 1572872 | tf_op jit(solution)/shard_map/ppermute | solution.py:66
  270.7 17.2 %collective-permute-start.35 = (bf16[256,512]{1,0:T(8,128)(2,1)S(1)}, bf16[256,512]{1,0:T(8,128)(2,1)S(1)}, u32[]{:S(2)}, u32[]{:S(2)}) collective-permute-start(bf16[256,512]{1,0:T(8,128)(2,1)S(1)} %get-tuple-element.105), channel_id=1, source_target_pairs={{0,1},{1,0},{2,3},{3,2},{4,5},{5,4},{6,7},{7,6},{8,9},{9,8},{10,11... | collective-permute-start | bytes 786440 | tf_op jit(solution)/shard_map/ppermute | solution.py:66
  289.7 13.2 %collective-permute-start.33 = (bf16[256,512]{1,0:T(8,128)(2,1)S(1)}, bf16[256,512]{1,0:T(8,128)(2,1)S(1)}, u32[]{:S(2)}, u32[]{:S(2)}) collective-permute-start(bf16[256,512]{1,0:T(8,128)(2,1)S(1)} %add_convert_fusion.5), channel_id=1, source_target_pairs={{0,2},{2,0},{1,3},{3,1},{4,6},{6,4},{5,7},{7,5},{8,10},{10,8},{9,1... | collective-permute-start | bytes 786440 | tf_op jit(solution)/shard_map/ppermute | solution.py:70
  293.1 14.4 %collective-permute-start.40 = (f32[2,16,512]{2,1,0:T(8,128)S(1)}, f32[2,16,512]{2,1,0:T(8,128)S(1)}, u32[]{:S(2)}, u32[]{:S(2)}) collective-permute-start(f32[2,16,512]{2,1,0:T(8,128)S(1)} %add.188), channel_id=1, source_target_pairs={{0,2},{2,0},{1,3},{3,1},{4,6},{6,4},{5,7},{7,5},{8,10},{10,8},{9,1... | collective-permute-start | bytes 196616 | tf_op jit(solution)/shard_map/ppermute | solution.py:70
  294.3 13.1 %collective-permute-start.42 = (f32[16,512]{1,0:T(8,128)S(1)}, f32[16,512]{1,0:T(8,128)S(1)}, u32[]{:S(2)}, u32[]{:S(2)}) collective-permute-start(f32[16,512]{1,0:T(8,128)S(1)} %add.190), channel_id=1, source_target_pairs={{0,2},{2,0},{1,3},{3,1},{4,6},{6,4},{5,7},{7,5},{8,10},{10,8},{9,1... | collective-permute-start | bytes 98312 | tf_op jit(solution)/shard_map/ppermute | solution.py:70
  317.3 14.0 %collective-permute-start.45 = (bf16[4,2,128,256]{3,2,1,0:T(8,128)(2,1)S(1)}, bf16[4,2,128,256]{3,2,1,0:T(8,128)(2,1)S(1)}, u32[]{:S(2)}, u32[]{:S(2)}) collective-permute-start(bf16[4,2,128,256]{3,2,1,0:T(8,128)(2,1)S(1)} %add_convert_fusion.2), channel_id=1, source_target_pairs={{0,2},{2,0},{1,3},{3,1},{4,6},{6,4},{5,7},{7,5},{8,10},{10,8},{9,1... | collective-permute-start | bytes 1572872 | tf_op jit(solution)/shard_map/ppermute | solution.py:70
  362.9 40.4 %all-to-all-start.3 = ((bf16[8,3,128,256]{3,2,1,0:T(8,128)(2,1)}), bf16[8,3,128,256]{3,2,1,0:T(8,128)(2,1)}, u32[]{:S(2)}, u32[]{:S(2)}) async-start(bf16[8,3,128,256]{3,2,1,0:T(8,128)(2,1)} %attention_back.1), calls=%async_computation.3 | async-start | bytes 3145728 | tf_op jit(solution)/shard_map/all_to_all | solution.py:606
  403.3 33.2 %all-to-all-start.6 = ((bf16[8,24,2048]{2,1,0:T(8,128)(2,1)}), bf16[8,24,2048]{2,1,0:T(8,128)(2,1)}, u32[]{:S(2)}, u32[]{:S(2)}) async-start(bf16[8,24,2048]{2,1,0:T(8,128)(2,1)} %bitcast.58), calls=%async_computation.6 | async-start | bytes 1572864 | tf_op jit(solution)/shard_map/all_to_all | solution.py:763
  436.6 25.0 %all-to-all-start.4 = ((bf16[8,88,512]{2,1,0:T(8,128)(2,1)}), bf16[8,88,512]{2,1,0:T(8,128)(2,1)}, u32[]{:S(2)}, u32[]{:S(2)}) async-start(bf16[8,88,512]{2,1,0:T(8,128)(2,1)} %bitcast.60), calls=%async_computation.4 | async-start | bytes 1441792 | tf_op jit(solution)/shard_map/all_to_all | solution.py:763
  462.5 24.2 %all-to-all-start.7 = ((bf16[8,24,2048]{2,1,0:T(8,128)(2,1)}), bf16[8,24,2048]{2,1,0:T(8,128)(2,1)}, u32[]{:S(2)}, u32[]{:S(2)}) async-start(bf16[8,24,2048]{2,1,0:T(8,128)(2,1)} %broadcast_in_dim.120), calls=%async_computation.7 | async-start | bytes 1572864 | tf_op jit(solution)/shard_map/all_to_all | solution.py:765
  466.8 24.4 %collective-permute-start.53 = (bf16[128,2048]{1,0:T(8,128)(2,1)}, bf16[128,2048]{1,0:T(8,128)(2,1)}, u32[]{:S(2)}, u32[]{:S(2)}) collective-permute-start(bf16[128,2048]{1,0:T(8,128)(2,1)} %copy-done.75), channel_id=1, source_target_pairs={{0,1},{1,0},{2,3},{3,2},{4,5},{5,4},{6,7},{7,6},{8,9},{9,8},{10,11... | collective-permute-start | bytes 1572872 | tf_op jit(solution)/shard_map/ppermute | solution.py:66
  477.8 17.6 %collective-permute-start.52 = (bf16[128,2048]{1,0:T(8,128)(2,1)}, bf16[128,2048]{1,0:T(8,128)(2,1)S(1)}, u32[]{:S(2)}, u32[]{:S(2)}) collective-permute-start(bf16[128,2048]{1,0:T(8,128)(2,1)} %get-tuple-element.125), channel_id=1, source_target_pairs={{0,1},{1,0},{2,3},{3,2},{4,5},{5,4},{6,7},{7,6},{8,9},{9,8},{10,11... | collective-permute-start | bytes 1572872 | tf_op jit(solution)/shard_map/ppermute | solution.py:66
  487.6 22.4 %all-to-all-start.5 = ((bf16[8,88,512]{2,1,0:T(8,128)(2,1)}), bf16[8,88,512]{2,1,0:T(8,128)(2,1)S(1)}, u32[]{:S(2)}, u32[]{:S(2)}) async-start(bf16[8,88,512]{2,1,0:T(8,128)(2,1)} %broadcast_in_dim.119), calls=%async_computation.5 | async-start | bytes 1441792 | tf_op jit(solution)/shard_map/all_to_all | solution.py:765
  492.4 13.6 %collective-permute-start.54 = (bf16[128,2048]{1,0:T(8,128)(2,1)S(1)}, bf16[128,2048]{1,0:T(8,128)(2,1)S(1)}, u32[]{:S(2)}, u32[]{:S(2)}) collective-permute-start(bf16[128,2048]{1,0:T(8,128)(2,1)S(1)} %add_convert_fusion), channel_id=1, source_target_pairs={{0,2},{2,0},{1,3},{3,1},{4,6},{6,4},{5,7},{7,5},{8,10},{10,8},{9,1... | collective-permute-start | bytes 1572872 | tf_op jit(solution)/shard_map/ppermute | solution.py:70
  (111 other events, 1244.7 us)
